TPU v7x, 128 devices: a whole 4x4x4 slice. The times are simulated.
128 devices in a mesh: lat: 4 (over x_hi, core), lon: 32 (over z, x_lo, y).
Axes of the slice: x: 4 (x_hi: 2, x_lo: 2; x = x_hi * 2 + x_lo), y: 4, z: 4, core: 2. Of those that a mesh axis runs over, the one named last changes fastest.
Arguments:
- tokens: bfloat16 [4, 48, 384, 512], P(None, 'lat', 'lon'), may hold values from -6 to 6
- region: int32 [4, 48, 384], P(None, 'lat', 'lon'), may hold values from 0 to 2
- norm_gain1: float32 [2, 512], replicated, may hold values from 0.25 to 1.75
- qkv_weight: bfloat16 [2, 512, 1536], replicated, may hold values from -3 to 3
- proj_weight: bfloat16 [2, 512, 512], replicated, may hold values from -0.25 to 0.25
- norm_gain2: float32 [2, 512], replicated, may hold values from 0.25 to 1.75
- up_weight: bfloat16 [2, 512, 2048], replicated, may hold values from -0.25 to 0.25
- down_weight: bfloat16 [2, 2048, 512], replicated, may hold values from -0.125 to 0.125
Outputs:
- result: bfloat16 [4, 48, 384, 512], P(None, 'lat', 'lon')
All inputs are finite; a program needn't handle non-finite values.
Results may differ from a plain program's by a relative error of at most 0.012.
Values may be sent and summed in bfloat16 or wider, within the bound.
No kernel may reach another device: no remote copies, remote signals or barrier semaphores. Data moves between devices by JAX's collectives and lax.ppermute only.
A program may use at most 64 MiB of HBM per device.

v0:
```python
import math

import jax
import jax.numpy as jnp
from jax import lax
from jax.sharding import PartitionSpec as P

HEADS = 8
WLEV = 2
WLAT = 6
WLON = 12


epsilon = 1e-05


def shifted_2(value, axis, steps):
    count = lax.axis_size(axis)
    pairs = [(source, (source + steps) % count) for source in range(count)]
    return lax.ppermute(value, axis, pairs)


def layer_norm(field, gain_vector):
    field = field.astype(jnp.float32)
    average = jnp.mean(field, axis=-1, keepdims=True)
    centered = field - average
    variance = jnp.mean(centered * centered, axis=-1, keepdims=True)
    return centered * lax.rsqrt(variance + epsilon) * gain_vector


def to_windows(field):
    level_count, row_count, column_count = field.shape[:3]
    trailing = tuple(field.shape[3:])
    shaped = field.reshape(
        (level_count // WLEV, WLEV, row_count // WLAT, WLAT, column_count // WLON, WLON) + trailing
    )
    order = (0, 2, 4, 1, 3, 5) + tuple(range(6, 6 + len(trailing)))
    return jnp.transpose(shaped, order).reshape((-1, WLEV * WLAT * WLON) + trailing)


def from_windows(windows, level_count, row_count, column_count):
    trailing = tuple(windows.shape[2:])
    shaped = windows.reshape(
        (level_count // WLEV, row_count // WLAT, column_count // WLON, WLEV, WLAT, WLON) + trailing
    )
    order = (0, 3, 1, 4, 2, 5) + tuple(range(6, 6 + len(trailing)))
    return jnp.transpose(shaped, order).reshape((level_count, row_count, column_count) + trailing)


def window_attention(normed, labels, w_qkv, w_proj):
    count, span, features = normed.shape
    head_size = features // HEADS
    mixed = jnp.dot(normed, w_qkv, preferred_element_type=jnp.float32).astype(jnp.bfloat16)
    queries = mixed[..., :features].reshape(count, span, HEADS, head_size)
    key_vectors = mixed[..., features : 2 * features].reshape(count, span, HEADS, head_size)
    values = mixed[..., 2 * features :].reshape(count, span, HEADS, head_size)
    scores = jnp.einsum("wqhd,wkhd->whqk", queries, key_vectors, preferred_element_type=jnp.float32)
    scores = scores * (1.0 / math.sqrt(head_size))
    allowed = labels[:, None, :, None] == labels[:, None, None, :]
    scores = jnp.where(allowed, scores, -jnp.inf)
    peak = jnp.max(scores, axis=-1, keepdims=True)
    exponent = jnp.exp(scores - peak)
    attention_weights = (exponent / jnp.sum(exponent, axis=-1, keepdims=True)).astype(jnp.bfloat16)
    gathered = jnp.einsum(
        "whqk,wkhd->wqhd", attention_weights, values, preferred_element_type=jnp.float32
    )
    gathered = gathered.astype(jnp.bfloat16).reshape(count, span, features)
    return jnp.dot(gathered, w_proj, preferred_element_type=jnp.float32)


def attention_part(field, labels, gain_vector, w_qkv, w_proj):
    level_count, row_count, column_count, features = field.shape
    normed = layer_norm(field, gain_vector).astype(jnp.bfloat16)
    projected = window_attention(to_windows(normed), to_windows(labels), w_qkv, w_proj)
    return field.astype(jnp.float32) + from_windows(projected, level_count, row_count, column_count)


def feed_forward(field, gain_vector, w_up, w_down):
    normed = layer_norm(field, gain_vector).astype(jnp.bfloat16)
    hidden_units = jax.nn.gelu(jnp.dot(normed, w_up, preferred_element_type=jnp.float32)).astype(
        jnp.bfloat16
    )
    return (field + jnp.dot(hidden_units, w_down, preferred_element_type=jnp.float32)).astype(
        jnp.bfloat16
    )


def per_device(
    tokens, region, norm_gain1, qkv_weight, proj_weight, norm_gain2, up_weight, down_weight
):
    level_count, row_count, column_count, features = tokens.shape
    half_level = WLEV // 2
    half_row = WLAT // 2
    half_column = WLON // 2
    mixed_first = attention_part(tokens, region, norm_gain1[0], qkv_weight[0], proj_weight[0])
    first_out = feed_forward(mixed_first, norm_gain2[0], up_weight[0], down_weight[0])
    shifted = jnp.roll(first_out, -half_level, axis=0)
    label_field = jnp.roll(region.astype(jnp.bfloat16), -half_level, axis=0)
    below_field, below_labels = shifted_2(
        (shifted[:, :half_row], label_field[:, :half_row]), "lat", -1
    )
    shifted = jnp.concatenate([shifted[:, half_row:], below_field], axis=1)
    label_field = jnp.concatenate([label_field[:, half_row:], below_labels], axis=1)
    beside_field, beside_labels = shifted_2(
        (shifted[:, :, :half_column], label_field[:, :, :half_column]), "lon", -1
    )
    shifted = jnp.concatenate([shifted[:, :, half_column:], beside_field], axis=2)
    label_field = jnp.concatenate([label_field[:, :, half_column:], beside_labels], axis=2)
    level_index = jnp.arange(level_count, dtype=jnp.int32)[:, None, None]
    global_row = (
        lax.axis_index("lat") * row_count + jnp.arange(row_count, dtype=jnp.int32)[None, :, None]
    )
    wrapped_level = (level_index >= level_count - half_level).astype(jnp.int32)
    wrapped_row = (global_row >= row_count * lax.axis_size("lat") - half_row).astype(jnp.int32)
    labels_second = label_field.astype(jnp.int32) * 4 + wrapped_level * 2 + wrapped_row
    mixed_second = attention_part(
        shifted, labels_second, norm_gain1[1], qkv_weight[1], proj_weight[1]
    )
    keep_columns = column_count - half_column
    keep_rows = row_count - half_row
    finished = feed_forward(mixed_second, norm_gain2[1], up_weight[1], down_weight[1])
    left_part = shifted_2(finished[:, :, keep_columns:], "lon", 1)
    restored = jnp.concatenate([left_part, finished[:, :, :keep_columns]], axis=2)
    upper_part = shifted_2(restored[:, keep_rows:], "lat", 1)
    restored = jnp.concatenate([upper_part, restored[:, :keep_rows]], axis=1)
    return jnp.roll(restored, half_level, axis=0)


def solution(mesh):
    return jax.shard_map(
        per_device,
        mesh=mesh,
        in_specs=(P(None, "lat", "lon", None), P(None, "lat", "lon"), P(), P(), P(), P(), P(), P()),
        out_specs=P(None, "lat", "lon", None),
        check_vma=False,
    )
```

profile of v0, /device:TPU:0, one launch (start us, length us, event | category | flops | bytes accessed | tf_op | source)
XLA Modules:
  0.0 110.7 jit_solution(5888625771330534101)
XLA Ops:
  0.0 1.3 %convert_reduce_fusion.1 = f32[4,12,12]{2,1,0:T(8,128)S(1)} fusion(bf16[4,12,12,512]{3,0,2,1:T(4,128)(2,1)} %param.8), kind=kLoop, calls=%fused_computation.37 | loop fusion | flops 589248 | bytes 592128 | tf_op jit(solution)/shard_map/reduce_sum | solution.py:25
  1.4 1.5 %fusion.52 = f32[4,12,12]{2,1,0:T(8,128)S(1)} fusion(bf16[4,12,12,512]{3,0,2,1:T(4,128)(2,1)} %param.8, f32[4,12,12]{2,1,0:T(8,128)S(1)} %broadcast_multiply_fusion.3), kind=kLoop, calls=%fused_computation.60 | loop fusion | flops 1179072 | bytes 594432 | tf_op jit(solution)/shard_map/reduce_sum | solution.py:27
  2.9 0.8 fusion.120
  3.6 0.3 fusion.54
  4.0 0.6 copy.145
  4.6 0.2 reshape.272
  4.8 2.5 %convolution_convert_fusion.1 = bf16[4,144,1536]{2,1,0:T(8,128)(2,1)S(1)} fusion(bf16[2,512,1536]{2,1,0:T(8,128)(2,1)} %param.11, bf16[4,144,512]{2,0,1:T(4,128)(2,1)S(1)} %reshape.272), kind=kOutput, calls=%fused_computation.31 | convolution fusion | flops 906854400 | bytes 3932160 | tf_op jit(solution)/shard_map/dot_general | solution.py:53
  7.3 0.2 fusion.117
  7.5 0.5 copy.103
  8.0 1.3 %copy.104 = bf16[4,144,512]{1,2,0:T(8,128)(2,1)} copy(bf16[4,144,512]{2,1,0:T(8,128)(2,1)S(1)} %get-tuple-element.8) | data formatting | bytes 1179648 | tf_op jit(solution)/shard_map/reshape | solution.py:55
  9.3 0.1 eq.40
  9.4 0.2 broadcast_compare_fusion.1
  9.5 1.3 %copy.102 = bf16[4,144,512]{1,2,0:T(8,128)(2,1)} copy(bf16[4,144,512]{2,1,0:T(8,128)(2,1)S(1)} %get-tuple-element.10) | data formatting | bytes 1179648 | tf_op jit(solution)/shard_map/reshape | solution.py:56
  10.8 4.0 %fusion.121 = (f32[4,8,144]{2,1,0:T(8,128)S(1)}, f32[4,8,144,144]{2,3,1,0:T(8,128)}) fusion(pred[4,144,144]{1,2,0:T(8,128)(4,1)S(1)} %broadcast_compare_fusion.1, bf16[4,144,8,64]{1,3,2,0:T(8,128)(2,1)S(1)} %bitcast.151, bf16[4,144,8,64]{1,3,2,0:T(8,128)(2,1)S(1)} %bitcast.152), kind=kOutput, calls=%fused_computation.152 | convolution fusion | flops 87589008 | bytes 3935232 | tf_op jit(solution)/shard_map/sub | solution.py:62
  14.8 3.2 %fusion.74 = bf16[4,144,8,64]{1,3,2,0:T(8,128)(2,1)S(1)} fusion(bf16[4,144,8,64]{1,3,2,0:T(8,128)(2,1)} %bitcast.154, f32[4,8,144,144]{2,3,1,0:T(8,128)} %get-tuple-element.22, f32[4,8,144]{2,1,0:T(8,128)S(1)} %get-tuple-element.21), kind=kOutput, calls=%fused_computation.83 | convolution fusion | flops 86556672 | bytes 3852288 | tf_op jit(solution)/shard_map/whqk,wkhd->wqhd/dot_general | solution.py:64
  18.0 0.8 copy.105
  18.8 0.8 reshape.293
  19.6 1.6 %convolution_bitcast_fusion.1 = f32[2,2,2,6,1,12,512]{6,5,3,1,2,0,4:T(8,128)S(1)} fusion(bf16[2,2,2,6,12,512]{5,4,3,2,1,0:T(8,128)(2,1)S(1)} %reshape.293, bf16[2,512,512]{2,1,0:T(8,128)(2,1)} %param.12), kind=kOutput, calls=%fused_computation.80 | convolution fusion | flops 301989888 | bytes 2293760 | tf_op jit(solution)/shard_map/dot_general | solution.py:68
  21.2 0.2 copy.106
  21.5 0.3 fusion.84
  21.8 0.5 multiply_reduce_fusion.1
  22.3 0.2 copy-done.5
  22.5 6.0 %add_convert_fusion = bf16[4,12,12,512]{3,2,1,0:T(8,128)(2,1)S(1)} fusion(bf16[2,2048,512]{2,1,0:T(8,128)(2,1)} %param.15, bf16[2,512,2048]{2,1,0:T(8,128)(2,1)} %param.14, f32[512]{0:T(512)S(1)} %bitcast.167, f32[4,12,12]{2,1,0:T(8,128)S(1)} %add_rsqrt_fusion.2, f32[4,12,12]{2,1,0:T(8,128)S(1)} %broadcast_multiply_fusion.2, ...), kind=kOutput, calls=%fused_computation.75 | convolution fusion | flops 2429485056 | bytes 9177088 | tf_op jit(solution)/shard_map/dot_general | solution.py:83
  28.6 2.6 %collective-permute-start = (bf16[4,3,12,512]{3,2,1,0:T(8,128)(2,1)S(1)}, bf16[4,3,12,512]{3,2,1,0:T(8,128)(2,1)S(1)}, u32[]{:S(2)}, u32[]{:S(2)}) collective-permute-start(bf16[4,3,12,512]{3,2,1,0:T(8,128)(2,1)S(1)} %pad_maximum_fusion.8), channel_id=1, source_target_pairs={{0,96},{32,0},{64,32},{96,64},{1,97},{33,1},{65,33},{97,65},{2,98}... | collective-permute-start | bytes 442376 | tf_op jit(solution)/shard_map/ppermute | solution.py:20
  31.2 0.8 collective-permute-start.2
  32.0 0.1 fusion.85
  32.1 2.3 %collective-permute-done.2 = bf16[4,3,12]{2,0,1:T(4,128)(2,1)S(1)} collective-permute-done((bf16[4,3,12]{2,0,1:T(4,128)(2,1)S(1)}, bf16[4,3,12]{2,0,1:T(4,128)(2,1)S(1)}, u32[]{:S(2)}, u32[]{:S(2)}) %collective-permute-start.2) | collective-permute-done | bytes 320 | tf_op jit(solution)/shard_map/ppermute | solution.py:20
  34.4 0.1 slice_maximum_fusion
  34.5 6.5 %collective-permute-start.3 = (bf16[4,12,6]{2,0,1:T(4,128)(2,1)S(1)}, bf16[4,12,6]{2,0,1:T(4,128)(2,1)S(1)}, u32[]{:S(2)}, u32[]{:S(2)}) collective-permute-start(bf16[4,12,6]{2,0,1:T(4,128)(2,1)S(1)} %get-tuple-element.16), channel_id=1, source_target_pairs={{0,31},{1,0},{2,1},{3,2},{4,3},{5,4},{6,5},{7,6},{8,7},{9,8},{10,9... | collective-permute-start | bytes 1736 | tf_op jit(solution)/shard_map/ppermute | solution.py:20
  41.1 1.4 %collective-permute-done.3 = bf16[4,12,6]{2,0,1:T(4,128)(2,1)S(1)} collective-permute-done((bf16[4,12,6]{2,0,1:T(4,128)(2,1)S(1)}, bf16[4,12,6]{2,0,1:T(4,128)(2,1)S(1)}, u32[]{:S(2)}, u32[]{:S(2)}) %collective-permute-start.3) | collective-permute-done | bytes 608 | tf_op jit(solution)/shard_map/ppermute | solution.py:20
  42.5 0.2 fusion.92
  42.6 6.8 %collective-permute-start.1 = (bf16[4,12,6,512]{3,2,1,0:T(8,128)(2,1)S(1)}, bf16[4,12,6,512]{3,2,1,0:T(8,128)(2,1)S(1)}, u32[]{:S(2)}, u32[]{:S(2)}) collective-permute-start(bf16[4,12,6,512]{3,2,1,0:T(8,128)(2,1)S(1)} %get-tuple-element.14), channel_id=1, source_target_pairs={{0,31},{1,0},{2,1},{3,2},{4,3},{5,4},{6,5},{7,6},{8,7},{9,8},{10,9... | collective-permute-start | bytes 884744 | tf_op jit(solution)/shard_map/ppermute | solution.py:20
  49.4 0.1 add_bitcast_fusion
  49.5 0.1 eq.44
  49.6 0.8 broadcast_compare_fusion
  50.4 8.1 %collective-permute-done.1 = bf16[4,12,6,512]{3,2,1,0:T(8,128)(2,1)S(1)} collective-permute-done((bf16[4,12,6,512]{3,2,1,0:T(8,128)(2,1)S(1)}, bf16[4,12,6,512]{3,2,1,0:T(8,128)(2,1)S(1)}, u32[]{:S(2)}, u32[]{:S(2)}) %collective-permute-start.1) | collective-permute-done | bytes 294944 | tf_op jit(solution)/shard_map/ppermute | solution.py:20
  58.4 0.4 convert_reduce_fusion
  58.8 0.5 fusion.59
  59.4 0.4 fusion.76
  59.9 0.1 reshape.294
  60.0 2.5 %convolution_convert_fusion = bf16[4,144,1536]{2,1,0:T(8,128)(2,1)S(1)} fusion(bf16[4,144,512]{2,1,0:T(8,128)(2,1)S(1)} %reshape.294, bf16[2,512,1536]{2,1,0:T(8,128)(2,1)} %param.11), kind=kOutput, calls=%fused_computation.30 | convolution fusion | flops 906854400 | bytes 3932160 | tf_op jit(solution)/shard_map/dot_general | solution.py:53
  62.5 0.1 fusion.116
  62.7 1.3 %copy.110 = bf16[4,144,512]{1,2,0:T(8,128)(2,1)} copy(bf16[4,144,512]{2,1,0:T(8,128)(2,1)S(1)} %get-tuple-element.6) | data formatting | bytes 1179648 | tf_op jit(solution)/shard_map/reshape | solution.py:54
  64.0 1.3 %copy.111 = bf16[4,144,512]{1,2,0:T(8,128)(2,1)} copy(bf16[4,144,512]{2,1,0:T(8,128)(2,1)S(1)} %get-tuple-element.5) | data formatting | bytes 1179648 | tf_op jit(solution)/shard_map/reshape | solution.py:55
  65.3 1.3 %copy.109 = bf16[4,144,512]{1,2,0:T(8,128)(2,1)} copy(bf16[4,144,512]{2,1,0:T(8,128)(2,1)S(1)} %get-tuple-element.7) | data formatting | bytes 1179648 | tf_op jit(solution)/shard_map/reshape | solution.py:56
  66.6 0.0 copy-done.3
  66.6 4.9 %fusion.122 = (f32[4,8,144]{2,1,0:T(8,128)S(1)}, f32[4,8,144,144]{2,3,1,0:T(8,128)}) fusion(pred[4,144,144]{1,2,0:T(8,128)(4,1)} %broadcast_compare_fusion, bf16[4,144,8,64]{1,3,2,0:T(8,128)(2,1)S(1)} %bitcast.153, bf16[4,144,8,64]{1,3,2,0:T(8,128)(2,1)S(1)} %bitcast.155), kind=kOutput, calls=%fused_computation.153 | convolution fusion | flops 87589008 | bytes 3935232 | tf_op jit(solution)/shard_map/sub | solution.py:62
  71.5 3.2 %fusion.75 = bf16[4,144,8,64]{1,3,2,0:T(8,128)(2,1)S(1)} fusion(bf16[4,144,8,64]{1,3,2,0:T(8,128)(2,1)} %bitcast.156, f32[4,8,144,144]{2,3,1,0:T(8,128)} %get-tuple-element.24, f32[4,8,144]{2,1,0:T(8,128)S(1)} %get-tuple-element.23), kind=kOutput, calls=%fused_computation.84 | convolution fusion | flops 86556672 | bytes 3852288 | tf_op jit(solution)/shard_map/whqk,wkhd->wqhd/dot_general | solution.py:64
  74.7 0.8 copy.112
  75.5 0.8 reshape.295
  76.3 1.8 %fusion.91 = (f32[2,2,2,6,12]{4,3,1,2,0:T(8,128)S(1)}, f32[2,2,2,6,1,12,512]{6,5,3,1,2,0,4:T(8,128)S(1)}) fusion(bf16[2,2,2,6,12,512]{5,4,3,2,1,0:T(8,128)(2,1)S(1)} %reshape.295, bf16[2,512,512]{2,1,0:T(8,128)(2,1)} %param.12, bf16[2,2,2,6,1,6,512]{6,5,3,2,1,0,4:T(8,128)(2,1)S(1)} %bitcast.145, bf16[2,2,2,6,1,6,512]{6,5,3,2,1,0,4:T(8,128)(2,1)S(1)} %bitcast.138), kind=kOutput, calls=%fused_computation.108 | convolution fusion | flops 304053696 | bytes 2885888 | tf_op jit(solution)/shard_map/dot_general | solution.py:68
  78.1 0.2 copy.90
  78.3 0.6 multiply_reduce_fusion
  78.9 0.5 multiply_convert_fusion
  79.4 0.9 copy.113
  80.4 6.1 %fusion.61 = bf16[4,12,12,512]{3,2,1,0:T(8,128)(2,1)S(1)} fusion(f32[4,12,12,512]{3,2,1,0:T(8,128)S(1)} %bitcast.150, bf16[4,12,6,512]{3,2,1,0:T(8,128)(2,1)S(1)} %collective-permute-done.1, bf16[4,12,6,512]{3,2,1,0:T(8,128)(2,1)S(1)} %get-tuple-element.13, bf16[2,2048,512]{2,1,0:T(8,128)(2,1)} %param.15, bf16[4,12,12,512]{3,2,1,0:T(8,128)(2,1)} %bitcast.157, ...), kind=kOutput, calls=%fused_computation.69 | convolution fusion | flops 2428600320 | bytes 7340032 | tf_op jit(solution)/shard_map/dot_general | solution.py:83
  86.5 0.1 fusion.118
  86.7 0.1 collective-permute-start.4
  86.7 15.7 %collective-permute-done.4 = bf16[4,12,6,512]{3,2,1,0:T(8,128)(2,1)S(1)} collective-permute-done((bf16[4,12,6,512]{3,2,1,0:T(8,128)(2,1)S(1)}, bf16[4,12,6,512]{3,2,1,0:T(8,128)(2,1)S(1)}, u32[]{:S(2)}, u32[]{:S(2)}) %collective-permute-start.4) | collective-permute-done | bytes 294944 | tf_op jit(solution)/shard_map/ppermute | solution.py:20
  102.4 0.1 pad_maximum_fusion.7
  102.5 0.1 collective-permute-start.5
  102.6 6.6 %collective-permute-done.5 = bf16[4,3,12,512]{3,2,1,0:T(8,128)(2,1)S(1)} collective-permute-done((bf16[4,3,12,512]{3,2,1,0:T(8,128)(2,1)S(1)}, bf16[4,3,12,512]{3,2,1,0:T(8,128)(2,1)S(1)}, u32[]{:S(2)}, u32[]{:S(2)}) %collective-permute-start.5) | collective-permute-done | bytes 147488 | tf_op jit(solution)/shard_map/ppermute | solution.py:20
  109.2 0.2 fusion.77
  109.4 1.3 %copy.93 = bf16[4,12,12,512]{3,0,2,1:T(4,128)(2,1)} copy(bf16[4,12,12,512]{3,2,1,0:T(8,128)(2,1)S(1)} %fusion.77) | data formatting | bytes 1179648 | tf_op jit(solution)/shard_map/jit(_roll_static)/concatenate | solution.py:126
  (37 shorter events, 0.3 us)
Async XLA Ops:
  0.0 3.6 %copy-start = (bf16[4,12,12,512]{3,0,2,1:T(4,128)(2,1)S(1)}, bf16[4,12,12,512]{3,0,2,1:T(4,128)(2,1)}, u32[]{:S(2)}) copy-start(bf16[4,12,12,512]{3,0,2,1:T(4,128)(2,1)} %param.8) | copy-start | bytes 1769476
  7.5 1.8 %copy-start.4 = (s32[4,12,12]{2,0,1:T(4,128)S(1)}, s32[4,12,12]{2,0,1:T(4,128)}, u32[]{:S(2)}) copy-start(s32[4,12,12]{2,0,1:T(4,128)} %param.9) | copy-start | bytes 6916
  9.3 1.6 %copy-start.1 = (bf16[4,144,512]{1,2,0:T(8,128)(2,1)S(1)}, bf16[4,144,512]{1,2,0:T(8,128)(2,1)}, u32[]{:S(2)}) copy-start(bf16[4,144,512]{1,2,0:T(8,128)(2,1)} %copy.104) | copy-start | bytes 1769476
  21.8 0.7 copy-start.5
  28.6 13.9 %collective-permute-start = (bf16[4,3,12,512]{3,2,1,0:T(8,128)(2,1)S(1)}, bf16[4,3,12,512]{3,2,1,0:T(8,128)(2,1)S(1)}, u32[]{:S(2)}, u32[]{:S(2)}) collective-permute-start(bf16[4,3,12,512]{3,2,1,0:T(8,128)(2,1)S(1)} %pad_maximum_fusion.8), channel_id=1, source_target_pairs={{0,96},{32,0},{64,32},{96,64},{1,97},{33,1},{65,33},{97,65},{2,98}... | collective-permute-start | bytes 442376 | tf_op jit(solution)/shard_map/ppermute | solution.py:20
  31.2 3.2 %collective-permute-start.2 = (bf16[4,3,12]{2,0,1:T(4,128)(2,1)S(1)}, bf16[4,3,12]{2,0,1:T(4,128)(2,1)S(1)}, u32[]{:S(2)}, u32[]{:S(2)}) collective-permute-start(bf16[4,3,12]{2,0,1:T(4,128)(2,1)S(1)} %pad_maximum_fusion.10), channel_id=1, source_target_pairs={{0,96},{32,0},{64,32},{96,64},{1,97},{33,1},{65,33},{97,65},{2,98}... | collective-permute-start | bytes 872 | tf_op jit(solution)/shard_map/ppermute | solution.py:20
  34.5 8.0 %collective-permute-start.3 = (bf16[4,12,6]{2,0,1:T(4,128)(2,1)S(1)}, bf16[4,12,6]{2,0,1:T(4,128)(2,1)S(1)}, u32[]{:S(2)}, u32[]{:S(2)}) collective-permute-start(bf16[4,12,6]{2,0,1:T(4,128)(2,1)S(1)} %get-tuple-element.16), channel_id=1, source_target_pairs={{0,31},{1,0},{2,1},{3,2},{4,3},{5,4},{6,5},{7,6},{8,7},{9,8},{10,9... | collective-permute-start | bytes 1736 | tf_op jit(solution)/shard_map/ppermute | solution.py:20
  42.6 15.8 %collective-permute-start.1 = (bf16[4,12,6,512]{3,2,1,0:T(8,128)(2,1)S(1)}, bf16[4,12,6,512]{3,2,1,0:T(8,128)(2,1)S(1)}, u32[]{:S(2)}, u32[]{:S(2)}) collective-permute-start(bf16[4,12,6,512]{3,2,1,0:T(8,128)(2,1)S(1)} %get-tuple-element.14), channel_id=1, source_target_pairs={{0,31},{1,0},{2,1},{3,2},{4,3},{5,4},{6,5},{7,6},{8,7},{9,8},{10,9... | collective-permute-start | bytes 884744 | tf_op jit(solution)/shard_map/ppermute | solution.py:20
  64.0 2.6 %copy-start.2 = (bf16[4,144,512]{1,2,0:T(8,128)(2,1)S(1)}, bf16[4,144,512]{1,2,0:T(8,128)(2,1)}, u32[]{:S(2)}) copy-start(bf16[4,144,512]{1,2,0:T(8,128)(2,1)} %copy.110) | copy-start | bytes 1769476
  65.3 1.3 %copy-start.3 = (bf16[4,144,512]{1,2,0:T(8,128)(2,1)S(1)}, bf16[4,144,512]{1,2,0:T(8,128)(2,1)}, u32[]{:S(2)}) copy-start(bf16[4,144,512]{1,2,0:T(8,128)(2,1)} %copy.111) | copy-start | bytes 1769476
  86.7 15.8 %collective-permute-start.4 = (bf16[4,12,6,512]{3,2,1,0:T(8,128)(2,1)S(1)}, bf16[4,12,6,512]{3,2,1,0:T(8,128)(2,1)S(1)}, u32[]{:S(2)}, u32[]{:S(2)}) collective-permute-start(bf16[4,12,6,512]{3,2,1,0:T(8,128)(2,1)S(1)} %get-tuple-element.11), channel_id=1, source_target_pairs={{0,1},{1,2},{2,3},{3,4},{4,5},{5,6},{6,7},{7,8},{8,9},{9,10},{10,1... | collective-permute-start | bytes 884744 | tf_op jit(solution)/shard_map/ppermute | solution.py:20
  102.5 6.7 %collective-permute-start.5 = (bf16[4,3,12,512]{3,2,1,0:T(8,128)(2,1)S(1)}, bf16[4,3,12,512]{3,2,1,0:T(8,128)(2,1)S(1)}, u32[]{:S(2)}, u32[]{:S(2)}) collective-permute-start(bf16[4,3,12,512]{3,2,1,0:T(8,128)(2,1)S(1)} %pad_maximum_fusion.7), channel_id=1, source_target_pairs={{0,32},{32,64},{64,96},{96,0},{1,33},{33,65},{65,97},{97,1},{2,34}... | collective-permute-start | bytes 442376 | tf_op jit(solution)/shard_map/ppermute | solution.py:20
where the time goes:
time: 111 us
  matrix products  35.7 us (32%)
  waiting for transfers between devices  34 us (31%)
  starting transfers between devices  16.8 us (15%)
  local copies, waits for them, and re-layouts  15.5 us (14%)
  other arithmetic  8.23 us (7%)
    ppermute x6, waiting for transfers between devices, shifted_2(): return lax.ppermute(value, axis, pairs)  34 us
    ppermute x6, starting transfers between devices, shifted_2(): return lax.ppermute(value, axis, pairs)  16.8 us
    dot_general x2, matrix products, feed_forward(): jnp.dot(hidden_units, w_down, preferred_element_type=jnp.float32)  12.1 us
    sub x2, matrix products, window_attention(): exponent = jnp.exp(scores - peak)  8.88 us
    dot_general x2, matrix products, window_attention(): jnp.einsum('whqk,wkhd->wqhd', attention_weights, values, preferred_elemen...  6.32 us
    dot_general x2, matrix products, window_attention(): jnp.dot(normed, w_qkv, preferred_element_type=jnp.float32)  4.98 us
    dot_general x2, matrix products, window_attention(): return jnp.dot(gathered, w_proj, preferred_element_type=jnp.float32)  3.39 us
    another operation x4, local copies, waits for them, and re-layouts  3.25 us
  transfers between devices with their start and end apart: 6, of which 5 were waited for; matrix products, arithmetic and copies ran while one was open for 1% of the time, Pallas kernels for 0%

commit v1 on v0

v1 whole, which is shorter than its diff:
```python
import math

import jax
import jax.numpy as jnp
import numpy as np
from jax import lax
from jax.experimental import pallas as pl
from jax.experimental.pallas import tpu as pltpu
from jax.sharding import PartitionSpec as P

BF = jnp.bfloat16
F32 = jnp.float32
LEV, D, FF, HEADS, HD = 4, 512, 2048, 8, 64
ROWS = COLS = 12
UNIT = 18
GROUP = LEV * UNIT
PER_RT = 2 * GROUP
NPAD = LEV * 3 * 16
EPS = 1e-05
BIG = 1e30
EXP_SCALE = math.log2(math.e) / math.sqrt(HD)
VMEM_LIMIT = 56 * 1024 * 1024
FCHUNK = 512


def permutation():
    p = np.zeros((PER_RT, NPAD), np.float32)
    for half in range(2):
        for level in range(LEV):
            for row in range(3):
                for col in range(6):
                    to = half * GROUP + level * UNIT + row * 6 + col
                    p[to, (level * 3 + row) * 16 + half * 6 + col] = 1.0
    return p


def layer_norm(x, gain):
    mean = jnp.mean(x, axis=-1, keepdims=True)
    centered = x - mean
    variance = jnp.mean(centered * centered, axis=-1, keepdims=True)
    return centered * lax.rsqrt(variance + EPS) * gain


def one_hot(labels, rows):
    lane = lax.broadcasted_iota(jnp.int32, (rows, 128), 1) & 63
    return lane.astype(F32) == labels


def query_features(labels, rows):
    return jnp.where(one_hot(labels, rows), -BIG, 0.0).astype(BF)


def key_features(labels, rows):
    return jnp.where(one_hot(labels, rows), 0.0, 1.0).astype(BF)


def low_lanes(rows):
    return lax.broadcasted_iota(jnp.int32, (rows, 128), 1) < 64


def attend(q, k, v, qf, kf):
    m, n = q.shape[0], k.shape[0]
    low_q, low_k = low_lanes(m), low_lanes(n)
    ones = jnp.ones((n, 128), BF)
    tiles = []
    for pair in range(HEADS // 2):
        lanes = slice(pair * 128, (pair + 1) * 128)
        qt, kt, vt = q[:, lanes], k[:, lanes], v[:, lanes]
        got = []
        for odd in range(2):
            if odd:
                qh, kh, vh = jnp.where(low_q, qf, qt), jnp.where(low_k, kf, kt), jnp.where(low_k, ones, vt)
            else:
                qh, kh, vh = jnp.where(low_q, qt, qf), jnp.where(low_k, kt, kf), jnp.where(low_k, vt, ones)
            s = lax.dot_general(qh, kh, (((1,), (1,)), ((), ())), preferred_element_type=F32)
            peak = jnp.max(s, axis=-1, keepdims=True)
            e = jnp.exp2((s - peak) * EXP_SCALE).astype(BF)
            got.append(jnp.dot(e, vh, preferred_element_type=F32))
        num = jnp.where(low_q, got[0], got[1])
        den = pltpu.roll(jnp.where(low_q, got[1], got[0]), 64, 1)
        tiles.append(num / den)
    return jnp.concatenate(tiles, axis=1)


def mlp(h, gain, wup, wdown):
    a = layer_norm(h, gain).astype(BF)
    acc = h
    for c in range(0, FF, FCHUNK):
        u = jnp.dot(a, wup[:, c : c + FCHUNK], preferred_element_type=F32)
        g = jax.nn.gelu(u).astype(BF)
        acc = acc + jnp.dot(g, wdown[c : c + FCHUNK, :], preferred_element_type=F32)
    return acc


class Weights:
    def __init__(self, block, sources, buffers, sem):
        self.copies = [
            pltpu.make_async_copy(s.at[block], b, sem.at[i]) for i, (s, b) in enumerate(zip(sources, buffers))
        ]
        for c in self.copies:
            c.start()

    def wait(self, i):
        self.copies[i].wait()


WEIGHT_SCRATCH = [
    pltpu.VMEM((D, 3 * D), BF),
    pltpu.VMEM((D, D), BF),
    pltpu.VMEM((D, FF), BF),
    pltpu.VMEM((FF, D), BF),
    pltpu.SemaphoreType.DMA((4,)),
]


def first_kernel(
    x_ref, lab_ref, labrow_ref, p_ref, g1_ref, g2_ref, wq_hbm, wp_hbm, wu_hbm, wd_hbm,
    own_ref, up_ref, down_ref, left_ref, right_ref,
    xp, wq, wp, wu, wd, sem,
):
    weights = Weights(0, (wq_hbm, wp_hbm, wu_hbm, wd_hbm), (wq, wp, wu, wd), sem)
    xp[...] = jnp.zeros_like(xp)
    for rt in range(4):
        for level in range(LEV):
            for row in range(3):
                xp[rt, level * 3 + row, 0:COLS, :] = x_ref[level, rt * 3 + row]
    g1, g2 = g1_ref[0:1, :], g2_ref[0:1, :]
    for half in range(2):
        x = jnp.concatenate(
            [
                jnp.dot(p_ref[...], xp[rt].reshape(NPAD, D), preferred_element_type=F32)
                for rt in (2 * half, 2 * half + 1)
            ],
            axis=0,
        )
        a = layer_norm(x, g1).astype(BF)
        if half == 0:
            weights.wait(0)
        qkv = jnp.dot(a, wq[...], preferred_element_type=F32).astype(BF)
        lab = lab_ref[half * 288 : half * 288 + 288, 0:1]
        o = attend(
            qkv[:, :D], qkv[:, D : 2 * D], qkv[:, 2 * D :], query_features(lab, 288), key_features(lab, 288)
        ).astype(BF)
        if half == 0:
            weights.wait(1)
        h = x + jnp.dot(o, wp[...], preferred_element_type=F32)
        if half == 0:
            weights.wait(2)
            weights.wait(3)
        y = mlp(h, g2, wu, wd)
        for i in range(2):
            rt = 2 * half + i
            for side in range(2):
                part = y[(2 * i + side) * GROUP : (2 * i + side + 1) * GROUP].astype(BF)
                own_ref[rt * 2 + side] = part
                (left_ref, right_ref)[side][rt * GROUP : (rt + 1) * GROUP, :] = part
                if rt == 0:
                    up_ref[side * GROUP : (side + 1) * GROUP, :] = part
                if rt == 3:
                    down_ref[side * GROUP : (side + 1) * GROUP, :] = part
    up_ref[PER_RT:, :] = labrow_ref[0]
    down_ref[PER_RT:, :] = labrow_ref[1]
    left_ref[4 * GROUP :, :] = labrow_ref[2]
    right_ref[4 * GROUP :, :] = labrow_ref[3]


def column_of(rows, count):
    return jnp.transpose(rows.astype(F32)[:, :count], (1, 0))[:, 0:1]


def second_body(windows, labels_of, p_ref, g1_ref, g2_ref, hbm, out_hbm, scratch, rts):
    wq, wp, wu, wd, sem, o_s, x_s, y_s, out_sem = scratch
    weights = Weights(1, hbm, (wq, wp, wu, wd), sem)
    g1, g2 = g1_ref[1:2, :], g2_ref[1:2, :]
    for index, (own, halo) in enumerate(windows):
        n_own = len(own) * GROUP
        x = jnp.concatenate([s[0].astype(F32) for s in own + halo], axis=0)
        lab = jnp.concatenate([s[1] for s in own + halo], axis=0)
        a = layer_norm(x, g1).astype(BF)
        if index == 0:
            weights.wait(0)
        kv = jnp.dot(a, wq[:, D:], preferred_element_type=F32).astype(BF)
        q = jnp.dot(a[:n_own], wq[:, :D], preferred_element_type=F32).astype(BF)
        o = attend(q, kv[:, :D], kv[:, D:], query_features(lab[:n_own], n_own), key_features(lab, 288))
        for i, s in enumerate(own):
            rows = slice(s[2] * GROUP, (s[2] + 1) * GROUP)
            o_s[rows, :] = o[i * GROUP : (i + 1) * GROUP]
            x_s[rows, :] = x[i * GROUP : (i + 1) * GROUP]
    weights.wait(1)
    h = x_s[...] + jnp.dot(o_s[...].astype(BF), wp[...], preferred_element_type=F32)
    weights.wait(2)
    weights.wait(3)
    y = mlp(h, g2, wu, wd).astype(BF)
    copies = []
    for i, rt in enumerate(rts):
        nat = lax.dot_general(
            p_ref[...], y[i * PER_RT : (i + 1) * PER_RT], (((0,), (0,)), ((), ())), preferred_element_type=F32
        ).astype(BF).reshape(LEV * 3, 16, D)
        for level in range(LEV):
            for row in range(3):
                y_s[i, level, row] = nat[level * 3 + row, :COLS]
        c = pltpu.make_async_copy(y_s.at[i], out_hbm.at[:, rt * 3 : rt * 3 + 3], out_sem.at[i])
        c.start()
        copies.append(c)
    for c in copies:
        c.wait()


def middle_kernel(
    own_ref, lh_ref, rh_ref, lab_ref, p_ref, g1_ref, g2_ref, wq_hbm, wp_hbm, wu_hbm, wd_hbm, out_hbm, *scratch
):
    windows = []
    for side, halo_ref in enumerate((lh_ref, rh_ref)):
        col = column_of(halo_ref[4 * GROUP :, :], 384)
        own = [
            (own_ref[rt * 2 + side], lab_ref[(rt * 2 + side) * GROUP : (rt * 2 + side + 1) * GROUP, 1:2], (rt - 1) * 2 + side)
            for rt in (1, 2)
        ]
        halo = [
            (halo_ref[rt * GROUP : (rt + 1) * GROUP, :], col[rt * GROUP : (rt + 1) * GROUP]) for rt in (1, 2)
        ]
        windows.append((own, halo))
    second_body(windows, None, p_ref, g1_ref, g2_ref, (wq_hbm, wp_hbm, wu_hbm, wd_hbm), out_hbm, scratch, (1, 2))


def edge_kernel(
    out_in, own_ref, u_ref, d_ref, lh_ref, rh_ref, lhh_ref, rhh_ref, lab_ref, p_ref, g1_ref, g2_ref,
    wq_hbm, wp_hbm, wu_hbm, wd_hbm, out_hbm, *scratch
):
    windows = []
    for rt, v_ref in ((0, u_ref), (3, d_ref)):
        vcol = column_of(v_ref[PER_RT:, :], 256)
        at = 0 if rt == 0 else 1
        for side, (h_ref, hh_ref) in enumerate(((lh_ref, lhh_ref), (rh_ref, rhh_ref))):
            hcol = column_of(h_ref[4 * GROUP :, :], 384)
            other = 1 - side
            hvcol = column_of(hh_ref[PER_RT + 8 * at : PER_RT + 8 * at + 8, :], 256)
            own = [
                (own_ref[rt * 2 + side], lab_ref[(rt * 2 + side) * GROUP : (rt * 2 + side + 1) * GROUP, 1:2], at * 2 + side)
            ]
            halo = [
                (v_ref[side * GROUP : (side + 1) * GROUP, :], vcol[side * GROUP : (side + 1) * GROUP]),
                (h_ref[rt * GROUP : (rt + 1) * GROUP, :], hcol[rt * GROUP : (rt + 1) * GROUP]),
                (hh_ref[at * GROUP : (at + 1) * GROUP, :], hvcol[other * GROUP : (other + 1) * GROUP]),
            ]
            windows.append((own, halo))
    second_body(windows, None, p_ref, g1_ref, g2_ref, (wq_hbm, wp_hbm, wu_hbm, wd_hbm), out_hbm, scratch, (0, 3))


SECOND_SCRATCH = WEIGHT_SCRATCH + [
    pltpu.VMEM((4 * GROUP, D), F32),
    pltpu.VMEM((4 * GROUP, D), F32),
    pltpu.VMEM((2, LEV, 3, COLS, D), BF),
    pltpu.SemaphoreType.DMA((2,)),
]

VM = pl.BlockSpec(memory_space=pltpu.VMEM)
ANY = pl.BlockSpec(memory_space=pl.ANY)


def cost(flops, nbytes):
    return pl.CostEstimate(flops=int(flops), bytes_accessed=int(nbytes), transcendentals=0)


def shift(value, axis, steps):
    count = lax.axis_size(axis)
    return lax.ppermute(value, axis, [(s, (s + steps) % count) for s in range(count)])


def per_device(tokens, region, norm_gain1, qkv_weight, proj_weight, norm_gain2, up_weight, down_weight):
    p = jnp.asarray(permutation(), BF)
    tr = region.reshape(LEV, 4, 3, 2, 6).transpose(1, 3, 0, 2, 4)
    level = jnp.arange(LEV, dtype=jnp.int32)[None, None, :, None, None]
    row = (
        lax.axis_index("lat") * ROWS
        + 3 * jnp.arange(4, dtype=jnp.int32)[:, None, None, None, None]
        + jnp.arange(3, dtype=jnp.int32)[None, None, None, :, None]
    )
    lab1 = (tr * 2 + level // 2).reshape(576)
    pair = jnp.where((level == 1) | (level == 2), 0, 1)
    lab2 = ((tr * 4 + 2 * (level == 0) + (row < 3)) * 2 + pair).reshape(4, 2, GROUP)
    labs = jnp.stack([lab1, lab2.reshape(576)], axis=1).astype(F32)

    def as_row(v):
        return jnp.pad(v.reshape(-1), (0, 512 - v.size))

    rows = jnp.stack([as_row(lab2[0]), as_row(lab2[3]), as_row(lab2[:, 0]), as_row(lab2[:, 1])])
    labrow = jnp.broadcast_to(rows[:, None, :], (4, 8, 512)).astype(BF)

    weights = (qkv_weight, proj_weight, up_weight, down_weight)
    params = pltpu.CompilerParams(vmem_limit_bytes=VMEM_LIMIT)
    own, up, down, left, right = pl.pallas_call(
        first_kernel,
        out_shape=(
            jax.ShapeDtypeStruct((8, GROUP, D), BF),
            jax.ShapeDtypeStruct((PER_RT + 8, D), BF),
            jax.ShapeDtypeStruct((PER_RT + 8, D), BF),
            jax.ShapeDtypeStruct((4 * GROUP + 8, D), BF),
            jax.ShapeDtypeStruct((4 * GROUP + 8, D), BF),
        ),
        in_specs=[VM] * 6 + [ANY] * 4,
        out_specs=[VM] * 5,
        scratch_shapes=[pltpu.VMEM((4, LEV * 3, 16, D), BF)] + WEIGHT_SCRATCH,
        compiler_params=params,
        cost_estimate=cost(4e9, 8e6),
        name="first_block",
    )(tokens, labs, labrow, p, norm_gain1, norm_gain2, *weights)

    below = shift(up, "lat", -1)
    above = shift(down, "lat", 1)
    right_halo = shift(left, "lon", -1)
    left_halo = shift(right, "lon", 1)
    to_left = jnp.concatenate([above[:GROUP], below[:GROUP], above[PER_RT:], below[PER_RT:]], axis=0)
    to_right = jnp.concatenate([above[GROUP:PER_RT], below[GROUP:PER_RT], above[PER_RT:], below[PER_RT:]], axis=0)
    right_corner = shift(to_left, "lon", -1)
    left_corner = shift(to_right, "lon", 1)

    out_shape = jax.ShapeDtypeStruct((LEV, ROWS, COLS, D), BF)
    out = pl.pallas_call(
        middle_kernel,
        out_shape=out_shape,
        in_specs=[VM] * 7 + [ANY] * 4,
        out_specs=ANY,
        scratch_shapes=SECOND_SCRATCH,
        compiler_params=params,
        cost_estimate=cost(2.5e9, 8e6),
        name="second_middle",
    )(own, left_halo, right_halo, labs, p, norm_gain1, norm_gain2, *weights)
    return pl.pallas_call(
        edge_kernel,
        out_shape=out_shape,
        in_specs=[ANY] + [VM] * 11 + [ANY] * 4,
        out_specs=ANY,
        scratch_shapes=SECOND_SCRATCH,
        input_output_aliases={0: 0},
        compiler_params=params,
        cost_estimate=cost(2.5e9, 8e6),
        name="second_edge",
    )(out, own, above, below, left_halo, right_halo, left_corner, right_corner, labs, p, norm_gain1, norm_gain2, *weights)


def solution(mesh):
    return jax.shard_map(
        per_device,
        mesh=mesh,
        in_specs=(P(None, "lat", "lon", None), P(None, "lat", "lon"), P(), P(), P(), P(), P(), P()),
        out_specs=P(None, "lat", "lon", None),
        check_vma=False,
    )
```

time: 111 us -> 74.9 us (0.67)
  Pallas kernels: 0 us -> 43.4 us
  matrix products: 35.7 us -> 0 us
  waiting for transfers between devices: 34 us -> 4.79 us
  local copies, waits for them, and re-layouts: 15.5 us -> 8.55 us
  other arithmetic: 8.23 us -> 1.79 us
    pallas_call x0 -> x3, Pallas kernels: none -> 43.4 us  [the longest x1 16.9 us: per_device(): pl.pallas_call(edge_kernel, out_shape=out_shape, in_specs=[ANY] + [VM] *...]
    ppermute x6, waiting for transfers between devices: 34 us -> 4.79 us  [shift(): lax.ppermute(value, axis, [(s, (s + steps) % count) for s in range(count)])]
    dot_general x8 -> x0, matrix products: 26.8 us -> none  [the longest x2 12.1 us: feed_forward(): jnp.dot(hidden_units, w_down, preferred_element_type=jnp.float32)]
    sub x2 -> x0, matrix products: 8.88 us -> none  [window_attention(): exponent = jnp.exp(scores - peak)]
    reshape x11 -> x0, local copies, waits for them, and re-layouts: 8.15 us -> none  [the longest x2 2.6 us: window_attention(): mixed[..., features:2 * features].reshape(count, span, HEADS, head_size)]
    reduce_sum x7 -> x0, other arithmetic: 5.16 us -> none  [the longest x4 3.11 us: layer_norm(): variance = jnp.mean(centered * centered, axis=-1, keepdims=True)]
    unnamed x12 -> x13, local copies, waits for them, and re-layouts: 0.21 us -> 4.28 us
    pallas_call x0 -> x1, local copies, waits for them, and re-layouts: none -> 2.41 us  [per_device(): pl.pallas_call(edge_kernel, out_shape=out_shape, in_specs=[ANY] + [VM] *...]
  transfers between devices with their start and end apart: 6 -> 6, of which waited for: 5 -> 1; matrix products, arithmetic and copies ran while one was open for 1% -> 0% of each run, Pallas kernels for 0% -> 16%
where the time goes in v1:
time: 74.9 us; the launch traced here: 74.6 us
  Pallas kernels  43.4 us (58%)
  starting transfers between devices  15.8 us (21%)
  local copies, waits for them, and re-layouts  8.55 us (11%)
  waiting for transfers between devices  4.79 us (6%)
  other arithmetic  1.79 us (2%)
    pallas_call x1, Pallas kernels, per_device(): pl.pallas_call(edge_kernel, out_shape=out_shape, in_specs=[ANY] + [VM] *...  16.9 us
    ppermute x6, starting transfers between devices, shift(): lax.ppermute(value, axis, [(s, (s + steps) % count) for s in range(count)])  15.8 us
    pallas_call x1, Pallas kernels, per_device(): pl.pallas_call(first_kernel, out_shape=(jax.ShapeDtypeStruct((8, GROUP, D...  14.9 us
    pallas_call x1, Pallas kernels, per_device(): pl.pallas_call(middle_kernel, out_shape=out_shape, in_specs=[VM] * 7 + [A...  11.7 us
    ppermute x6, waiting for transfers between devices, shift(): lax.ppermute(value, axis, [(s, (s + steps) % count) for s in range(count)])  4.79 us
    unnamed x13, local copies, waits for them, and re-layouts  4.28 us
    pallas_call x1, local copies, waits for them, and re-layouts, per_device(): pl.pallas_call(edge_kernel, out_shape=out_shape, in_specs=[ANY] + [VM] *...  2.41 us
  transfers between devices with their start and end apart: 6, of which 1 were waited for; matrix products, arithmetic and copies ran while one was open for 0% of the time, Pallas kernels for 16%

profile of v1, /device:TPU:0, one launch (start us, length us, event | category | flops | bytes accessed | tf_op | source)
XLA Modules:
  0.0 74.6 jit_solution(1778469838751576139)
XLA Ops:
  0.0 0.1 fusion.5
  0.1 0.7 %broadcast_multiply_fusion.1 = (s32[4,12,12]{2,0,1:T(4,128)S(1)}, s32[4,12,12]{2,0,1:T(4,128)S(1)}) fusion(s32[4,12,12]{2,0,1:T(4,128)} %param.10), kind=kLoop, calls=%fused_computation.12 | loop fusion | flops 1152 | bytes 6912 | tf_op jit(solution)/shard_map/mul | solution.py:279
  0.8 0.1 mul.41
  0.9 0.1 fusion.6
  1.0 0.1 reshape.107
  1.2 0.1 mul.38
  1.3 0.1 fusion.4
  1.4 0.1 stack_reshape.3
  1.5 0.1 stack_reshape_reshape.3
  1.7 0.1 reshape_squeeze.16
  1.8 0.1 reshape_squeeze.18
  1.9 0.1 reshape_squeeze.17
  2.0 0.1 reshape_squeeze.19
  2.2 0.2 copy.34
  2.3 0.7 convert_element_type.14.lab_ref
  3.0 2.1 %copy.35.x_ref = bf16[4,12,12,512]{3,2,1,0:T(8,128)(2,1)} copy(bf16[4,12,12,512]{3,0,2,1:T(4,128)(2,1)} %param.9) | data formatting | bytes 1179648 | tf_op args[0]
  5.2 0.6 broadcast_in_dim.4.labrow_ref
  5.8 14.9 %first_block.1 = (bf16[8,72,512]{2,1,0:T(8,128)(2,1)}, bf16[152,512]{1,0:T(8,128)(2,1)}, bf16[152,512]{1,0:T(8,128)(2,1)}, bf16[296,512]{1,0:T(8,128)(2,1)}, bf16[296,512]{1,0:T(8,128)(2,1)}) custom-call(bf16[4,12,12,512]{3,2,1,0:T(8,128)(2,1)} %copy.35.x_ref, f32[576,2]{1,0:T(8,128)} %convert_element_type.14.lab_ref, ...), custom_call_target="tpu_custom_call" | custom-call | flops 4000000000 | bytes 8000000 | tf_op jit(solution)/shard_map/first_block/pallas_call | solution.py:292
  20.7 0.1 collective-permute-start.2
  20.7 3.2 %collective-permute-start.3 = (bf16[152,512]{1,0:T(8,128)(2,1)}, bf16[152,512]{1,0:T(8,128)(2,1)S(1)}, u32[]{:S(2)}, u32[]{:S(2)}) collective-permute-start(bf16[152,512]{1,0:T(8,128)(2,1)} %get-tuple-element.14), channel_id=1, source_target_pairs={{0,96},{32,0},{64,32},{96,64},{1,97},{33,1},{65,33},{97,65},{2,98}... | collective-permute-start | bytes 466952 | tf_op jit(solution)/shard_map/ppermute | solution.py:267
  24.0 1.7 %collective-permute-start = (bf16[296,512]{1,0:T(8,128)(2,1)}, bf16[296,512]{1,0:T(8,128)(2,1)S(1)}, u32[]{:S(2)}, u32[]{:S(2)}) collective-permute-start(bf16[296,512]{1,0:T(8,128)(2,1)} %get-tuple-element.11), channel_id=1, source_target_pairs={{0,1},{1,2},{2,3},{3,4},{4,5},{5,6},{6,7},{7,8},{8,9},{9,10},{10,1... | collective-permute-start | bytes 909320 | tf_op jit(solution)/shard_map/ppermute | solution.py:267
  25.6 5.8 %collective-permute-start.1 = (bf16[296,512]{1,0:T(8,128)(2,1)}, bf16[296,512]{1,0:T(8,128)(2,1)S(1)}, u32[]{:S(2)}, u32[]{:S(2)}) collective-permute-start(bf16[296,512]{1,0:T(8,128)(2,1)} %get-tuple-element.12), channel_id=1, source_target_pairs={{0,31},{1,0},{2,1},{3,2},{4,3},{5,4},{6,5},{7,6},{8,7},{9,8},{10,9... | collective-permute-start | bytes 909320 | tf_op jit(solution)/shard_map/ppermute | solution.py:267
  31.5 0.0 collective-permute-done.2.u_ref
  31.5 0.0 copy-start.2
  31.5 0.0 collective-permute-done.3.d_ref
  31.5 0.0 copy-start.3
  31.6 5.0 %collective-permute-start.5 = (bf16[160,512]{1,0:T(8,128)(2,1)S(1)}, bf16[160,512]{1,0:T(8,128)(2,1)S(1)}, u32[]{:S(2)}, u32[]{:S(2)}) collective-permute-start(bf16[160,512]{1,0:T(8,128)(2,1)S(1)} %get-tuple-element.27), channel_id=1, source_target_pairs={{0,31},{1,0},{2,1},{3,2},{4,3},{5,4},{6,5},{7,6},{8,7},{9,8},{10,9... | collective-permute-start | bytes 491528 | tf_op jit(solution)/shard_map/ppermute | solution.py:267
  36.6 0.0 collective-permute-start.4
  36.6 4.8 %collective-permute-done.lh_ref = bf16[296,512]{1,0:T(8,128)(2,1)S(1)} collective-permute-done((bf16[296,512]{1,0:T(8,128)(2,1)}, bf16[296,512]{1,0:T(8,128)(2,1)S(1)}, u32[]{:S(2)}, u32[]{:S(2)}) %collective-permute-start) | collective-permute-done | bytes 303136 | tf_op jit(solution)/shard_map/ppermute | solution.py:267
  41.4 0.0 copy-start
  41.4 0.0 collective-permute-done.1.rh_ref
  41.4 0.0 copy-start.1
  41.4 0.7 copy-done
  42.1 0.1 copy-done.1
  42.2 11.7 %second_middle.1.out_in = bf16[4,12,12,512]{3,2,1,0:T(8,128)(2,1)} custom-call(bf16[8,72,512]{2,1,0:T(8,128)(2,1)} %get-tuple-element.10.own_ref, bf16[296,512]{1,0:T(8,128)(2,1)} %copy-done, bf16[296,512]{1,0:T(8,128)(2,1)} %copy-done.1, f32[576,2]{1,0:T(8,128)} %convert_element_type.14.lab_ref, bf16[144,192]{1,0:T(8,128)(2,1)} %constant.41.clone.p_ref, ...), custom_call_target="tpu_custom_call" | custom-call | flops 2500000000 | bytes 8000000 | tf_op jit(solution)/shard_map/second_middle/pallas_call | solution.py:319
  53.9 0.0 copy-done.2
  53.9 0.0 copy-done.3
  53.9 0.0 collective-permute-done.5.rhh_ref
  53.9 0.0 copy-start.4
  53.9 0.0 collective-permute-done.4.lhh_ref
  53.9 0.7 copy-done.4
  54.6 0.0 copy-start.5
  54.6 0.7 copy-done.5
  55.2 16.9 %second_edge.1 = bf16[4,12,12,512]{3,2,1,0:T(8,128)(2,1)} custom-call(bf16[4,12,12,512]{3,2,1,0:T(8,128)(2,1)} %second_middle.1.out_in, bf16[8,72,512]{2,1,0:T(8,128)(2,1)} %get-tuple-element.10.own_ref, bf16[152,512]{1,0:T(8,128)(2,1)} %copy-done.2, bf16[152,512]{1,0:T(8,128)(2,1)} %copy-done.3, ...), custom_call_target="tpu_custom_call", output_to_operand_aliasing={{}: (0, {})} | custom-call | flops 2500000000 | bytes 8000000 | tf_op jit(solution)/shard_map/second_edge/pallas_call | solution.py:329
  72.1 2.4 %copy.36 = bf16[4,12,12,512]{3,0,2,1:T(4,128)(2,1)} copy(bf16[4,12,12,512]{3,2,1,0:T(8,128)(2,1)} %second_edge.1) | data formatting | bytes 1179648 | tf_op jit(solution)/shard_map/second_edge/pallas_call | solution.py:329
  (21 shorter events, 0.2 us)
Async XLA Ops:
  20.7 10.8 %collective-permute-start.2 = (bf16[152,512]{1,0:T(8,128)(2,1)}, bf16[152,512]{1,0:T(8,128)(2,1)S(1)}, u32[]{:S(2)}, u32[]{:S(2)}) collective-permute-start(bf16[152,512]{1,0:T(8,128)(2,1)} %get-tuple-element.13), channel_id=1, source_target_pairs={{0,32},{32,64},{64,96},{96,0},{1,33},{33,65},{65,97},{97,1},{2,34}... | collective-permute-start | bytes 466952 | tf_op jit(solution)/shard_map/ppermute | solution.py:267
  20.7 10.8 %collective-permute-start.3 = (bf16[152,512]{1,0:T(8,128)(2,1)}, bf16[152,512]{1,0:T(8,128)(2,1)S(1)}, u32[]{:S(2)}, u32[]{:S(2)}) collective-permute-start(bf16[152,512]{1,0:T(8,128)(2,1)} %get-tuple-element.14), channel_id=1, source_target_pairs={{0,96},{32,0},{64,32},{96,64},{1,97},{33,1},{65,33},{97,65},{2,98}... | collective-permute-start | bytes 466952 | tf_op jit(solution)/shard_map/ppermute | solution.py:267
  24.0 17.4 %collective-permute-start = (bf16[296,512]{1,0:T(8,128)(2,1)}, bf16[296,512]{1,0:T(8,128)(2,1)S(1)}, u32[]{:S(2)}, u32[]{:S(2)}) collective-permute-start(bf16[296,512]{1,0:T(8,128)(2,1)} %get-tuple-element.11), channel_id=1, source_target_pairs={{0,1},{1,2},{2,3},{3,4},{4,5},{5,6},{6,7},{7,8},{8,9},{9,10},{10,1... | collective-permute-start | bytes 909320 | tf_op jit(solution)/shard_map/ppermute | solution.py:267
  25.6 15.7 %collective-permute-start.1 = (bf16[296,512]{1,0:T(8,128)(2,1)}, bf16[296,512]{1,0:T(8,128)(2,1)S(1)}, u32[]{:S(2)}, u32[]{:S(2)}) collective-permute-start(bf16[296,512]{1,0:T(8,128)(2,1)} %get-tuple-element.12), channel_id=1, source_target_pairs={{0,31},{1,0},{2,1},{3,2},{4,3},{5,4},{6,5},{7,6},{8,7},{9,8},{10,9... | collective-permute-start | bytes 909320 | tf_op jit(solution)/shard_map/ppermute | solution.py:267
  31.5 22.4 %copy-start.2 = (bf16[152,512]{1,0:T(8,128)(2,1)}, bf16[152,512]{1,0:T(8,128)(2,1)S(1)}, u32[]{:S(2)}) copy-start(bf16[152,512]{1,0:T(8,128)(2,1)S(1)} %collective-permute-done.2.u_ref) | copy-start | bytes 466948
  31.5 22.4 %copy-start.3 = (bf16[152,512]{1,0:T(8,128)(2,1)}, bf16[152,512]{1,0:T(8,128)(2,1)S(1)}, u32[]{:S(2)}) copy-start(bf16[152,512]{1,0:T(8,128)(2,1)S(1)} %collective-permute-done.3.d_ref) | copy-start | bytes 466948
  31.6 22.3 %collective-permute-start.5 = (bf16[160,512]{1,0:T(8,128)(2,1)S(1)}, bf16[160,512]{1,0:T(8,128)(2,1)S(1)}, u32[]{:S(2)}, u32[]{:S(2)}) collective-permute-start(bf16[160,512]{1,0:T(8,128)(2,1)S(1)} %get-tuple-element.27), channel_id=1, source_target_pairs={{0,31},{1,0},{2,1},{3,2},{4,3},{5,4},{6,5},{7,6},{8,7},{9,8},{10,9... | collective-permute-start | bytes 491528 | tf_op jit(solution)/shard_map/ppermute | solution.py:267
  36.6 17.3 %collective-permute-start.4 = (bf16[160,512]{1,0:T(8,128)(2,1)S(1)}, bf16[160,512]{1,0:T(8,128)(2,1)S(1)}, u32[]{:S(2)}, u32[]{:S(2)}) collective-permute-start(bf16[160,512]{1,0:T(8,128)(2,1)S(1)} %get-tuple-element.28), channel_id=1, source_target_pairs={{0,1},{1,2},{2,3},{3,4},{4,5},{5,6},{6,7},{7,8},{8,9},{9,10},{10,1... | collective-permute-start | bytes 491528 | tf_op jit(solution)/shard_map/ppermute | solution.py:267
  41.4 0.7 copy-start
  41.4 0.8 %copy-start.1 = (bf16[296,512]{1,0:T(8,128)(2,1)}, bf16[296,512]{1,0:T(8,128)(2,1)S(1)}, u32[]{:S(2)}) copy-start(bf16[296,512]{1,0:T(8,128)(2,1)S(1)} %collective-permute-done.1.rh_ref) | copy-start | bytes 909316
  53.9 0.7 copy-start.4
  54.6 0.7 copy-start.5

commit v2 on v1

v2 whole, which is shorter than its diff:
```python
import math

import jax
import jax.numpy as jnp
import numpy as np
from jax import lax
from jax.experimental import pallas as pl
from jax.experimental.pallas import tpu as pltpu
from jax.sharding import PartitionSpec as P

BF = jnp.bfloat16
F32 = jnp.float32
LEV, D, FF, HEADS, HD = 4, 512, 2048, 8, 64
ROWS = COLS = 12
PIECE = 6 * LEV
GROUP = 3 * PIECE
PER_RT = 2 * GROUP
HALF = 2 * PER_RT
TOKENS = 2 * HALF
EPS = 1e-05
BIG = 1e30
EXP_SCALE = math.log2(math.e) / math.sqrt(HD)
VMEM_LIMIT = 56 * 1024 * 1024
FCHUNK = 512
STAGE = 8


def token_tables():
    pick = np.zeros((HALF, 128), np.float32)
    lane = np.zeros((HALF, 128), np.float32)
    for row in range(6):
        for col in range(COLS):
            for level in range(LEV):
                t = (row * COLS + col) * LEV + level
                pick[t, row * LEV + level] = 1.0
                lane[t, col] = 1.0
    level = np.arange(HALF) % LEV
    row = np.arange(HALF) // (COLS * LEV)
    adds = np.zeros((HALF, 128), np.float32)
    adds[:, 0] = level // 2
    adds[:, 1] = 4 * (level == 0) + np.where((level == 1) | (level == 2), 0, 1)
    adds[:, 2] = 2 * (row < 3)
    return pick, lane, adds


def layer_norm(x, gain):
    mean = jnp.mean(x, axis=-1, keepdims=True)
    centered = x - mean
    variance = jnp.mean(centered * centered, axis=-1, keepdims=True)
    return centered * lax.rsqrt(variance + EPS) * gain


def one_hot(labels, rows):
    lane = lax.broadcasted_iota(jnp.int32, (rows, 128), 1) & 63
    return lane.astype(F32) == labels


def query_features(labels, rows):
    return jnp.where(one_hot(labels, rows), -BIG, 0.0).astype(BF)


def key_features(labels, rows):
    return jnp.where(one_hot(labels, rows), 0.0, 1.0).astype(BF)


def low_lanes(rows):
    return lax.broadcasted_iota(jnp.int32, (rows, 128), 1) < 64


def attend(q, k, v, qf, kf):
    m, n = q.shape[0], k.shape[0]
    low_q, low_k = low_lanes(m), low_lanes(n)
    ones = jnp.ones((n, 128), BF)
    tiles = []
    for first in range(0, HEADS, STAGE):
        heads = range(first, first + STAGE)
        scores, weights, got = [], [], []
        for h in heads:
            lanes = slice(h // 2 * 128, (h // 2 + 1) * 128)
            if h % 2:
                qh, kh = jnp.where(low_q, qf, q[:, lanes]), jnp.where(low_k, kf, k[:, lanes])
            else:
                qh, kh = jnp.where(low_q, q[:, lanes], qf), jnp.where(low_k, k[:, lanes], kf)
            scores.append(lax.dot_general(qh, kh, (((1,), (1,)), ((), ())), preferred_element_type=F32))
        for s in scores:
            peak = jnp.max(s, axis=-1, keepdims=True)
            weights.append(jnp.exp2((s - peak) * EXP_SCALE).astype(BF))
        for h, e in zip(heads, weights):
            lanes = slice(h // 2 * 128, (h // 2 + 1) * 128)
            vh = jnp.where(low_k, ones, v[:, lanes]) if h % 2 else jnp.where(low_k, v[:, lanes], ones)
            got.append(jnp.dot(e, vh, preferred_element_type=F32))
        for even, odd in zip(got[::2], got[1::2]):
            num = jnp.where(low_q, even, odd)
            den = pltpu.roll(jnp.where(low_q, odd, even), 64, 1)
            tiles.append(num / den)
    return jnp.concatenate(tiles, axis=1)


def mlp(h, gain, wup, wdown):
    a = layer_norm(h, gain).astype(BF)
    acc = h
    for c in range(0, FF, FCHUNK):
        u = jnp.dot(a, wup[:, c : c + FCHUNK], preferred_element_type=F32)
        g = jax.nn.gelu(u).astype(BF)
        acc = acc + jnp.dot(g, wdown[c : c + FCHUNK, :], preferred_element_type=F32)
    return acc


class Weights:
    def __init__(self, block, sources, buffers, sem):
        self.copies = [
            pltpu.make_async_copy(s.at[block], b, sem.at[i]) for i, (s, b) in enumerate(zip(sources, buffers))
        ]
        for c in self.copies:
            c.start()

    def wait(self, i):
        self.copies[i].wait()


WEIGHT_SCRATCH = [
    pltpu.VMEM((D, 3 * D), BF),
    pltpu.VMEM((D, D), BF),
    pltpu.VMEM((D, FF), BF),
    pltpu.VMEM((FF, D), BF),
    pltpu.SemaphoreType.DMA((4,)),
]


def token_labels(region_ref, half, pick_ref, lane_ref, adds_ref, lab_s, first_row):
    lab_s[...] = jnp.zeros_like(lab_s)
    for row in range(6):
        lab_s[row * LEV : (row + 1) * LEV, 0:COLS] = region_ref[half * 6 + row].astype(F32)
    rows = jnp.dot(pick_ref[...], lab_s[...].astype(BF), preferred_element_type=F32)
    region = jnp.sum(rows * lane_ref[...].astype(F32), axis=-1, keepdims=True)
    lab1 = region * 2 + adds_ref[:, 0:1]
    lab2 = region * 8 + adds_ref[:, 1:2]
    if half == 0:
        lab2 = lab2 + adds_ref[:, 2:3] * first_row
    return lab1, lab2


def piece(row, side):
    start = row * 2 * PIECE + side * PIECE
    return slice(start, start + PIECE)


def grouped(value, rt, side):
    return jnp.concatenate([value[piece(rt * 3 + r, side)] for r in range(3)], axis=0)


def first_kernel(
    x_ref, region_ref, pick_ref, lane_ref, adds_ref, g1_ref, g2_ref, wq_hbm, wp_hbm, wu_hbm, wd_hbm,
    own_ref, up_ref, down_ref, left_ref, right_ref, labs_ref,
    xs, lab_s, wq, wp, wu, wd, sem,
):
    weights = Weights(0, (wq_hbm, wp_hbm, wu_hbm, wd_hbm), (wq, wp, wu, wd), sem)
    first_row = (lax.axis_index("lat") == 0).astype(F32)
    g1, g2 = g1_ref[0:1, :], g2_ref[0:1, :]
    tiles = []
    for half in range(2):
        for n in range(half * 72, half * 72 + 72):
            xs[n * LEV : (n + 1) * LEV, :] = x_ref[n // COLS, n % COLS].astype(F32)
        lab1, lab2 = token_labels(region_ref, half, pick_ref, lane_ref, adds_ref, lab_s, first_row)
        x = xs[half * HALF : (half + 1) * HALF]
        a = layer_norm(x, g1).astype(BF)
        if half == 0:
            weights.wait(0)
        qkv = jnp.dot(a, wq[...], preferred_element_type=F32).astype(BF)
        o = attend(
            qkv[:, :D], qkv[:, D : 2 * D], qkv[:, 2 * D :], query_features(lab1, HALF), key_features(lab1, HALF)
        ).astype(BF)
        if half == 0:
            weights.wait(1)
        h = x + jnp.dot(o, wp[...], preferred_element_type=F32)
        if half == 0:
            weights.wait(2)
            weights.wait(3)
        y = mlp(h, g2, wu, wd)
        order = []
        for i in range(2):
            rt = 2 * half + i
            for side in range(2):
                part = grouped(y, i, side).astype(BF)
                labs_ref[(rt * 2 + side) * GROUP : (rt * 2 + side + 1) * GROUP, :] = jnp.broadcast_to(
                    grouped(lab2, i, side), (GROUP, 128)
                )
                own_ref[rt * 2 + side] = part
                (left_ref, right_ref)[side][rt * GROUP : (rt + 1) * GROUP, :] = part
                if rt == 0:
                    up_ref[side * GROUP : (side + 1) * GROUP, :] = part
                if rt == 3:
                    down_ref[side * GROUP : (side + 1) * GROUP, :] = part
        mine = labs_ref[half * HALF : (half + 1) * HALF, :]
        mine = jnp.concatenate([mine, mine[: 384 - HALF]], axis=0)
        tiles.append(jnp.transpose(mine, (1, 0))[0:8])
    row = lax.broadcasted_iota(jnp.int32, (8, 384), 0)
    tile = jnp.where(row == 0, tiles[0], tiles[1])
    tile = jnp.concatenate([tile, jnp.zeros((8, 128), F32)], axis=1).astype(BF)
    up_ref[PER_RT:, :] = tile
    down_ref[PER_RT:, :] = tile
    left_ref[4 * GROUP :, :] = tile
    right_ref[4 * GROUP :, :] = tile


def columns_of(tile):
    t = jnp.transpose(tile.astype(F32)[:, :384], (1, 0))
    return [t[(g % 4) * GROUP : (g % 4 + 1) * GROUP, g // 4 : g // 4 + 1] for g in range(8)]


def second_body(windows, g1_ref, g2_ref, hbm, out_hbm, scratch, rts):
    wq, wp, wu, wd, sem, o_s, x_s, y_s, out_sem = scratch
    weights = Weights(1, hbm, (wq, wp, wu, wd), sem)
    g1, g2 = g1_ref[1:2, :], g2_ref[1:2, :]
    for index, (own, halo) in enumerate(windows):
        n_own = len(own) * GROUP
        x = jnp.concatenate([s[0].astype(F32) for s in own + halo], axis=0)
        lab = jnp.concatenate([s[1] for s in own + halo], axis=0)
        a = layer_norm(x, g1).astype(BF)
        if index == 0:
            weights.wait(0)
        kv = jnp.dot(a, wq[:, D:], preferred_element_type=F32).astype(BF)
        q = jnp.dot(a[:n_own], wq[:, :D], preferred_element_type=F32).astype(BF)
        o = attend(q, kv[:, :D], kv[:, D:], query_features(lab[:n_own], n_own), key_features(lab, 4 * GROUP))
        for i, s in enumerate(own):
            at, side = s[2]
            for r in range(3):
                rows = piece(at * 3 + r, side)
                o_s[rows, :] = o[i * GROUP + r * PIECE : i * GROUP + (r + 1) * PIECE]
                x_s[rows, :] = x[i * GROUP + r * PIECE : i * GROUP + (r + 1) * PIECE]
    weights.wait(1)
    h = x_s[...] + jnp.dot(o_s[...].astype(BF), wp[...], preferred_element_type=F32)
    weights.wait(2)
    weights.wait(3)
    o_s[...] = mlp(h, g2, wu, wd)
    copies = []
    for i, rt in enumerate(rts):
        for n in range(36):
            t = i * PER_RT + n * LEV
            y_s[i * 3 + n // COLS, n % COLS] = o_s[t : t + LEV, :].astype(BF)
        c = pltpu.make_async_copy(y_s.at[i * 3 : i * 3 + 3], out_hbm.at[rt * 3 : rt * 3 + 3], out_sem.at[i])
        c.start()
        copies.append(c)
    for c in copies:
        c.wait()


def own_labels(lab_ref, rt, side):
    start = (rt * 2 + side) * GROUP
    return lab_ref[start : start + GROUP, 0:1]


def middle_kernel(
    own_ref, lh_ref, rh_ref, lab_ref, g1_ref, g2_ref, wq_hbm, wp_hbm, wu_hbm, wd_hbm, out_hbm, *scratch
):
    windows = []
    for side, halo_ref in enumerate((lh_ref, rh_ref)):
        cols = columns_of(halo_ref[4 * GROUP :, :])
        own = [(own_ref[rt * 2 + side], own_labels(lab_ref, rt, side), (rt - 1, side)) for rt in (1, 2)]
        halo = [(halo_ref[rt * GROUP : (rt + 1) * GROUP, :], cols[rt * 2 + 1 - side]) for rt in (1, 2)]
        windows.append((own, halo))
    second_body(windows, g1_ref, g2_ref, (wq_hbm, wp_hbm, wu_hbm, wd_hbm), out_hbm, scratch, (1, 2))


def edge_kernel(
    out_in, own_ref, above_ref, below_ref, lh_ref, rh_ref, lc_ref, rc_ref, lab_ref, g1_ref, g2_ref,
    wq_hbm, wp_hbm, wu_hbm, wd_hbm, out_hbm, *scratch
):
    windows = []
    for at, (rt, v_ref) in enumerate(((0, above_ref), (3, below_ref))):
        theirs = 3 - rt
        vcols = columns_of(v_ref[PER_RT:, :])
        for side, (h_ref, c_ref) in enumerate(((lh_ref, lc_ref), (rh_ref, rc_ref))):
            hcols = columns_of(h_ref[4 * GROUP :, :])
            ccols = columns_of(c_ref[PER_RT + 8 * at : PER_RT + 8 * at + 8, :])
            own = [(own_ref[rt * 2 + side], own_labels(lab_ref, rt, side), (at, side))]
            halo = [
                (v_ref[side * GROUP : (side + 1) * GROUP, :], vcols[theirs * 2 + side]),
                (h_ref[rt * GROUP : (rt + 1) * GROUP, :], hcols[rt * 2 + 1 - side]),
                (c_ref[at * GROUP : (at + 1) * GROUP, :], ccols[theirs * 2 + 1 - side]),
            ]
            windows.append((own, halo))
    second_body(windows, g1_ref, g2_ref, (wq_hbm, wp_hbm, wu_hbm, wd_hbm), out_hbm, scratch, (0, 3))


SECOND_SCRATCH = WEIGHT_SCRATCH + [
    pltpu.VMEM((HALF, D), F32),
    pltpu.VMEM((HALF, D), F32),
    pltpu.VMEM((6, COLS, LEV, D), BF),
    pltpu.SemaphoreType.DMA((2,)),
]

VM = pl.BlockSpec(memory_space=pltpu.VMEM)
ANY = pl.BlockSpec(memory_space=pl.ANY)


def cost(flops, nbytes):
    return pl.CostEstimate(flops=int(flops), bytes_accessed=int(nbytes), transcendentals=0)


def shift(value, axis, steps):
    count = lax.axis_size(axis)
    return lax.ppermute(value, axis, [(s, (s + steps) % count) for s in range(count)])


def first_call(x, region, norm_gain1, norm_gain2, weights):
    pick, lane, adds = token_tables()
    return pl.pallas_call(
        first_kernel,
        out_shape=(
            jax.ShapeDtypeStruct((8, GROUP, D), BF),
            jax.ShapeDtypeStruct((PER_RT + 8, D), BF),
            jax.ShapeDtypeStruct((PER_RT + 8, D), BF),
            jax.ShapeDtypeStruct((4 * GROUP + 8, D), BF),
            jax.ShapeDtypeStruct((4 * GROUP + 8, D), BF),
            jax.ShapeDtypeStruct((TOKENS, 128), F32),
        ),
        in_specs=[VM] * 7 + [ANY] * 4,
        out_specs=[VM] * 6,
        scratch_shapes=[pltpu.VMEM((TOKENS, D), F32), pltpu.VMEM((128, 128), F32)] + WEIGHT_SCRATCH,
        compiler_params=pltpu.CompilerParams(vmem_limit_bytes=VMEM_LIMIT),
        cost_estimate=cost(4e9, 8e6),
        name="first_block",
    )(x, region, jnp.asarray(pick, BF), jnp.asarray(lane, BF), jnp.asarray(adds), norm_gain1, norm_gain2, *weights)


def second_calls(own, left_halo, right_halo, above, below, left_corner, right_corner, labs, norm_gain1, norm_gain2, weights):
    params = pltpu.CompilerParams(vmem_limit_bytes=VMEM_LIMIT)
    out_shape = jax.ShapeDtypeStruct((ROWS, COLS, LEV, D), BF)
    out = pl.pallas_call(
        middle_kernel,
        out_shape=out_shape,
        in_specs=[VM] * 6 + [ANY] * 4,
        out_specs=ANY,
        scratch_shapes=SECOND_SCRATCH,
        compiler_params=params,
        cost_estimate=cost(2.5e9, 8e6),
        name="second_middle",
    )(own, left_halo, right_halo, labs, norm_gain1, norm_gain2, *weights)
    out = pl.pallas_call(
        edge_kernel,
        out_shape=out_shape,
        in_specs=[ANY] + [VM] * 10 + [ANY] * 4,
        out_specs=ANY,
        scratch_shapes=SECOND_SCRATCH,
        input_output_aliases={0: 0},
        compiler_params=params,
        cost_estimate=cost(2.5e9, 8e6),
        name="second_edge",
    )(out, own, above, below, left_halo, right_halo, left_corner, right_corner, labs, norm_gain1, norm_gain2, *weights)
    return out


def per_device(tokens, region, norm_gain1, qkv_weight, proj_weight, norm_gain2, up_weight, down_weight):
    weights = (qkv_weight, proj_weight, up_weight, down_weight)
    params = pltpu.CompilerParams(vmem_limit_bytes=VMEM_LIMIT)
    own, up, down, left, right, labs = first_call(
        jnp.transpose(tokens, (1, 2, 0, 3)), jnp.transpose(region, (1, 0, 2)), norm_gain1, norm_gain2, weights
    )
    below = shift(up, "lat", -1)
    above = shift(down, "lat", 1)
    right_halo = shift(left, "lon", -1)
    left_halo = shift(right, "lon", 1)
    to_left = jnp.concatenate([above[:GROUP], below[:GROUP], above[PER_RT:], below[PER_RT:]], axis=0)
    to_right = jnp.concatenate([above[GROUP:PER_RT], below[GROUP:PER_RT], above[PER_RT:], below[PER_RT:]], axis=0)
    right_corner = shift(to_left, "lon", -1)
    left_corner = shift(to_right, "lon", 1)

    out = second_calls(own, left_halo, right_halo, above, below, left_corner, right_corner, labs, norm_gain1, norm_gain2, weights)
    return jnp.transpose(out, (2, 0, 1, 3))


def solution(mesh):
    return jax.shard_map(
        per_device,
        mesh=mesh,
        in_specs=(P(None, "lat", "lon", None), P(None, "lat", "lon"), P(), P(), P(), P(), P(), P()),
        out_specs=P(None, "lat", "lon", None),
        check_vma=False,
    )
```

time: 74.9 us -> 54.6 us (0.73)
  Pallas kernels: 43.4 us -> 31.3 us
  local copies, waits for them, and re-layouts: 8.55 us -> 2.17 us
  other arithmetic: 1.79 us -> 0.03 us
    pallas_call x3, Pallas kernels: 43.4 us -> 31.3 us  [the longest x1 12.1 us: first_call(): pl.pallas_call(first_kernel, out_shape=(jax.ShapeDtypeStruct((8, GROUP, D...]
    pallas_call x1 -> x0, local copies, waits for them, and re-layouts: 2.41 us -> none  [per_device(): pl.pallas_call(edge_kernel, out_shape=out_shape, in_specs=[ANY] + [VM] *...]
    unnamed x13 -> x12, local copies, waits for them, and re-layouts: 4.28 us -> 2.15 us
    another operation x12 -> x0, local copies, waits for them, and re-layouts: 0.94 us -> none  [the longest x3 0.44 us: per_device(): labs = jnp.stack([lab1, lab2.reshape(576)], axis=1).astype(F32)]
    convert_element_type x2 -> x0, other arithmetic: 0.8 us -> none  [the longest x1 0.72 us: per_device(): labs = jnp.stack([lab1, lab2.reshape(576)], axis=1).astype(F32)]
where the time goes in v2:
time: 54.6 us; the launch traced here: 54.4 us
  Pallas kernels  31.3 us (57%)
  starting transfers between devices  15.6 us (29%)
  waiting for transfers between devices  4.97 us (9%)
  local copies, waits for them, and re-layouts  2.17 us (4%)
    ppermute x6, starting transfers between devices, shift(): lax.ppermute(value, axis, [(s, (s + steps) % count) for s in range(count)])  15.6 us
    pallas_call x1, Pallas kernels, first_call(): pl.pallas_call(first_kernel, out_shape=(jax.ShapeDtypeStruct((8, GROUP, D...  12.1 us
    pallas_call x1, Pallas kernels, second_calls(): pl.pallas_call(edge_kernel, out_shape=out_shape, in_specs=[ANY] + [VM] *...  10.6 us
    pallas_call x1, Pallas kernels, second_calls(): pl.pallas_call(middle_kernel, out_shape=out_shape, in_specs=[VM] * 6 + [A...  8.56 us
    ppermute x6, waiting for transfers between devices, shift(): lax.ppermute(value, axis, [(s, (s + steps) % count) for s in range(count)])  4.97 us
    unnamed x12, local copies, waits for them, and re-layouts  2.15 us
  transfers between devices with their start and end apart: 6, of which 1 were waited for; matrix products, arithmetic and copies ran while one was open for 0% of the time, Pallas kernels for 16%

profile of v2, /device:TPU:0, one launch (start us, length us, event | category | flops | bytes accessed | tf_op | source)
XLA Modules:
  0.0 54.4 jit_solution(12284813088535508904)
XLA Ops:
  0.0 12.1 %first_block.1 = (bf16[8,72,512]{2,1,0:T(8,128)(2,1)}, bf16[152,512]{1,0:T(8,128)(2,1)}, bf16[152,512]{1,0:T(8,128)(2,1)}, bf16[296,512]{1,0:T(8,128)(2,1)}, bf1...) custom-call(bf16[12,12,4,512]{3,2,1,0:T(4,128)(2,1)} %bitcast.3, s32[12,4,12]{2,1,0:T(4,128)} %bitcast.4, ...), custom_call_target="tpu_custom_call" | custom-call | flops 4000000000 | bytes 8000000 | tf_op jit(solution)/shard_map/first_block/pallas_call | solution.py:308
  12.1 0.1 collective-permute-start.2
  12.2 3.2 %collective-permute-start.3 = (bf16[152,512]{1,0:T(8,128)(2,1)}, bf16[152,512]{1,0:T(8,128)(2,1)S(1)}, u32[]{:S(2)}, u32[]{:S(2)}) collective-permute-start(bf16[152,512]{1,0:T(8,128)(2,1)} %get-tuple-element.16), channel_id=1, source_target_pairs={{0,96},{32,0},{64,32},{96,64},{1,97},{33,1},{65,33},{97,65},{2,98}... | collective-permute-start | bytes 466952 | tf_op jit(solution)/shard_map/ppermute | solution.py:303
  15.5 1.6 %collective-permute-start = (bf16[296,512]{1,0:T(8,128)(2,1)}, bf16[296,512]{1,0:T(8,128)(2,1)S(1)}, u32[]{:S(2)}, u32[]{:S(2)}) collective-permute-start(bf16[296,512]{1,0:T(8,128)(2,1)} %get-tuple-element.12), channel_id=1, source_target_pairs={{0,1},{1,2},{2,3},{3,4},{4,5},{5,6},{6,7},{7,8},{8,9},{9,10},{10,1... | collective-permute-start | bytes 909320 | tf_op jit(solution)/shard_map/ppermute | solution.py:303
  17.1 5.8 %collective-permute-start.1 = (bf16[296,512]{1,0:T(8,128)(2,1)}, bf16[296,512]{1,0:T(8,128)(2,1)S(1)}, u32[]{:S(2)}, u32[]{:S(2)}) collective-permute-start(bf16[296,512]{1,0:T(8,128)(2,1)} %get-tuple-element.13), channel_id=1, source_target_pairs={{0,31},{1,0},{2,1},{3,2},{4,3},{5,4},{6,5},{7,6},{8,7},{9,8},{10,9... | collective-permute-start | bytes 909320 | tf_op jit(solution)/shard_map/ppermute | solution.py:303
  22.9 0.0 collective-permute-done.2.above_ref
  22.9 0.0 copy-start.2
  23.0 0.0 collective-permute-done.3.below_ref
  23.0 0.0 copy-start.3
  23.0 4.8 %collective-permute-start.5 = (bf16[160,512]{1,0:T(8,128)(2,1)S(1)}, bf16[160,512]{1,0:T(8,128)(2,1)S(1)}, u32[]{:S(2)}, u32[]{:S(2)}) collective-permute-start(bf16[160,512]{1,0:T(8,128)(2,1)S(1)} %get-tuple-element.21), channel_id=1, source_target_pairs={{0,31},{1,0},{2,1},{3,2},{4,3},{5,4},{6,5},{7,6},{8,7},{9,8},{10,9... | collective-permute-start | bytes 491528 | tf_op jit(solution)/shard_map/ppermute | solution.py:303
  27.9 0.0 collective-permute-start.4
  27.9 5.0 %collective-permute-done.lh_ref = bf16[296,512]{1,0:T(8,128)(2,1)S(1)} collective-permute-done((bf16[296,512]{1,0:T(8,128)(2,1)}, bf16[296,512]{1,0:T(8,128)(2,1)S(1)}, u32[]{:S(2)}, u32[]{:S(2)}) %collective-permute-start) | collective-permute-done | bytes 303136 | tf_op jit(solution)/shard_map/ppermute | solution.py:303
  32.8 0.0 copy-start
  32.8 0.0 collective-permute-done.1.rh_ref
  32.8 0.0 copy-start.1
  32.8 0.7 %copy-done = bf16[296,512]{1,0:T(8,128)(2,1)} copy-done((bf16[296,512]{1,0:T(8,128)(2,1)}, bf16[296,512]{1,0:T(8,128)(2,1)S(1)}, u32[]{:S(2)}) %copy-start) | copy-done | bytes 303128
  33.5 0.1 copy-done.1
  33.6 8.6 %second_middle.1.out_in = bf16[12,12,4,512]{3,2,1,0:T(4,128)(2,1)} custom-call(bf16[8,72,512]{2,1,0:T(8,128)(2,1)} %get-tuple-element.11.own_ref, bf16[296,512]{1,0:T(8,128)(2,1)} %copy-done, bf16[296,512]{1,0:T(8,128)(2,1)} %copy-done.1, f32[576,128]{1,0:T(8,128)} %get-tuple-element.14.lab_ref, f32[2,512]{1,0:T(2,128)} %g1_ref.5, f32[2,512]{1,0:T(2,128)} %g2_ref.5, ...), custom_call_target="tpu_custom_call" | custom-call | flops 2500000000 | bytes 8000000 | tf_op jit(solution)/shard_map/second_middle/pallas_call | solution.py:330
  42.2 0.0 copy-done.2
  42.2 0.0 copy-done.3
  42.2 0.0 collective-permute-done.5.rc_ref
  42.2 0.0 copy-start.4
  42.3 0.0 collective-permute-done.4.lc_ref
  42.3 0.7 %copy-done.4 = bf16[160,512]{1,0:T(8,128)(2,1)} copy-done((bf16[160,512]{1,0:T(8,128)(2,1)}, bf16[160,512]{1,0:T(8,128)(2,1)S(1)}, u32[]{:S(2)}) %copy-start.4) | copy-done | bytes 163864
  42.9 0.0 copy-start.5
  42.9 0.7 %copy-done.5 = bf16[160,512]{1,0:T(8,128)(2,1)} copy-done((bf16[160,512]{1,0:T(8,128)(2,1)}, bf16[160,512]{1,0:T(8,128)(2,1)S(1)}, u32[]{:S(2)}) %copy-start.5) | copy-done | bytes 163864
  43.6 10.6 %second_edge.1 = bf16[12,12,4,512]{3,2,1,0:T(4,128)(2,1)} custom-call(bf16[12,12,4,512]{3,2,1,0:T(4,128)(2,1)} %second_middle.1.out_in, bf16[8,72,512]{2,1,0:T(8,128)(2,1)} %get-tuple-element.11.own_ref, bf16[152,512]{1,0:T(8,128)(2,1)} %copy-done.2, bf16[152,512]{1,0:T(8,128)(2,1)} %copy-done.3, ...), custom_call_target="tpu_custom_call", output_to_operand_aliasing={{}: (0, {})} | custom-call | flops 2500000000 | bytes 8000000 | tf_op jit(solution)/shard_map/second_edge/pallas_call | solution.py:340
  (5 shorter events, 0.1 us)
Async XLA Ops:
  12.1 10.8 %collective-permute-start.2 = (bf16[152,512]{1,0:T(8,128)(2,1)}, bf16[152,512]{1,0:T(8,128)(2,1)S(1)}, u32[]{:S(2)}, u32[]{:S(2)}) collective-permute-start(bf16[152,512]{1,0:T(8,128)(2,1)} %get-tuple-element.15), channel_id=1, source_target_pairs={{0,32},{32,64},{64,96},{96,0},{1,33},{33,65},{65,97},{97,1},{2,34}... | collective-permute-start | bytes 466952 | tf_op jit(solution)/shard_map/ppermute | solution.py:303
  12.2 10.7 %collective-permute-start.3 = (bf16[152,512]{1,0:T(8,128)(2,1)}, bf16[152,512]{1,0:T(8,128)(2,1)S(1)}, u32[]{:S(2)}, u32[]{:S(2)}) collective-permute-start(bf16[152,512]{1,0:T(8,128)(2,1)} %get-tuple-element.16), channel_id=1, source_target_pairs={{0,96},{32,0},{64,32},{96,64},{1,97},{33,1},{65,33},{97,65},{2,98}... | collective-permute-start | bytes 466952 | tf_op jit(solution)/shard_map/ppermute | solution.py:303
  15.5 17.4 %collective-permute-start = (bf16[296,512]{1,0:T(8,128)(2,1)}, bf16[296,512]{1,0:T(8,128)(2,1)S(1)}, u32[]{:S(2)}, u32[]{:S(2)}) collective-permute-start(bf16[296,512]{1,0:T(8,128)(2,1)} %get-tuple-element.12), channel_id=1, source_target_pairs={{0,1},{1,2},{2,3},{3,4},{4,5},{5,6},{6,7},{7,8},{8,9},{9,10},{10,1... | collective-permute-start | bytes 909320 | tf_op jit(solution)/shard_map/ppermute | solution.py:303
  17.1 15.7 %collective-permute-start.1 = (bf16[296,512]{1,0:T(8,128)(2,1)}, bf16[296,512]{1,0:T(8,128)(2,1)S(1)}, u32[]{:S(2)}, u32[]{:S(2)}) collective-permute-start(bf16[296,512]{1,0:T(8,128)(2,1)} %get-tuple-element.13), channel_id=1, source_target_pairs={{0,31},{1,0},{2,1},{3,2},{4,3},{5,4},{6,5},{7,6},{8,7},{9,8},{10,9... | collective-permute-start | bytes 909320 | tf_op jit(solution)/shard_map/ppermute | solution.py:303
  22.9 19.3 %copy-start.2 = (bf16[152,512]{1,0:T(8,128)(2,1)}, bf16[152,512]{1,0:T(8,128)(2,1)S(1)}, u32[]{:S(2)}) copy-start(bf16[152,512]{1,0:T(8,128)(2,1)S(1)} %collective-permute-done.2.above_ref) | copy-start | bytes 466948
  23.0 19.3 %copy-start.3 = (bf16[152,512]{1,0:T(8,128)(2,1)}, bf16[152,512]{1,0:T(8,128)(2,1)S(1)}, u32[]{:S(2)}) copy-start(bf16[152,512]{1,0:T(8,128)(2,1)S(1)} %collective-permute-done.3.below_ref) | copy-start | bytes 466948
  23.0 19.2 %collective-permute-start.5 = (bf16[160,512]{1,0:T(8,128)(2,1)S(1)}, bf16[160,512]{1,0:T(8,128)(2,1)S(1)}, u32[]{:S(2)}, u32[]{:S(2)}) collective-permute-start(bf16[160,512]{1,0:T(8,128)(2,1)S(1)} %get-tuple-element.21), channel_id=1, source_target_pairs={{0,31},{1,0},{2,1},{3,2},{4,3},{5,4},{6,5},{7,6},{8,7},{9,8},{10,9... | collective-permute-start | bytes 491528 | tf_op jit(solution)/shard_map/ppermute | solution.py:303
  27.9 14.4 %collective-permute-start.4 = (bf16[160,512]{1,0:T(8,128)(2,1)S(1)}, bf16[160,512]{1,0:T(8,128)(2,1)S(1)}, u32[]{:S(2)}, u32[]{:S(2)}) collective-permute-start(bf16[160,512]{1,0:T(8,128)(2,1)S(1)} %get-tuple-element.22), channel_id=1, source_target_pairs={{0,1},{1,2},{2,3},{3,4},{4,5},{5,6},{6,7},{7,8},{8,9},{9,10},{10,1... | collective-permute-start | bytes 491528 | tf_op jit(solution)/shard_map/ppermute | solution.py:303
  32.8 0.7 %copy-start = (bf16[296,512]{1,0:T(8,128)(2,1)}, bf16[296,512]{1,0:T(8,128)(2,1)S(1)}, u32[]{:S(2)}) copy-start(bf16[296,512]{1,0:T(8,128)(2,1)S(1)} %collective-permute-done.lh_ref) | copy-start | bytes 909316
  32.8 0.8 %copy-start.1 = (bf16[296,512]{1,0:T(8,128)(2,1)}, bf16[296,512]{1,0:T(8,128)(2,1)S(1)}, u32[]{:S(2)}) copy-start(bf16[296,512]{1,0:T(8,128)(2,1)S(1)} %collective-permute-done.1.rh_ref) | copy-start | bytes 909316
  42.2 0.7 %copy-start.4 = (bf16[160,512]{1,0:T(8,128)(2,1)}, bf16[160,512]{1,0:T(8,128)(2,1)S(1)}, u32[]{:S(2)}) copy-start(bf16[160,512]{1,0:T(8,128)(2,1)S(1)} %collective-permute-done.5.rc_ref) | copy-start | bytes 491524
  42.9 0.7 %copy-start.5 = (bf16[160,512]{1,0:T(8,128)(2,1)}, bf16[160,512]{1,0:T(8,128)(2,1)S(1)}, u32[]{:S(2)}) copy-start(bf16[160,512]{1,0:T(8,128)(2,1)S(1)} %collective-permute-done.4.lc_ref) | copy-start | bytes 491524

commit v3 on v2

v3 whole, which is shorter than its diff:
```python
import math

import jax
import jax.numpy as jnp
import numpy as np
from jax import lax
from jax.experimental import pallas as pl
from jax.experimental.pallas import tpu as pltpu
from jax.sharding import PartitionSpec as P

BF = jnp.bfloat16
F32 = jnp.float32
LEV, D, FF, HEADS, HD = 4, 512, 2048, 8, 64
ROWS = COLS = 12
PIECE = 6 * LEV
GROUP = 3 * PIECE
PER_RT = 2 * GROUP
HALF = 2 * PER_RT
TOKENS = 2 * HALF
EPS = 1e-05
BIG = 1e30
EXP_SCALE = math.log2(math.e) / math.sqrt(HD)
VMEM_LIMIT = 40 * 1024 * 1024
FCHUNK = 512
STAGE = 8


def token_tables():
    pick = np.zeros((HALF, 128), np.float32)
    lane = np.zeros((HALF, 128), np.float32)
    for row in range(6):
        for col in range(COLS):
            for level in range(LEV):
                t = (row * COLS + col) * LEV + level
                pick[t, row * LEV + level] = 1.0
                lane[t, col] = 1.0
    level = np.arange(HALF) % LEV
    row = np.arange(HALF) // (COLS * LEV)
    adds = np.zeros((HALF, 128), np.float32)
    adds[:, 0] = level // 2
    adds[:, 1] = 4 * (level == 0) + np.where((level == 1) | (level == 2), 0, 1)
    adds[:, 2] = 2 * (row < 3)
    return pick, lane, adds


def layer_norm(x, gain):
    mean = jnp.mean(x, axis=-1, keepdims=True)
    centered = x - mean
    variance = jnp.mean(centered * centered, axis=-1, keepdims=True)
    return centered * lax.rsqrt(variance + EPS) * gain


def one_hot(labels, rows):
    lane = lax.broadcasted_iota(jnp.int32, (rows, 128), 1) & 63
    return lane.astype(F32) == labels


def query_features(labels, rows):
    return jnp.where(one_hot(labels, rows), -BIG, 0.0).astype(BF)


def key_features(labels, rows):
    return jnp.where(one_hot(labels, rows), 0.0, 1.0).astype(BF)


def low_lanes(rows):
    return lax.broadcasted_iota(jnp.int32, (rows, 128), 1) < 64


def attend(q, k, v, qf, kf):
    m, n = q.shape[0], k.shape[0]
    low_q, low_k = low_lanes(m), low_lanes(n)
    ones = jnp.ones((n, 128), BF)
    tiles = []
    for first in range(0, HEADS, STAGE):
        heads = range(first, first + STAGE)
        scores, weights, got = [], [], []
        for h in heads:
            lanes = slice(h // 2 * 128, (h // 2 + 1) * 128)
            if h % 2:
                qh, kh = jnp.where(low_q, qf, q[:, lanes]), jnp.where(low_k, kf, k[:, lanes])
            else:
                qh, kh = jnp.where(low_q, q[:, lanes], qf), jnp.where(low_k, k[:, lanes], kf)
            scores.append(lax.dot_general(qh, kh, (((1,), (1,)), ((), ())), preferred_element_type=F32))
        for s in scores:
            peak = jnp.max(s, axis=-1, keepdims=True)
            weights.append(jnp.exp2((s - peak) * EXP_SCALE).astype(BF))
        for h, e in zip(heads, weights):
            lanes = slice(h // 2 * 128, (h // 2 + 1) * 128)
            vh = jnp.where(low_k, ones, v[:, lanes]) if h % 2 else jnp.where(low_k, v[:, lanes], ones)
            got.append(jnp.dot(e, vh, preferred_element_type=F32))
        for even, odd in zip(got[::2], got[1::2]):
            num = jnp.where(low_q, even, odd)
            den = pltpu.roll(jnp.where(low_q, odd, even), 64, 1)
            tiles.append(num / den)
    return jnp.concatenate(tiles, axis=1)


def token_labels(region_ref, half, pick_ref, lane_ref, adds_ref, lab_s, first_row):
    lab_s[...] = jnp.zeros_like(lab_s)
    for row in range(6):
        lab_s[row * LEV : (row + 1) * LEV, 0:COLS] = region_ref[half * 6 + row].astype(F32)
    rows = jnp.dot(pick_ref[...], lab_s[...].astype(BF), preferred_element_type=F32)
    region = jnp.sum(rows * lane_ref[...].astype(F32), axis=-1, keepdims=True)
    lab1 = region * 2 + adds_ref[:, 0:1]
    lab2 = region * 8 + adds_ref[:, 1:2]
    if half == 0:
        lab2 = lab2 + adds_ref[:, 2:3] * first_row
    return lab1, lab2


def piece(row, side):
    start = row * 2 * PIECE + side * PIECE
    return slice(start, start + PIECE)


def grouped(value, rt, side):
    return jnp.concatenate([value[piece(rt * 3 + r, side)] for r in range(3)], axis=0)


class Inputs:
    def __init__(self, pairs, sem):
        self.copies = [pltpu.make_async_copy(s, b, sem.at[i]) for i, (s, b) in enumerate(pairs)]
        for c in self.copies:
            c.start()

    def wait(self, *which):
        for i in which:
            self.copies[i].wait()


def mlp_chunks(wu_hbm, wd_hbm, block, wu, wd):
    pairs = []
    for c in range(0, FF, FCHUNK):
        pairs.append((wu_hbm.at[block, :, c : c + FCHUNK], wu.at[:, c : c + FCHUNK]))
        pairs.append((wd_hbm.at[block, c : c + FCHUNK, :], wd.at[c : c + FCHUNK, :]))
    return pairs


N_CHUNK = 2 * (FF // FCHUNK)


def mlp(h, gain, wup, wdown, arrived):
    a = layer_norm(h, gain).astype(BF)
    acc = h
    for i, c in enumerate(range(0, FF, FCHUNK)):
        arrived(2 * i, 2 * i + 1)
        u = jnp.dot(a, wup[:, c : c + FCHUNK], preferred_element_type=F32)
        g = jax.nn.gelu(u).astype(BF)
        acc = acc + jnp.dot(g, wdown[c : c + FCHUNK, :], preferred_element_type=F32)
    return acc


def first_kernel(
    x_hbm, region_ref, pick_ref, lane_ref, adds_ref, g1_ref, g2_ref, wq_hbm, wp_hbm, wu_hbm, wd_hbm,
    up_ref, down_ref, tile_ref, mid_hbm,
    xv, xs, lab_s, labs, wq, wp, wu, wd, sem, mid_sem,
):
    inputs = Inputs(
        [(x_hbm.at[0:6], xv.at[0:6]), (wq_hbm.at[0], wq), (x_hbm.at[6:12], xv.at[6:12]), (wp_hbm.at[0], wp)]
        + mlp_chunks(wu_hbm, wd_hbm, 0, wu, wd),
        sem,
    )
    first_row = (lax.axis_index("lat") == 0).astype(F32)
    g1, g2 = g1_ref[0:1, :], g2_ref[0:1, :]
    tiles = []
    for half in range(2):
        lab1, lab2 = token_labels(region_ref, half, pick_ref, lane_ref, adds_ref, lab_s, first_row)
        inputs.wait(2 * half)
        for n in range(half * 72, half * 72 + 72):
            xs[n * LEV : (n + 1) * LEV, :] = xv[n // COLS, n % COLS].astype(F32)
        rows = slice(half * HALF, (half + 1) * HALF)
        a = layer_norm(xs[rows], g1).astype(BF)
        if half == 0:
            inputs.wait(1)
        qkv = jnp.dot(a, wq[...], preferred_element_type=F32).astype(BF)
        o = attend(
            qkv[:, :D], qkv[:, D : 2 * D], qkv[:, 2 * D :], query_features(lab1, HALF), key_features(lab1, HALF)
        ).astype(BF)
        if half == 0:
            inputs.wait(3)
        xs[rows] = xs[rows] + jnp.dot(o, wp[...], preferred_element_type=F32)
        for i in range(2):
            for side in range(2):
                start = (i * 2 + side) * GROUP
                labs[start : start + GROUP, :] = jnp.broadcast_to(grouped(lab2, i, side), (GROUP, 128))
        tiles.append(jnp.transpose(labs[...], (1, 0))[0:8])
    mid = pltpu.make_async_copy(xs.at[PER_RT : 3 * PER_RT], mid_hbm, mid_sem)
    mid.start()
    row = lax.broadcasted_iota(jnp.int32, (8, 384), 0)
    tile = jnp.where(row == 0, tiles[0], tiles[1])
    tile = jnp.concatenate([tile, jnp.zeros((8, 128), F32)], axis=1).astype(BF)
    tile_ref[...] = tile
    h = jnp.concatenate([xs[0:PER_RT], xs[3 * PER_RT :]], axis=0)
    y = mlp(h, g2, wu, wd, lambda *which: inputs.wait(*[4 + w for w in which]))
    for i, ref in enumerate((up_ref, down_ref)):
        for side in range(2):
            ref[side * GROUP : (side + 1) * GROUP, :] = grouped(y, i, side).astype(BF)
        ref[PER_RT:, :] = tile
    mid.wait()


def middle_mlp_kernel(mid_hbm, tile_ref, g2_ref, wu_hbm, wd_hbm, left_ref, right_ref, mid, wu, wd, sem):
    inputs = Inputs([(mid_hbm, mid)] + mlp_chunks(wu_hbm, wd_hbm, 0, wu, wd), sem)
    inputs.wait(0)
    y = mlp(mid[...], g2_ref[0:1, :], wu, wd, lambda *which: inputs.wait(*[1 + w for w in which]))
    for side, ref in enumerate((left_ref, right_ref)):
        for i in range(2):
            ref[i * GROUP : (i + 1) * GROUP, :] = grouped(y, i, side).astype(BF)
        ref[PER_RT:, :] = tile_ref[...]


def columns_of(tile):
    t = jnp.transpose(tile.astype(F32)[:, :384], (1, 0))
    return [t[(g % 4) * GROUP : (g % 4 + 1) * GROUP, g // 4 : g // 4 + 1] for g in range(8)]


def second_body(arrays, windows_of, g1_ref, g2_ref, hbm, out_hbm, scratch, rts):
    wq, wp, wu, wd, sem, o_s, x_s, y_s, out_sem, *buffers = scratch
    wq_hbm, wp_hbm, wu_hbm, wd_hbm = hbm
    inputs = Inputs(
        list(zip(arrays, buffers))
        + [(wq_hbm.at[1, :, D:], wq.at[:, D:]), (wq_hbm.at[1, :, :D], wq.at[:, :D]), (wp_hbm.at[1], wp)]
        + mlp_chunks(wu_hbm, wd_hbm, 1, wu, wd),
        sem,
    )
    at_weights = len(arrays)
    g1, g2 = g1_ref[1:2, :], g2_ref[1:2, :]
    inputs.wait(*range(at_weights))
    for index, (own, halo) in enumerate(windows_of(*buffers)):
        n_own = len(own) * GROUP
        x = jnp.concatenate([s[0].astype(F32) for s in own + halo], axis=0)
        lab = jnp.concatenate([s[1] for s in own + halo], axis=0)
        a = layer_norm(x, g1).astype(BF)
        if index == 0:
            inputs.wait(at_weights)
        kv = jnp.dot(a, wq[:, D:], preferred_element_type=F32).astype(BF)
        if index == 0:
            inputs.wait(at_weights + 1)
        q = jnp.dot(a[:n_own], wq[:, :D], preferred_element_type=F32).astype(BF)
        o = attend(q, kv[:, :D], kv[:, D:], query_features(lab[:n_own], n_own), key_features(lab, 4 * GROUP))
        for i, s in enumerate(own):
            at, side = s[2]
            for r in range(3):
                rows = piece(at * 3 + r, side)
                o_s[rows, :] = o[i * GROUP + r * PIECE : i * GROUP + (r + 1) * PIECE]
                x_s[rows, :] = x[i * GROUP + r * PIECE : i * GROUP + (r + 1) * PIECE]
    inputs.wait(at_weights + 2)
    h = x_s[...] + jnp.dot(o_s[...].astype(BF), wp[...], preferred_element_type=F32)
    o_s[...] = mlp(h, g2, wu, wd, lambda *which: inputs.wait(*[at_weights + 3 + w for w in which]))
    copies = []
    for i, rt in enumerate(rts):
        for n in range(36):
            t = i * PER_RT + n * LEV
            y_s[i * 3 + n // COLS, n % COLS] = o_s[t : t + LEV, :].astype(BF)
        c = pltpu.make_async_copy(y_s.at[i * 3 : i * 3 + 3], out_hbm.at[rt * 3 : rt * 3 + 3], out_sem.at[i])
        c.start()
        copies.append(c)
    for c in copies:
        c.wait()


def rows_of(ref, i):
    return ref[i * GROUP : (i + 1) * GROUP, :]


def middle_windows(left, right, left_halo, right_halo):
    mine = columns_of(left[PER_RT:, :])
    windows = []
    for side, (own_ref, halo_ref) in enumerate(((left, left_halo), (right, right_halo))):
        theirs = columns_of(halo_ref[PER_RT:, :])
        own = [(rows_of(own_ref, rt - 1), mine[rt * 2 + side], (rt - 1, side)) for rt in (1, 2)]
        halo = [(rows_of(halo_ref, rt - 1), theirs[rt * 2 + 1 - side]) for rt in (1, 2)]
        windows.append((own, halo))
    return windows


def edge_windows(up, down, above, below, left_halo, right_halo):
    mine = columns_of(up[PER_RT:, :])
    beside = []
    for ref in (left_halo, right_halo):
        beside.append([columns_of(ref[4 * GROUP + 8 * i : 4 * GROUP + 8 * i + 8, :]) for i in range(3)])
    windows = []
    for at, (rt, own_ref, v_ref) in enumerate(((0, up, above), (3, down, below))):
        theirs = columns_of(v_ref[PER_RT:, :])
        for side, ref in enumerate((left_halo, right_halo)):
            labels = beside[side]
            own = [(rows_of(own_ref, side), mine[rt * 2 + side], (at, side))]
            halo = [
                (rows_of(v_ref, side), theirs[(3 - rt) * 2 + side]),
                (rows_of(ref, at), labels[0][rt * 2 + 1 - side]),
                (rows_of(ref, 2 + at), labels[1 + at][(3 - rt) * 2 + 1 - side]),
            ]
            windows.append((own, halo))
    return windows


def middle_kernel(a, b, c, d, g1_ref, g2_ref, wq_hbm, wp_hbm, wu_hbm, wd_hbm, out_hbm, *scratch):
    hbm = (wq_hbm, wp_hbm, wu_hbm, wd_hbm)
    second_body((a, b, c, d), middle_windows, g1_ref, g2_ref, hbm, out_hbm, scratch, (1, 2))


def edge_kernel(out_in, a, b, c, d, e, f, g1_ref, g2_ref, wq_hbm, wp_hbm, wu_hbm, wd_hbm, out_hbm, *scratch):
    hbm = (wq_hbm, wp_hbm, wu_hbm, wd_hbm)
    second_body((a, b, c, d, e, f), edge_windows, g1_ref, g2_ref, hbm, out_hbm, scratch, (0, 3))


MLP_SCRATCH = [pltpu.VMEM((D, FF), BF), pltpu.VMEM((FF, D), BF)]
WEIGHT_SCRATCH = [pltpu.VMEM((D, 3 * D), BF), pltpu.VMEM((D, D), BF)] + MLP_SCRATCH


def dma(n):
    return pltpu.SemaphoreType.DMA((n,))


def second_scratch(arrays):
    return (
        WEIGHT_SCRATCH
        + [dma(len(arrays) + 3 + N_CHUNK), pltpu.VMEM((HALF, D), F32), pltpu.VMEM((HALF, D), F32)]
        + [pltpu.VMEM((6, COLS, LEV, D), BF), dma(2)]
        + [pltpu.VMEM(a.shape, BF) for a in arrays]
    )


VM = pl.BlockSpec(memory_space=pltpu.VMEM)
ANY = pl.BlockSpec(memory_space=pl.ANY)
HBM = pl.BlockSpec(memory_space=pltpu.HBM)


def cost(flops, nbytes):
    return pl.CostEstimate(flops=int(flops), bytes_accessed=int(nbytes), transcendentals=0)


def in_hbm(value):
    return pltpu.with_memory_space_constraint(value, pltpu.HBM)


def exchange(to_before, to_after, axis):
    count = lax.axis_size(axis)
    odd = lax.axis_index(axis) % 2 == 1
    even_pairs = [(s, s + 1 - 2 * (s % 2)) for s in range(count)]
    odd_pairs = [(s, (s - 1 + 2 * (s % 2)) % count) for s in range(count)]
    one = lax.ppermute(jnp.where(odd, to_before, to_after), axis, even_pairs)
    two = lax.ppermute(jnp.where(odd, to_after, to_before), axis, odd_pairs)
    return one, two, odd


def sorted_out(one, two, odd):
    return jnp.where(odd, one, two), jnp.where(odd, two, one)


def first_calls(tokens, region, g1, g2, weights):
    pick, lane, adds = token_tables()
    tables = [in_hbm(jnp.asarray(t, d)) for t, d in ((pick, BF), (lane, BF), (adds, F32))]
    params = pltpu.CompilerParams(vmem_limit_bytes=VMEM_LIMIT)
    edge_out = jax.ShapeDtypeStruct((PER_RT + 8, D), BF)
    up, down, tile, mid = pl.pallas_call(
        first_kernel,
        out_shape=(
            edge_out, edge_out, jax.ShapeDtypeStruct((8, D), BF), jax.ShapeDtypeStruct((HALF, D), F32),
        ),
        in_specs=[HBM] + [VM] * 6 + [HBM] * 4,
        out_specs=[VM] * 3 + [ANY],
        scratch_shapes=[
            pltpu.VMEM((ROWS, COLS, LEV, D), BF), pltpu.VMEM((TOKENS, D), F32), pltpu.VMEM((128, 128), F32),
            pltpu.VMEM((384, 128), F32),
        ] + WEIGHT_SCRATCH + [dma(4 + N_CHUNK), pltpu.SemaphoreType.DMA],
        compiler_params=params,
        cost_estimate=cost(4e9, 8e6),
        name="first_block",
    )(tokens, region, *tables, g1, g2, *weights)
    left, right = pl.pallas_call(
        middle_mlp_kernel,
        out_shape=(edge_out, edge_out),
        in_specs=[ANY, VM, VM, HBM, HBM],
        out_specs=[VM] * 2,
        scratch_shapes=[pltpu.VMEM((HALF, D), F32)] + MLP_SCRATCH + [dma(1 + N_CHUNK)],
        compiler_params=params,
        cost_estimate=cost(1.3e9, 5e6),
        name="first_middle",
    )(mid, tile, g2, weights[2], weights[3])
    return up, down, left, right


def second_call(kernel, arrays, g1, g2, weights, out=None, name=None):
    given = () if out is None else (out,)
    return pl.pallas_call(
        kernel,
        out_shape=jax.ShapeDtypeStruct((ROWS, COLS, LEV, D), BF),
        in_specs=[HBM] * len(given) + [ANY] * len(arrays) + [VM] * 2 + [HBM] * 4,
        out_specs=HBM,
        scratch_shapes=second_scratch(arrays),
        input_output_aliases={0: 0} if given else {},
        compiler_params=pltpu.CompilerParams(vmem_limit_bytes=VMEM_LIMIT),
        cost_estimate=cost(2.5e9, 8e6),
        name=name,
    )(*given, *arrays, g1, g2, *weights)


def per_device(tokens, region, norm_gain1, qkv_weight, proj_weight, norm_gain2, up_weight, down_weight):
    weights = [in_hbm(w) for w in (qkv_weight, proj_weight, up_weight, down_weight)]
    g1, g2 = in_hbm(norm_gain1), in_hbm(norm_gain2)
    up, down, left, right = first_calls(
        in_hbm(jnp.transpose(tokens, (1, 2, 0, 3))), in_hbm(jnp.transpose(region, (1, 0, 2))), g1, g2, weights
    )
    one, two, odd = exchange(up, down, "lat")
    left, right, one, two = lax.optimization_barrier((left, right, one, two))
    above, below = sorted_out(one, two, odd)
    left_halo, right_halo = sorted_out(*exchange(left, right, "lon"))

    def edge_of(side):
        rows = slice(side * GROUP, (side + 1) * GROUP)
        tiles = [v[PER_RT:] for v in (up, above, below)]
        return jnp.concatenate([up[rows], down[rows], above[rows], below[rows]] + tiles, axis=0)

    left_edge, right_edge = sorted_out(*exchange(edge_of(0), edge_of(1), "lon"))
    out = second_call(middle_kernel, (left, right, left_halo, right_halo), g1, g2, weights, name="second_middle")
    arrays = (up, down, above, below, left_edge, right_edge)
    out = second_call(edge_kernel, arrays, g1, g2, weights, out, name="second_edge")
    return jnp.transpose(out, (2, 0, 1, 3))


def solution(mesh):
    return jax.shard_map(
        per_device,
        mesh=mesh,
        in_specs=(P(None, "lat", "lon", None), P(None, "lat", "lon"), P(), P(), P(), P(), P(), P()),
        out_specs=P(None, "lat", "lon", None),
        check_vma=False,
    )
```

time: 54.6 us -> 51 us (0.934)
  starting transfers between devices: 15.6 us -> 12.8 us
  Pallas kernels: 31.3 us -> 33.9 us
  local copies, waits for them, and re-layouts: 2.17 us -> 0.06 us
  waiting for transfers between devices: 4.97 us -> 3.44 us
    ppermute x6, starting transfers between devices: 15.6 us -> 12.8 us  [the longest x3 10.9 us: exchange(): two = lax.ppermute(jnp.where(odd, to_after, to_before), axis, odd_pairs)]
    pallas_call x3 -> x4, Pallas kernels: 31.3 us -> 33.9 us  [the longest x2 19.9 us: second_call(): pl.pallas_call(kernel, out_shape=jax.ShapeDtypeStruct((ROWS, COLS, LEV, D...]
    unnamed x12 -> x6, local copies, waits for them, and re-layouts: 2.15 us -> 0.06 us
    ppermute x6, waiting for transfers between devices: 4.97 us -> 3.44 us  [the longest x3 3.43 us: exchange(): two = lax.ppermute(jnp.where(odd, to_after, to_before), axis, odd_pairs)]
  transfers between devices with their start and end apart: 6 -> 6, of which waited for: 1 -> 2; matrix products, arithmetic and copies ran while one was open for 0% -> 0% of each run, Pallas kernels for 16% -> 26%
where the time goes in v3:
time: 51 us; the launch traced here: 50.7 us
  Pallas kernels  33.9 us (66%)
  starting transfers between devices  12.8 us (25%)
  waiting for transfers between devices  3.44 us (7%)
    pallas_call x2, Pallas kernels, second_call(): pl.pallas_call(kernel, out_shape=jax.ShapeDtypeStruct((ROWS, COLS, LEV, D...  19.9 us
    ppermute x3, starting transfers between devices, exchange(): two = lax.ppermute(jnp.where(odd, to_after, to_before), axis, odd_pairs)  10.9 us
    pallas_call x1, Pallas kernels, first_calls(): pl.pallas_call(first_kernel, out_shape=(edge_out, edge_out, jax.ShapeDtyp...  9.67 us
    pallas_call x1, Pallas kernels, first_calls(): pl.pallas_call(middle_mlp_kernel, out_shape=(edge_out, edge_out), in_spec...  4.27 us
    ppermute x3, waiting for transfers between devices, exchange(): two = lax.ppermute(jnp.where(odd, to_after, to_before), axis, odd_pairs)  3.43 us
    ppermute x3, starting transfers between devices, exchange(): one = lax.ppermute(jnp.where(odd, to_before, to_after), axis, even_pairs)  1.83 us
  transfers between devices with their start and end apart: 6, of which 2 were waited for; matrix products, arithmetic and copies ran while one was open for 0% of the time, Pallas kernels for 26%

profile of v3, /device:TPU:0, one launch (start us, length us, event | category | flops | bytes accessed | tf_op | source)
XLA Modules:
  0.0 50.7 jit_solution(15707918317622390647)
XLA Ops:
  0.0 9.7 %first_block.1 = (bf16[152,512]{1,0:T(8,128)(2,1)S(1)}, bf16[152,512]{1,0:T(8,128)(2,1)S(1)}, bf16[8,512]{1,0:T(8,128)(2,1)S(1)}, f32[288,512]{1,0:T(8,128)S(1)}) custom-call(bf16[12,12,4,512]{3,2,1,0:T(4,128)(2,1)} %bitcast.3, s32[12,4,12]{2,1,0:T(4,128)} %bitcast.4, bf16[288,128]{1,0:T(8,128)(2,1)} %constant.35.clone.pick_ref, ...), custom_call_target="tpu_custom_call" | custom-call | flops 4000000000 | bytes 8000000 | tf_op jit(solution)/shard_map/first_block/pallas_call | solution.py:357
  9.7 0.1 collective-permute-start
  9.8 3.2 %collective-permute-start.1 = (bf16[152,512]{1,0:T(8,128)(2,1)S(1)}, bf16[152,512]{1,0:T(8,128)(2,1)S(1)}, u32[]{:S(2)}, u32[]{:S(2)}) collective-permute-start(bf16[152,512]{1,0:T(8,128)(2,1)S(1)} %get-tuple-element.35), channel_id=1, source_target_pairs={{0,96},{32,64},{64,32},{96,0},{1,97},{33,65},{65,33},{97,1},{2,98}... | collective-permute-start | bytes 466952 | tf_op jit(solution)/shard_map/ppermute | solution.py:344
  13.1 4.3 %first_middle.1 = (bf16[152,512]{1,0:T(8,128)(2,1)S(1)}, bf16[152,512]{1,0:T(8,128)(2,1)S(1)}) custom-call(f32[288,512]{1,0:T(8,128)S(1)} %get-tuple-element.15.mid_hbm, bf16[8,512]{1,0:T(8,128)(2,1)S(1)} %get-tuple-element.16.tile_ref, f32[2,512]{1,0:T(2,128)} %g2_ref.7, bf16[2,512,2048]{2,1,0:T(8,128)(2,1)} %wu_hbm.7, bf16[2,2048,512]{2,1,0:T(8,128)(2,1)} %wd_hbm.7), custom_call_target="tpu_custom_call" | custom-call | flops 1300000000 | bytes 5000000 | tf_op jit(solution)/shard_map/first_middle/pallas_call | solution.py:372
  17.3 0.0 collective-permute-done
  17.4 0.0 collective-permute-done.1
  17.4 1.7 %collective-permute-start.2 = (bf16[152,512]{1,0:T(8,128)(2,1)S(1)}, bf16[152,512]{1,0:T(8,128)(2,1)S(1)}, u32[]{:S(2)}, u32[]{:S(2)}) collective-permute-start(bf16[152,512]{1,0:T(8,128)(2,1)S(1)} %get-tuple-element.34), channel_id=1, source_target_pairs={{0,1},{1,0},{2,3},{3,2},{4,5},{5,4},{6,7},{7,6},{8,9},{9,8},{10,11... | collective-permute-start | bytes 466952 | tf_op jit(solution)/shard_map/ppermute | solution.py:343
  19.1 6.5 %collective-permute-start.3 = (bf16[152,512]{1,0:T(8,128)(2,1)S(1)}, bf16[152,512]{1,0:T(8,128)(2,1)S(1)}, u32[]{:S(2)}, u32[]{:S(2)}) collective-permute-start(bf16[152,512]{1,0:T(8,128)(2,1)S(1)} %get-tuple-element.33), channel_id=1, source_target_pairs={{0,31},{1,2},{2,1},{3,4},{4,3},{5,6},{6,5},{7,8},{8,7},{9,10},{10,... | collective-permute-start | bytes 466952 | tf_op jit(solution)/shard_map/ppermute | solution.py:344
  25.7 0.1 collective-permute-start.4
  25.8 1.3 %collective-permute-start.5 = (bf16[312,512]{1,0:T(8,128)(2,1)S(1)}, bf16[312,512]{1,0:T(8,128)(2,1)S(1)}, u32[]{:S(2)}, u32[]{:S(2)}) collective-permute-start(bf16[312,512]{1,0:T(8,128)(2,1)S(1)} %get-tuple-element.27), channel_id=1, source_target_pairs={{0,31},{1,2},{2,1},{3,4},{4,3},{5,6},{6,5},{7,8},{8,7},{9,10},{10,... | collective-permute-start | bytes 958472 | tf_op jit(solution)/shard_map/ppermute | solution.py:344
  27.0 0.0 collective-permute-done.2
  27.1 2.9 %collective-permute-done.3 = bf16[152,512]{1,0:T(8,128)(2,1)S(1)} collective-permute-done((bf16[152,512]{1,0:T(8,128)(2,1)S(1)}, bf16[152,512]{1,0:T(8,128)(2,1)S(1)}, u32[]{:S(2)}, u32[]{:S(2)}) %collective-permute-start.3) | collective-permute-done | bytes 155680 | tf_op jit(solution)/shard_map/ppermute | solution.py:344
  29.9 9.0 %second_middle.1.out_in = bf16[12,12,4,512]{3,2,1,0:T(4,128)(2,1)} custom-call(bf16[152,512]{1,0:T(8,128)(2,1)S(1)} %get-tuple-element.21.a, bf16[152,512]{1,0:T(8,128)(2,1)S(1)} %get-tuple-element.22.b, bf16[152,512]{1,0:T(8,128)(2,1)S(1)} %get-tuple-element.32.c, bf16[152,512]{1,0:T(8,128)(2,1)S(1)} %get-tuple-element.31.d, f32[2,512]{1,0:T(2,128)} %g1_ref.5, ...), custom_call_target="tpu_custom_call" | custom-call | flops 2500000000 | bytes 8000000 | tf_op jit(solution)/shard_map/second_middle/pallas_call | solution.py:387
  38.9 0.0 collective-permute-done.4
  38.9 0.6 %collective-permute-done.5 = bf16[312,512]{1,0:T(8,128)(2,1)S(1)} collective-permute-done((bf16[312,512]{1,0:T(8,128)(2,1)S(1)}, bf16[312,512]{1,0:T(8,128)(2,1)S(1)}, u32[]{:S(2)}, u32[]{:S(2)}) %collective-permute-start.5) | collective-permute-done | bytes 319520 | tf_op jit(solution)/shard_map/ppermute | solution.py:344
  39.5 11.0 %second_edge.1 = bf16[12,12,4,512]{3,2,1,0:T(4,128)(2,1)} custom-call(bf16[12,12,4,512]{3,2,1,0:T(4,128)(2,1)} %second_middle.1.out_in, bf16[152,512]{1,0:T(8,128)(2,1)S(1)} %get-tuple-element.19.a, bf16[152,512]{1,0:T(8,128)(2,1)S(1)} %get-tuple-element.20.b, bf16[152,512]{1,0:T(8,128)(2,1)S(1)} %get-tuple-element.30.c, ...), custom_call_target="tpu_custom_call", output_to_operand_aliasing={{}: (0, {})} | custom-call | flops 2500000000 | bytes 8000000 | tf_op jit(solution)/shard_map/second_edge/pallas_call | solution.py:387
  (13 shorter events, 0.3 us)
Async XLA Ops:
  9.7 7.6 %collective-permute-start = (bf16[152,512]{1,0:T(8,128)(2,1)S(1)}, bf16[152,512]{1,0:T(8,128)(2,1)S(1)}, u32[]{:S(2)}, u32[]{:S(2)}) collective-permute-start(bf16[152,512]{1,0:T(8,128)(2,1)S(1)} %get-tuple-element.36), channel_id=1, source_target_pairs={{0,32},{32,0},{64,96},{96,64},{1,33},{33,1},{65,97},{97,65},{2,34}... | collective-permute-start | bytes 466952 | tf_op jit(solution)/shard_map/ppermute | solution.py:343
  9.8 7.6 %collective-permute-start.1 = (bf16[152,512]{1,0:T(8,128)(2,1)S(1)}, bf16[152,512]{1,0:T(8,128)(2,1)S(1)}, u32[]{:S(2)}, u32[]{:S(2)}) collective-permute-start(bf16[152,512]{1,0:T(8,128)(2,1)S(1)} %get-tuple-element.35), channel_id=1, source_target_pairs={{0,96},{32,64},{64,32},{96,0},{1,97},{33,65},{65,33},{97,1},{2,98}... | collective-permute-start | bytes 466952 | tf_op jit(solution)/shard_map/ppermute | solution.py:344
  17.4 9.6 %collective-permute-start.2 = (bf16[152,512]{1,0:T(8,128)(2,1)S(1)}, bf16[152,512]{1,0:T(8,128)(2,1)S(1)}, u32[]{:S(2)}, u32[]{:S(2)}) collective-permute-start(bf16[152,512]{1,0:T(8,128)(2,1)S(1)} %get-tuple-element.34), channel_id=1, source_target_pairs={{0,1},{1,0},{2,3},{3,2},{4,5},{5,4},{6,7},{7,6},{8,9},{9,8},{10,11... | collective-permute-start | bytes 466952 | tf_op jit(solution)/shard_map/ppermute | solution.py:343
  19.1 10.8 %collective-permute-start.3 = (bf16[152,512]{1,0:T(8,128)(2,1)S(1)}, bf16[152,512]{1,0:T(8,128)(2,1)S(1)}, u32[]{:S(2)}, u32[]{:S(2)}) collective-permute-start(bf16[152,512]{1,0:T(8,128)(2,1)S(1)} %get-tuple-element.33), channel_id=1, source_target_pairs={{0,31},{1,2},{2,1},{3,4},{4,3},{5,6},{6,5},{7,8},{8,7},{9,10},{10,... | collective-permute-start | bytes 466952 | tf_op jit(solution)/shard_map/ppermute | solution.py:344
  25.7 13.2 %collective-permute-start.4 = (bf16[312,512]{1,0:T(8,128)(2,1)S(1)}, bf16[312,512]{1,0:T(8,128)(2,1)S(1)}, u32[]{:S(2)}, u32[]{:S(2)}) collective-permute-start(bf16[312,512]{1,0:T(8,128)(2,1)S(1)} %get-tuple-element.28), channel_id=1, source_target_pairs={{0,1},{1,0},{2,3},{3,2},{4,5},{5,4},{6,7},{7,6},{8,9},{9,8},{10,11... | collective-permute-start | bytes 958472 | tf_op jit(solution)/shard_map/ppermute | solution.py:343
  25.8 13.7 %collective-permute-start.5 = (bf16[312,512]{1,0:T(8,128)(2,1)S(1)}, bf16[312,512]{1,0:T(8,128)(2,1)S(1)}, u32[]{:S(2)}, u32[]{:S(2)}) collective-permute-start(bf16[312,512]{1,0:T(8,128)(2,1)S(1)} %get-tuple-element.27), channel_id=1, source_target_pairs={{0,31},{1,2},{2,1},{3,4},{4,3},{5,6},{6,5},{7,8},{8,7},{9,10},{10,... | collective-permute-start | bytes 958472 | tf_op jit(solution)/shard_map/ppermute | solution.py:344

commit v4 on v3

--- a/solution.py
+++ b/solution.py
@@ -20,7 +20,7 @@
 EPS = 1e-05
 BIG = 1e30
 EXP_SCALE = math.log2(math.e) / math.sqrt(HD)
-VMEM_LIMIT = 40 * 1024 * 1024
+VMEM_LIMIT = 24 * 1024 * 1024
 FCHUNK = 512
 STAGE = 8
 
@@ -96,6 +96,10 @@
     return jnp.concatenate(tiles, axis=1)
 
 
+def is_odd(axis):
+    return lax.rem(lax.axis_index(axis), 2) == 1
+
+
 def token_labels(region_ref, half, pick_ref, lane_ref, adds_ref, lab_s, first_row):
     lab_s[...] = jnp.zeros_like(lab_s)
     for row in range(6):
@@ -152,16 +156,22 @@
 
 
 def first_kernel(
-    x_hbm, region_ref, pick_ref, lane_ref, adds_ref, g1_ref, g2_ref, wq_hbm, wp_hbm, wu_hbm, wd_hbm,
-    up_ref, down_ref, tile_ref, mid_hbm,
-    xv, xs, lab_s, labs, wq, wp, wu, wd, sem, mid_sem,
+    x_hbm, region_hbm, pick_hbm, lane_hbm, adds_hbm, g1_hbm, g2_hbm, wq_hbm, wp_hbm, wu_hbm, wd_hbm,
+    one_ref, two_ref, tile_ref, mid_ref, wu, g1_ref, g2_ref,
+    xv, xs, lab_s, labs, region_ref, pick_ref, lane_ref, adds_ref, wq, wp, wd, sem, mlp_sem, small_sem,
 ):
+    small = Inputs(
+        [
+            (region_hbm, region_ref), (pick_hbm, pick_ref), (lane_hbm, lane_ref), (adds_hbm, adds_ref),
+            (g1_hbm, g1_ref), (g2_hbm, g2_ref),
+        ],
+        small_sem,
+    )
     inputs = Inputs(
-        [(x_hbm.at[0:6], xv.at[0:6]), (wq_hbm.at[0], wq), (x_hbm.at[6:12], xv.at[6:12]), (wp_hbm.at[0], wp)]
-        + mlp_chunks(wu_hbm, wd_hbm, 0, wu, wd),
-        sem,
+        [(x_hbm.at[0:6], xv.at[0:6]), (wq_hbm.at[0], wq), (x_hbm.at[6:12], xv.at[6:12]), (wp_hbm.at[0], wp)], sem
     )
     first_row = (lax.axis_index("lat") == 0).astype(F32)
+    small.wait(*range(6))
     g1, g2 = g1_ref[0:1, :], g2_ref[0:1, :]
     tiles = []
     for half in range(2):
@@ -173,6 +183,7 @@
         a = layer_norm(xs[rows], g1).astype(BF)
         if half == 0:
             inputs.wait(1)
+            mlp_inputs = Inputs(mlp_chunks(wu_hbm, wd_hbm, 0, wu, wd), mlp_sem)
         qkv = jnp.dot(a, wq[...], preferred_element_type=F32).astype(BF)
         o = attend(
             qkv[:, :D], qkv[:, D : 2 * D], qkv[:, 2 * D :], query_features(lab1, HALF), key_features(lab1, HALF)
@@ -185,29 +196,65 @@
                 start = (i * 2 + side) * GROUP
                 labs[start : start + GROUP, :] = jnp.broadcast_to(grouped(lab2, i, side), (GROUP, 128))
         tiles.append(jnp.transpose(labs[...], (1, 0))[0:8])
-    mid = pltpu.make_async_copy(xs.at[PER_RT : 3 * PER_RT], mid_hbm, mid_sem)
-    mid.start()
+    mid_ref[...] = xs[PER_RT : 3 * PER_RT]
     row = lax.broadcasted_iota(jnp.int32, (8, 384), 0)
     tile = jnp.where(row == 0, tiles[0], tiles[1])
     tile = jnp.concatenate([tile, jnp.zeros((8, 128), F32)], axis=1).astype(BF)
     tile_ref[...] = tile
     h = jnp.concatenate([xs[0:PER_RT], xs[3 * PER_RT :]], axis=0)
-    y = mlp(h, g2, wu, wd, lambda *which: inputs.wait(*[4 + w for w in which]))
-    for i, ref in enumerate((up_ref, down_ref)):
-        for side in range(2):
-            ref[side * GROUP : (side + 1) * GROUP, :] = grouped(y, i, side).astype(BF)
-        ref[PER_RT:, :] = tile
-    mid.wait()
-
-
-def middle_mlp_kernel(mid_hbm, tile_ref, g2_ref, wu_hbm, wd_hbm, left_ref, right_ref, mid, wu, wd, sem):
-    inputs = Inputs([(mid_hbm, mid)] + mlp_chunks(wu_hbm, wd_hbm, 0, wu, wd), sem)
-    inputs.wait(0)
-    y = mlp(mid[...], g2_ref[0:1, :], wu, wd, lambda *which: inputs.wait(*[1 + w for w in which]))
-    for side, ref in enumerate((left_ref, right_ref)):
-        for i in range(2):
-            ref[i * GROUP : (i + 1) * GROUP, :] = grouped(y, i, side).astype(BF)
-        ref[PER_RT:, :] = tile_ref[...]
+    y = mlp(h, g2, wu, wd, mlp_inputs.wait)
+    odd = is_odd("lat")
+    for side in range(2):
+        rows = slice(side * GROUP, (side + 1) * GROUP)
+        up, down = grouped(y, 0, side), grouped(y, 1, side)
+        one_ref[rows, :] = jnp.where(odd, up, down).astype(BF)
+        two_ref[rows, :] = jnp.where(odd, down, up).astype(BF)
+    one_ref[PER_RT:, :] = tile
+    two_ref[PER_RT:, :] = tile
+
+
+def middle_mlp_kernel(mid, tile_ref, g2_ref, wu, wd_hbm, wq_hbm, one_ref, two_ref, wq1, wd, sem):
+    chunks = [slice(c, c + FCHUNK) for c in range(0, FF, FCHUNK)]
+    inputs = Inputs([(wd_hbm.at[0, c], wd.at[c]) for c in chunks] + [(wq_hbm.at[1], wq1)], sem)
+    y = mlp(mid[...], g2_ref[0:1, :], wu, wd, lambda up, down: inputs.wait(down // 2))
+    odd = is_odd("lon")
+    for i in range(2):
+        rows = slice(i * GROUP, (i + 1) * GROUP)
+        left, right = grouped(y, i, 0), grouped(y, i, 1)
+        one_ref[rows, :] = jnp.where(odd, left, right).astype(BF)
+        two_ref[rows, :] = jnp.where(odd, right, left).astype(BF)
+    one_ref[PER_RT:, :] = tile_ref[...]
+    two_ref[PER_RT:, :] = tile_ref[...]
+    inputs.wait(N_CHUNK // 2)
+
+
+class Either:
+    def __init__(self, odd, first, second):
+        self.odd, self.first, self.second = odd, first, second
+
+    def __getitem__(self, at):
+        return jnp.where(self.odd, self.first[at].astype(F32), self.second[at].astype(F32))
+
+
+def both_ways(axis, one, two):
+    odd = is_odd(axis)
+    return Either(odd, one, two), Either(odd, two, one)
+
+
+def pack_kernel(own_one, own_two, one, two, first_ref, second_ref):
+    up, down = both_ways("lat", own_one, own_two)
+    above, below = both_ways("lat", one, two)
+    odd = is_odd("lon")
+    for i, v in enumerate((up, down, above, below)):
+        left, right = (v[side * GROUP : (side + 1) * GROUP, :] for side in range(2))
+        rows = slice(i * GROUP, (i + 1) * GROUP)
+        first_ref[rows, :] = jnp.where(odd, left, right).astype(BF)
+        second_ref[rows, :] = jnp.where(odd, right, left).astype(BF)
+    for i, v in enumerate((up, above, below)):
+        rows = slice(4 * GROUP + 8 * i, 4 * GROUP + 8 * i + 8)
+        tile = v[PER_RT:, :].astype(BF)
+        first_ref[rows, :] = tile
+        second_ref[rows, :] = tile
 
 
 def columns_of(tile):
@@ -215,28 +262,17 @@
     return [t[(g % 4) * GROUP : (g % 4 + 1) * GROUP, g // 4 : g // 4 + 1] for g in range(8)]
 
 
-def second_body(arrays, windows_of, g1_ref, g2_ref, hbm, out_hbm, scratch, rts):
-    wq, wp, wu, wd, sem, o_s, x_s, y_s, out_sem, *buffers = scratch
-    wq_hbm, wp_hbm, wu_hbm, wd_hbm = hbm
-    inputs = Inputs(
-        list(zip(arrays, buffers))
-        + [(wq_hbm.at[1, :, D:], wq.at[:, D:]), (wq_hbm.at[1, :, :D], wq.at[:, :D]), (wp_hbm.at[1], wp)]
-        + mlp_chunks(wu_hbm, wd_hbm, 1, wu, wd),
-        sem,
-    )
-    at_weights = len(arrays)
+def second_body(arrays, windows_of, g1_ref, g2_ref, hbm, weights, out_hbm, scratch, rts):
+    o_s, x_s, y_s, out_sem, *sem = scratch
+    wq, wp, wu, wd = weights
+    arrived = (lambda *which: None) if hbm is None else Inputs(second_copies(hbm, weights), sem[0]).wait
     g1, g2 = g1_ref[1:2, :], g2_ref[1:2, :]
-    inputs.wait(*range(at_weights))
-    for index, (own, halo) in enumerate(windows_of(*buffers)):
+    for own, halo in windows_of(*arrays):
         n_own = len(own) * GROUP
         x = jnp.concatenate([s[0].astype(F32) for s in own + halo], axis=0)
         lab = jnp.concatenate([s[1] for s in own + halo], axis=0)
         a = layer_norm(x, g1).astype(BF)
-        if index == 0:
-            inputs.wait(at_weights)
         kv = jnp.dot(a, wq[:, D:], preferred_element_type=F32).astype(BF)
-        if index == 0:
-            inputs.wait(at_weights + 1)
         q = jnp.dot(a[:n_own], wq[:, :D], preferred_element_type=F32).astype(BF)
         o = attend(q, kv[:, :D], kv[:, D:], query_features(lab[:n_own], n_own), key_features(lab, 4 * GROUP))
         for i, s in enumerate(own):
@@ -245,9 +281,9 @@
                 rows = piece(at * 3 + r, side)
                 o_s[rows, :] = o[i * GROUP + r * PIECE : i * GROUP + (r + 1) * PIECE]
                 x_s[rows, :] = x[i * GROUP + r * PIECE : i * GROUP + (r + 1) * PIECE]
-    inputs.wait(at_weights + 2)
+    arrived(0)
     h = x_s[...] + jnp.dot(o_s[...].astype(BF), wp[...], preferred_element_type=F32)
-    o_s[...] = mlp(h, g2, wu, wd, lambda *which: inputs.wait(*[at_weights + 3 + w for w in which]))
+    o_s[...] = mlp(h, g2, wu, wd, lambda *which: arrived(*[1 + w for w in which]))
     copies = []
     for i, rt in enumerate(rts):
         for n in range(36):
@@ -264,7 +300,9 @@
     return ref[i * GROUP : (i + 1) * GROUP, :]
 
 
-def middle_windows(left, right, left_halo, right_halo):
+def middle_windows(own_one, own_two, one, two):
+    left, right = both_ways("lon", own_one, own_two)
+    left_halo, right_halo = both_ways("lon", one, two)
     mine = columns_of(left[PER_RT:, :])
     windows = []
     for side, (own_ref, halo_ref) in enumerate(((left, left_halo), (right, right_halo))):
@@ -275,7 +313,10 @@
     return windows
 
 
-def edge_windows(up, down, above, below, left_halo, right_halo):
+def edge_windows(own_one, own_two, v_one, v_two, h_one, h_two):
+    up, down = both_ways("lat", own_one, own_two)
+    above, below = both_ways("lat", v_one, v_two)
+    left_halo, right_halo = both_ways("lon", h_one, h_two)
     mine = columns_of(up[PER_RT:, :])
     beside = []
     for ref in (left_halo, right_halo):
@@ -295,32 +336,35 @@
     return windows
 
 
-def middle_kernel(a, b, c, d, g1_ref, g2_ref, wq_hbm, wp_hbm, wu_hbm, wd_hbm, out_hbm, *scratch):
-    hbm = (wq_hbm, wp_hbm, wu_hbm, wd_hbm)
-    second_body((a, b, c, d), middle_windows, g1_ref, g2_ref, hbm, out_hbm, scratch, (1, 2))
-
-
-def edge_kernel(out_in, a, b, c, d, e, f, g1_ref, g2_ref, wq_hbm, wp_hbm, wu_hbm, wd_hbm, out_hbm, *scratch):
-    hbm = (wq_hbm, wp_hbm, wu_hbm, wd_hbm)
-    second_body((a, b, c, d, e, f), edge_windows, g1_ref, g2_ref, hbm, out_hbm, scratch, (0, 3))
-
-
-MLP_SCRATCH = [pltpu.VMEM((D, FF), BF), pltpu.VMEM((FF, D), BF)]
-WEIGHT_SCRATCH = [pltpu.VMEM((D, 3 * D), BF), pltpu.VMEM((D, D), BF)] + MLP_SCRATCH
+def second_copies(hbm, weights):
+    wp_hbm, wu_hbm, wd_hbm = hbm
+    wp, wu, wd = weights[1:]
+    return [(wp_hbm.at[1], wp)] + mlp_chunks(wu_hbm, wd_hbm, 1, wu, wd)
+
+
+def middle_kernel(a, b, c, d, g1_ref, g2_ref, wq, wp_hbm, wu_hbm, wd_hbm, out_hbm, wp, wu, wd, *scratch):
+    hbm = (wp_hbm, wu_hbm, wd_hbm)
+    second_body((a, b, c, d), middle_windows, g1_ref, g2_ref, hbm, (wq, wp, wu, wd), out_hbm, scratch, (1, 2))
+
+
+def edge_kernel(out_in, a, b, c, d, e, f, g1_ref, g2_ref, wq, wp, wu, wd, out_hbm, *scratch):
+    weights = (wq, wp, wu, wd)
+    second_body((a, b, c, d, e, f), edge_windows, g1_ref, g2_ref, None, weights, out_hbm, scratch, (0, 3))
+
+
+WEIGHT_SCRATCH = [pltpu.VMEM((D, 3 * D), BF), pltpu.VMEM((D, D), BF)]
 
 
 def dma(n):
     return pltpu.SemaphoreType.DMA((n,))
 
 
-def second_scratch(arrays):
-    return (
-        WEIGHT_SCRATCH
-        + [dma(len(arrays) + 3 + N_CHUNK), pltpu.VMEM((HALF, D), F32), pltpu.VMEM((HALF, D), F32)]
-        + [pltpu.VMEM((6, COLS, LEV, D), BF), dma(2)]
-        + [pltpu.VMEM(a.shape, BF) for a in arrays]
-    )
-
+SECOND_SCRATCH = [
+    pltpu.VMEM((HALF, D), F32),
+    pltpu.VMEM((HALF, D), F32),
+    pltpu.VMEM((6, COLS, LEV, D), BF),
+    dma(2),
+]
 
 VM = pl.BlockSpec(memory_space=pltpu.VMEM)
 ANY = pl.BlockSpec(memory_space=pl.ANY)
@@ -335,18 +379,11 @@
     return pltpu.with_memory_space_constraint(value, pltpu.HBM)
 
 
-def exchange(to_before, to_after, axis):
+def exchange(one, two, axis):
     count = lax.axis_size(axis)
-    odd = lax.axis_index(axis) % 2 == 1
     even_pairs = [(s, s + 1 - 2 * (s % 2)) for s in range(count)]
     odd_pairs = [(s, (s - 1 + 2 * (s % 2)) % count) for s in range(count)]
-    one = lax.ppermute(jnp.where(odd, to_before, to_after), axis, even_pairs)
-    two = lax.ppermute(jnp.where(odd, to_after, to_before), axis, odd_pairs)
-    return one, two, odd
-
-
-def sorted_out(one, two, odd):
-    return jnp.where(odd, one, two), jnp.where(odd, two, one)
+    return lax.ppermute(one, axis, even_pairs), lax.ppermute(two, axis, odd_pairs)
 
 
 def first_calls(tokens, region, g1, g2, weights):
@@ -354,69 +391,85 @@
     tables = [in_hbm(jnp.asarray(t, d)) for t, d in ((pick, BF), (lane, BF), (adds, F32))]
     params = pltpu.CompilerParams(vmem_limit_bytes=VMEM_LIMIT)
     edge_out = jax.ShapeDtypeStruct((PER_RT + 8, D), BF)
-    up, down, tile, mid = pl.pallas_call(
+    up, down, tile, mid, wu, g1, g2 = pl.pallas_call(
         first_kernel,
         out_shape=(
-            edge_out, edge_out, jax.ShapeDtypeStruct((8, D), BF), jax.ShapeDtypeStruct((HALF, D), F32),
+            edge_out, edge_out, pltpu.VMEM((8, D), BF), pltpu.VMEM((HALF, D), F32),
+            pltpu.VMEM((D, FF), BF), pltpu.VMEM((2, D), F32), pltpu.VMEM((2, D), F32),
         ),
-        in_specs=[HBM] + [VM] * 6 + [HBM] * 4,
-        out_specs=[VM] * 3 + [ANY],
+        in_specs=[HBM] * 11,
+        out_specs=[VM] * 7,
         scratch_shapes=[
             pltpu.VMEM((ROWS, COLS, LEV, D), BF), pltpu.VMEM((TOKENS, D), F32), pltpu.VMEM((128, 128), F32),
-            pltpu.VMEM((384, 128), F32),
-        ] + WEIGHT_SCRATCH + [dma(4 + N_CHUNK), pltpu.SemaphoreType.DMA],
+            pltpu.VMEM((384, 128), F32), pltpu.VMEM((ROWS, LEV, COLS), jnp.int32), pltpu.VMEM((HALF, 128), BF),
+            pltpu.VMEM((HALF, 128), BF), pltpu.VMEM((HALF, 128), F32),
+        ] + WEIGHT_SCRATCH + [pltpu.VMEM((FF, D), BF), dma(4), dma(N_CHUNK), dma(6)],
         compiler_params=params,
         cost_estimate=cost(4e9, 8e6),
         name="first_block",
     )(tokens, region, *tables, g1, g2, *weights)
-    left, right = pl.pallas_call(
+    left, right, early = pl.pallas_call(
         middle_mlp_kernel,
-        out_shape=(edge_out, edge_out),
-        in_specs=[ANY, VM, VM, HBM, HBM],
-        out_specs=[VM] * 2,
-        scratch_shapes=[pltpu.VMEM((HALF, D), F32)] + MLP_SCRATCH + [dma(1 + N_CHUNK)],
+        out_shape=(edge_out, edge_out, pltpu.VMEM((D, 3 * D), BF)),
+        in_specs=[VM] * 4 + [HBM] * 2,
+        out_specs=[VM] * 3,
+        scratch_shapes=[pltpu.VMEM((FF, D), BF), dma(N_CHUNK // 2 + 1)],
         compiler_params=params,
         cost_estimate=cost(1.3e9, 5e6),
         name="first_middle",
-    )(mid, tile, g2, weights[2], weights[3])
-    return up, down, left, right
-
-
-def second_call(kernel, arrays, g1, g2, weights, out=None, name=None):
-    given = () if out is None else (out,)
+    )(mid, tile, g2, wu, weights[3], weights[0])
+    return up, down, left, right, g1, g2, early
+
+
+def second_calls(middle, edge, g1, g2, early, weights):
+    params = pltpu.CompilerParams(vmem_limit_bytes=VMEM_LIMIT)
+    out_shape = jax.ShapeDtypeStruct((ROWS, COLS, LEV, D), BF)
+    out, *late = pl.pallas_call(
+        middle_kernel,
+        out_shape=(
+            out_shape, pltpu.VMEM((D, D), BF), pltpu.VMEM((D, FF), BF), pltpu.VMEM((FF, D), BF),
+        ),
+        in_specs=[VM] * 7 + [HBM] * 3,
+        out_specs=[HBM] + [VM] * 3,
+        scratch_shapes=SECOND_SCRATCH + [dma(1 + N_CHUNK)],
+        compiler_params=params,
+        cost_estimate=cost(2.5e9, 8e6),
+        name="second_middle",
+    )(*middle, g1, g2, early, *weights[1:])
     return pl.pallas_call(
-        kernel,
-        out_shape=jax.ShapeDtypeStruct((ROWS, COLS, LEV, D), BF),
-        in_specs=[HBM] * len(given) + [ANY] * len(arrays) + [VM] * 2 + [HBM] * 4,
+        edge_kernel,
+        out_shape=out_shape,
+        in_specs=[HBM] + [VM] * 12,
         out_specs=HBM,
-        scratch_shapes=second_scratch(arrays),
-        input_output_aliases={0: 0} if given else {},
-        compiler_params=pltpu.CompilerParams(vmem_limit_bytes=VMEM_LIMIT),
+        scratch_shapes=SECOND_SCRATCH,
+        input_output_aliases={0: 0},
+        compiler_params=params,
         cost_estimate=cost(2.5e9, 8e6),
-        name=name,
-    )(*given, *arrays, g1, g2, *weights)
+        name="second_edge",
+    )(out, *edge, g1, g2, early, *late)
 
 
 def per_device(tokens, region, norm_gain1, qkv_weight, proj_weight, norm_gain2, up_weight, down_weight):
     weights = [in_hbm(w) for w in (qkv_weight, proj_weight, up_weight, down_weight)]
     g1, g2 = in_hbm(norm_gain1), in_hbm(norm_gain2)
-    up, down, left, right = first_calls(
+    up, down, left, right, g1, g2, early = first_calls(
         in_hbm(jnp.transpose(tokens, (1, 2, 0, 3))), in_hbm(jnp.transpose(region, (1, 0, 2))), g1, g2, weights
     )
-    one, two, odd = exchange(up, down, "lat")
-    left, right, one, two = lax.optimization_barrier((left, right, one, two))
-    above, below = sorted_out(one, two, odd)
-    left_halo, right_halo = sorted_out(*exchange(left, right, "lon"))
-
-    def edge_of(side):
-        rows = slice(side * GROUP, (side + 1) * GROUP)
-        tiles = [v[PER_RT:] for v in (up, above, below)]
-        return jnp.concatenate([up[rows], down[rows], above[rows], below[rows]] + tiles, axis=0)
-
-    left_edge, right_edge = sorted_out(*exchange(edge_of(0), edge_of(1), "lon"))
-    out = second_call(middle_kernel, (left, right, left_halo, right_halo), g1, g2, weights, name="second_middle")
-    arrays = (up, down, above, below, left_edge, right_edge)
-    out = second_call(edge_kernel, arrays, g1, g2, weights, out, name="second_edge")
+    received = exchange(up, down, "lat")
+    left, right, above, below = lax.optimization_barrier((left, right, *received))
+    halo = exchange(left, right, "lon")
+    message = jax.ShapeDtypeStruct((4 * GROUP + 24, D), BF)
+    packed = pl.pallas_call(
+        pack_kernel,
+        out_shape=(message, message),
+        in_specs=[VM] * 4,
+        out_specs=[VM] * 2,
+        compiler_params=pltpu.CompilerParams(vmem_limit_bytes=8 * 1024 * 1024),
+        cost_estimate=cost(1e6, 1e6),
+        name="pack_edges",
+    )(up, down, above, below)
+    beside = exchange(*packed, "lon")
+    out = second_calls((left, right, *halo), (up, down, above, below, *beside), g1, g2, early, weights)
     return jnp.transpose(out, (2, 0, 1, 3))
 
 

time: 51 us -> 46.9 us (0.920)
  Pallas kernels: 33.9 us -> 27.3 us
  waiting for transfers between devices: 3.44 us -> 6.4 us
    pallas_call x4 -> x5, Pallas kernels: 33.9 us -> 27.3 us  [the longest x1 9.13 us: first_calls(): pl.pallas_call(first_kernel, out_shape=(edge_out, edge_out, pltpu.VMEM((8...]
    ppermute x6, waiting for transfers between devices: 3.44 us -> 6.4 us  [the longest x3 6.39 us: exchange(): lax.ppermute(two, axis, odd_pairs)]
  transfers between devices with their start and end apart: 6 -> 6, of which waited for: 2 -> 3; matrix products, arithmetic and copies ran while one was open for 0% -> 0% of each run, Pallas kernels for 26% -> 22%
where the time goes in v4:
time: 46.9 us; the launch traced here: 46.8 us
  Pallas kernels  27.3 us (58%)
  starting transfers between devices  12.9 us (28%)
  waiting for transfers between devices  6.4 us (14%)
    ppermute x3, starting transfers between devices, exchange(): lax.ppermute(two, axis, odd_pairs)  11.1 us
    pallas_call x1, Pallas kernels, first_calls(): pl.pallas_call(first_kernel, out_shape=(edge_out, edge_out, pltpu.VMEM((8...  9.13 us
    pallas_call x1, Pallas kernels, second_calls(): pl.pallas_call(edge_kernel, out_shape=out_shape, in_specs=[HBM] + [VM] *...  7.77 us
    pallas_call x1, Pallas kernels, second_calls(): pl.pallas_call(middle_kernel, out_shape=(out_shape, pltpu.VMEM((D, D), BF...  6.85 us
    ppermute x3, waiting for transfers between devices, exchange(): lax.ppermute(two, axis, odd_pairs)  6.39 us
    pallas_call x1, Pallas kernels, first_calls(): pl.pallas_call(middle_mlp_kernel, out_shape=(edge_out, edge_out, pltpu.VM...  3.3 us
    ppermute x3, starting transfers between devices, exchange(): lax.ppermute(one, axis, even_pairs)  1.85 us
  transfers between devices with their start and end apart: 6, of which 3 were waited for; matrix products, arithmetic and copies ran while one was open for 0% of the time, Pallas kernels for 22%

profile of v4, /device:TPU:0, one launch (start us, length us, event | category | flops | bytes accessed | tf_op | source)
XLA Modules:
  0.0 46.8 jit_solution(1573647610828516842)
XLA Ops:
  0.0 9.1 %first_block.1 = (bf16[152,512]{1,0:T(8,128)(2,1)S(1)}, bf16[152,512]{1,0:T(8,128)(2,1)S(1)}, bf16[8,512]{1,0:T(8,128)(2,1)S(1)}, f32[288,512]{1,0:T(8,128)S(1)}...) custom-call(bf16[12,12,4,512]{3,2,1,0:T(4,128)(2,1)} %bitcast.3, ...), custom_call_target="tpu_custom_call" | custom-call | flops 4000000000 | bytes 8000000 | tf_op jit(solution)/shard_map/first_block/pallas_call | solution.py:394
  9.1 0.1 collective-permute-start
  9.2 3.2 %collective-permute-start.1 = (bf16[152,512]{1,0:T(8,128)(2,1)S(1)}, bf16[152,512]{1,0:T(8,128)(2,1)S(1)}, u32[]{:S(2)}, u32[]{:S(2)}) collective-permute-start(bf16[152,512]{1,0:T(8,128)(2,1)S(1)} %get-tuple-element.32.own_two.b), channel_id=1, source_target_pairs={{0,96},{32,64},{64,32},{96,0},{1,97},{33,65},{65,33},{97,1},{2,98}... | collective-permute-start | bytes 466952 | tf_op jit(solution)/shard_map/ppermute | solution.py:386
  12.4 3.3 %first_middle.1 = (bf16[152,512]{1,0:T(8,128)(2,1)S(1)}, bf16[152,512]{1,0:T(8,128)(2,1)S(1)}, bf16[512,1536]{1,0:T(8,128)(2,1)S(1)}) custom-call(f32[288,512]{1,0:T(8,128)S(1)} %get-tuple-element.25.mid, bf16[8,512]{1,0:T(8,128)(2,1)S(1)} %get-tuple-element.26.tile_ref, f32[2,512]{1,0:T(2,128)S(1)} %get-tuple-element.27.g2_ref, ...), custom_call_target="tpu_custom_call" | custom-call | flops 1300000000 | bytes 5000000 | tf_op jit(solution)/shard_map/first_middle/pallas_call | solution.py:411
  15.8 0.0 collective-permute-done.one.c
  15.8 0.8 %collective-permute-done.1.two.d = bf16[152,512]{1,0:T(8,128)(2,1)S(1)} collective-permute-done((bf16[152,512]{1,0:T(8,128)(2,1)S(1)}, bf16[152,512]{1,0:T(8,128)(2,1)S(1)}, u32[]{:S(2)}, u32[]{:S(2)}) %collective-permute-start.1) | collective-permute-done | bytes 155680 | tf_op jit(solution)/shard_map/ppermute | solution.py:386
  16.6 1.7 %collective-permute-start.2 = (bf16[152,512]{1,0:T(8,128)(2,1)S(1)}, bf16[152,512]{1,0:T(8,128)(2,1)S(1)}, u32[]{:S(2)}, u32[]{:S(2)}) collective-permute-start(bf16[152,512]{1,0:T(8,128)(2,1)S(1)} %get-tuple-element.33.a), channel_id=1, source_target_pairs={{0,1},{1,0},{2,3},{3,2},{4,5},{5,4},{6,7},{7,6},{8,9},{9,8},{10,11... | collective-permute-start | bytes 466952 | tf_op jit(solution)/shard_map/ppermute | solution.py:386
  18.3 6.6 %collective-permute-start.3 = (bf16[152,512]{1,0:T(8,128)(2,1)S(1)}, bf16[152,512]{1,0:T(8,128)(2,1)S(1)}, u32[]{:S(2)}, u32[]{:S(2)}) collective-permute-start(bf16[152,512]{1,0:T(8,128)(2,1)S(1)} %get-tuple-element.34.b), channel_id=1, source_target_pairs={{0,31},{1,2},{2,1},{3,4},{4,3},{5,6},{6,5},{7,8},{8,7},{9,10},{10,... | collective-permute-start | bytes 466952 | tf_op jit(solution)/shard_map/ppermute | solution.py:386
  24.8 0.2 pack_edges.1
  25.1 0.1 collective-permute-start.4
  25.2 1.3 %collective-permute-start.5 = (bf16[312,512]{1,0:T(8,128)(2,1)S(1)}, bf16[312,512]{1,0:T(8,128)(2,1)S(1)}, u32[]{:S(2)}, u32[]{:S(2)}) collective-permute-start(bf16[312,512]{1,0:T(8,128)(2,1)S(1)} %get-tuple-element.41), channel_id=1, source_target_pairs={{0,31},{1,2},{2,1},{3,4},{4,3},{5,6},{6,5},{7,8},{8,7},{9,10},{10,... | collective-permute-start | bytes 958472 | tf_op jit(solution)/shard_map/ppermute | solution.py:386
  26.4 0.0 collective-permute-done.2.c
  26.4 2.8 %collective-permute-done.3.d = bf16[152,512]{1,0:T(8,128)(2,1)S(1)} collective-permute-done((bf16[152,512]{1,0:T(8,128)(2,1)S(1)}, bf16[152,512]{1,0:T(8,128)(2,1)S(1)}, u32[]{:S(2)}, u32[]{:S(2)}) %collective-permute-start.3) | collective-permute-done | bytes 155680 | tf_op jit(solution)/shard_map/ppermute | solution.py:386
  29.2 6.8 %second_middle.1 = (bf16[12,12,4,512]{3,2,1,0:T(4,128)(2,1)}, bf16[512,512]{1,0:T(8,128)(2,1)S(1)}, bf16[512,2048]{1,0:T(8,128)(2,1)S(1)}, bf16[2048,512]{1,0:T(8,128)(2,1)S(1)}) custom-call(bf16[152,512]{1,0:T(8,128)(2,1)S(1)} %get-tuple-element.33.a, bf16[152,512]{1,0:T(8,128)(2,1)S(1)} %get-tuple-element.34.b, ...), custom_call_target="tpu_custom_call" | custom-call | flops 2500000000 | bytes 8000000 | tf_op jit(solution)/shard_map/second_middle/pallas_call | solution.py:427
  36.1 0.0 collective-permute-done.4.e
  36.1 2.8 %collective-permute-done.5.f = bf16[312,512]{1,0:T(8,128)(2,1)S(1)} collective-permute-done((bf16[312,512]{1,0:T(8,128)(2,1)S(1)}, bf16[312,512]{1,0:T(8,128)(2,1)S(1)}, u32[]{:S(2)}, u32[]{:S(2)}) %collective-permute-start.5) | collective-permute-done | bytes 319520 | tf_op jit(solution)/shard_map/ppermute | solution.py:386
  38.9 7.8 %second_edge.1 = bf16[12,12,4,512]{3,2,1,0:T(4,128)(2,1)} custom-call(bf16[12,12,4,512]{3,2,1,0:T(4,128)(2,1)} %get-tuple-element.37.out_in, bf16[152,512]{1,0:T(8,128)(2,1)S(1)} %get-tuple-element.31.own_one.a, bf16[152,512]{1,0:T(8,128)(2,1)S(1)} %get-tuple-element.32.own_two.b, ...), custom_call_target="tpu_custom_call", output_to_operand_aliasing={{}: (0, {})} | custom-call | flops 2500000000 | bytes 8000000 | tf_op jit(solution)/shard_map/second_edge/pallas_call | solution.py:439
Async XLA Ops:
  9.1 6.6 %collective-permute-start = (bf16[152,512]{1,0:T(8,128)(2,1)S(1)}, bf16[152,512]{1,0:T(8,128)(2,1)S(1)}, u32[]{:S(2)}, u32[]{:S(2)}) collective-permute-start(bf16[152,512]{1,0:T(8,128)(2,1)S(1)} %get-tuple-element.31.own_one.a), channel_id=1, source_target_pairs={{0,32},{32,0},{64,96},{96,64},{1,33},{33,1},{65,97},{97,65},{2,34}... | collective-permute-start | bytes 466952 | tf_op jit(solution)/shard_map/ppermute | solution.py:386
  9.2 7.3 %collective-permute-start.1 = (bf16[152,512]{1,0:T(8,128)(2,1)S(1)}, bf16[152,512]{1,0:T(8,128)(2,1)S(1)}, u32[]{:S(2)}, u32[]{:S(2)}) collective-permute-start(bf16[152,512]{1,0:T(8,128)(2,1)S(1)} %get-tuple-element.32.own_two.b), channel_id=1, source_target_pairs={{0,96},{32,64},{64,32},{96,0},{1,97},{33,65},{65,33},{97,1},{2,98}... | collective-permute-start | bytes 466952 | tf_op jit(solution)/shard_map/ppermute | solution.py:386
  16.6 9.9 %collective-permute-start.2 = (bf16[152,512]{1,0:T(8,128)(2,1)S(1)}, bf16[152,512]{1,0:T(8,128)(2,1)S(1)}, u32[]{:S(2)}, u32[]{:S(2)}) collective-permute-start(bf16[152,512]{1,0:T(8,128)(2,1)S(1)} %get-tuple-element.33.a), channel_id=1, source_target_pairs={{0,1},{1,0},{2,3},{3,2},{4,5},{5,4},{6,7},{7,6},{8,9},{9,8},{10,11... | collective-permute-start | bytes 466952 | tf_op jit(solution)/shard_map/ppermute | solution.py:386
  18.3 11.0 %collective-permute-start.3 = (bf16[152,512]{1,0:T(8,128)(2,1)S(1)}, bf16[152,512]{1,0:T(8,128)(2,1)S(1)}, u32[]{:S(2)}, u32[]{:S(2)}) collective-permute-start(bf16[152,512]{1,0:T(8,128)(2,1)S(1)} %get-tuple-element.34.b), channel_id=1, source_target_pairs={{0,31},{1,2},{2,1},{3,4},{4,3},{5,6},{6,5},{7,8},{8,7},{9,10},{10,... | collective-permute-start | bytes 466952 | tf_op jit(solution)/shard_map/ppermute | solution.py:386
  25.1 11.0 %collective-permute-start.4 = (bf16[312,512]{1,0:T(8,128)(2,1)S(1)}, bf16[312,512]{1,0:T(8,128)(2,1)S(1)}, u32[]{:S(2)}, u32[]{:S(2)}) collective-permute-start(bf16[312,512]{1,0:T(8,128)(2,1)S(1)} %get-tuple-element.40), channel_id=1, source_target_pairs={{0,1},{1,0},{2,3},{3,2},{4,5},{5,4},{6,7},{7,6},{8,9},{9,8},{10,11... | collective-permute-start | bytes 958472 | tf_op jit(solution)/shard_map/ppermute | solution.py:386
  25.2 13.7 %collective-permute-start.5 = (bf16[312,512]{1,0:T(8,128)(2,1)S(1)}, bf16[312,512]{1,0:T(8,128)(2,1)S(1)}, u32[]{:S(2)}, u32[]{:S(2)}) collective-permute-start(bf16[312,512]{1,0:T(8,128)(2,1)S(1)} %get-tuple-element.41), channel_id=1, source_target_pairs={{0,31},{1,2},{2,1},{3,4},{4,3},{5,6},{6,5},{7,8},{8,7},{9,10},{10,... | collective-permute-start | bytes 958472 | tf_op jit(solution)/shard_map/ppermute | solution.py:386

commit v5 on v4

--- a/solution.py
+++ b/solution.py
@@ -456,7 +456,8 @@
         in_hbm(jnp.transpose(tokens, (1, 2, 0, 3))), in_hbm(jnp.transpose(region, (1, 0, 2))), g1, g2, weights
     )
     received = exchange(up, down, "lat")
-    left, right, above, below = lax.optimization_barrier((left, right, *received))
+    above, below = received
+    left, right, above = lax.optimization_barrier((left, right, above))
     halo = exchange(left, right, "lon")
     message = jax.ShapeDtypeStruct((4 * GROUP + 24, D), BF)
     packed = pl.pallas_call(

time: 46.9 us -> 44.9 us (0.957)
  waiting for transfers between devices: 6.4 us -> 4.87 us
  starting transfers between devices: 12.9 us -> 12.4 us
    ppermute x3, waiting for transfers between devices: 6.39 us -> 4.87 us  [exchange(): lax.ppermute(two, axis, odd_pairs)]
  transfers between devices with their start and end apart: 6 -> 6, of which waited for: 3 -> 2; matrix products, arithmetic and copies ran while one was open for 0% -> 0% of each run, Pallas kernels for 22% -> 23%
where the time goes in v5:
time: 44.9 us; the launch traced here: 44.8 us
  Pallas kernels  27.3 us (61%)
  starting transfers between devices  12.4 us (28%)
  waiting for transfers between devices  4.87 us (11%)
    ppermute x3, starting transfers between devices, exchange(): lax.ppermute(two, axis, odd_pairs)  10.6 us
    pallas_call x1, Pallas kernels, first_calls(): pl.pallas_call(first_kernel, out_shape=(edge_out, edge_out, pltpu.VMEM((8...  9.13 us
    pallas_call x1, Pallas kernels, second_calls(): pl.pallas_call(edge_kernel, out_shape=out_shape, in_specs=[HBM] + [VM] *...  7.77 us
    pallas_call x1, Pallas kernels, second_calls(): pl.pallas_call(middle_kernel, out_shape=(out_shape, pltpu.VMEM((D, D), BF...  6.84 us
    ppermute x3, waiting for transfers between devices, exchange(): lax.ppermute(two, axis, odd_pairs)  4.87 us
    pallas_call x1, Pallas kernels, first_calls(): pl.pallas_call(middle_mlp_kernel, out_shape=(edge_out, edge_out, pltpu.VM...  3.3 us
    ppermute x3, starting transfers between devices, exchange(): lax.ppermute(one, axis, even_pairs)  1.81 us
  transfers between devices with their start and end apart: 6, of which 2 were waited for; matrix products, arithmetic and copies ran while one was open for 0% of the time, Pallas kernels for 23%

profile of v5, /device:TPU:0, one launch (start us, length us, event | category | flops | bytes accessed | tf_op | source)
XLA Modules:
  0.0 44.8 jit_solution(17259036921286463848)
XLA Ops:
  0.0 9.1 %first_block.1 = (bf16[152,512]{1,0:T(8,128)(2,1)S(1)}, bf16[152,512]{1,0:T(8,128)(2,1)S(1)}, bf16[8,512]{1,0:T(8,128)(2,1)S(1)}, f32[288,512]{1,0:T(8,128)S(1)}...) custom-call(bf16[12,12,4,512]{3,2,1,0:T(4,128)(2,1)} %bitcast.3, ...), custom_call_target="tpu_custom_call" | custom-call | flops 4000000000 | bytes 8000000 | tf_op jit(solution)/shard_map/first_block/pallas_call | solution.py:394
  9.1 0.1 collective-permute-start
  9.2 3.2 %collective-permute-start.3 = (bf16[152,512]{1,0:T(8,128)(2,1)S(1)}, bf16[152,512]{1,0:T(8,128)(2,1)S(1)}, u32[]{:S(2)}, u32[]{:S(2)}) collective-permute-start(bf16[152,512]{1,0:T(8,128)(2,1)S(1)} %get-tuple-element.36.own_two.b), channel_id=1, source_target_pairs={{0,96},{32,64},{64,32},{96,0},{1,97},{33,65},{65,33},{97,1},{2,98}... | collective-permute-start | bytes 466952 | tf_op jit(solution)/shard_map/ppermute | solution.py:386
  12.4 3.3 %first_middle.1 = (bf16[152,512]{1,0:T(8,128)(2,1)S(1)}, bf16[152,512]{1,0:T(8,128)(2,1)S(1)}, bf16[512,1536]{1,0:T(8,128)(2,1)S(1)}) custom-call(f32[288,512]{1,0:T(8,128)S(1)} %get-tuple-element.24.mid, bf16[8,512]{1,0:T(8,128)(2,1)S(1)} %get-tuple-element.25.tile_ref, f32[2,512]{1,0:T(2,128)S(1)} %get-tuple-element.26.g2_ref, ...), custom_call_target="tpu_custom_call" | custom-call | flops 1300000000 | bytes 5000000 | tf_op jit(solution)/shard_map/first_middle/pallas_call | solution.py:411
  15.8 0.0 collective-permute-done.one.c
  15.8 1.6 %collective-permute-start.1 = (bf16[152,512]{1,0:T(8,128)(2,1)S(1)}, bf16[152,512]{1,0:T(8,128)(2,1)S(1)}, u32[]{:S(2)}, u32[]{:S(2)}) collective-permute-start(bf16[152,512]{1,0:T(8,128)(2,1)S(1)} %get-tuple-element.31.a), channel_id=1, source_target_pairs={{0,1},{1,0},{2,3},{3,2},{4,5},{5,4},{6,7},{7,6},{8,9},{9,8},{10,11... | collective-permute-start | bytes 466952 | tf_op jit(solution)/shard_map/ppermute | solution.py:386
  17.4 5.7 %collective-permute-start.2 = (bf16[152,512]{1,0:T(8,128)(2,1)S(1)}, bf16[152,512]{1,0:T(8,128)(2,1)S(1)}, u32[]{:S(2)}, u32[]{:S(2)}) collective-permute-start(bf16[152,512]{1,0:T(8,128)(2,1)S(1)} %get-tuple-element.32.b), channel_id=1, source_target_pairs={{0,31},{1,2},{2,1},{3,4},{4,3},{5,6},{6,5},{7,8},{8,7},{9,10},{10,... | collective-permute-start | bytes 466952 | tf_op jit(solution)/shard_map/ppermute | solution.py:386
  23.1 0.0 collective-permute-done.3.two.d
  23.1 0.2 pack_edges.1
  23.3 0.1 collective-permute-start.4
  23.4 1.7 %collective-permute-start.5 = (bf16[312,512]{1,0:T(8,128)(2,1)S(1)}, bf16[312,512]{1,0:T(8,128)(2,1)S(1)}, u32[]{:S(2)}, u32[]{:S(2)}) collective-permute-start(bf16[312,512]{1,0:T(8,128)(2,1)S(1)} %get-tuple-element.39), channel_id=1, source_target_pairs={{0,31},{1,2},{2,1},{3,4},{4,3},{5,6},{6,5},{7,8},{8,7},{9,10},{10,... | collective-permute-start | bytes 958472 | tf_op jit(solution)/shard_map/ppermute | solution.py:386
  25.1 0.0 collective-permute-done.1.c
  25.1 2.2 %collective-permute-done.2.d = bf16[152,512]{1,0:T(8,128)(2,1)S(1)} collective-permute-done((bf16[152,512]{1,0:T(8,128)(2,1)S(1)}, bf16[152,512]{1,0:T(8,128)(2,1)S(1)}, u32[]{:S(2)}, u32[]{:S(2)}) %collective-permute-start.2) | collective-permute-done | bytes 155680 | tf_op jit(solution)/shard_map/ppermute | solution.py:386
  27.4 6.8 %second_middle.1 = (bf16[12,12,4,512]{3,2,1,0:T(4,128)(2,1)}, bf16[512,512]{1,0:T(8,128)(2,1)S(1)}, bf16[512,2048]{1,0:T(8,128)(2,1)S(1)}, bf16[2048,512]{1,0:T(8,128)(2,1)S(1)}) custom-call(bf16[152,512]{1,0:T(8,128)(2,1)S(1)} %get-tuple-element.31.a, bf16[152,512]{1,0:T(8,128)(2,1)S(1)} %get-tuple-element.32.b, ...), custom_call_target="tpu_custom_call" | custom-call | flops 2500000000 | bytes 8000000 | tf_op jit(solution)/shard_map/second_middle/pallas_call | solution.py:427
  34.2 0.0 collective-permute-done.4.e
  34.2 2.6 %collective-permute-done.5.f = bf16[312,512]{1,0:T(8,128)(2,1)S(1)} collective-permute-done((bf16[312,512]{1,0:T(8,128)(2,1)S(1)}, bf16[312,512]{1,0:T(8,128)(2,1)S(1)}, u32[]{:S(2)}, u32[]{:S(2)}) %collective-permute-start.5) | collective-permute-done | bytes 319520 | tf_op jit(solution)/shard_map/ppermute | solution.py:386
  36.9 7.8 %second_edge.1 = bf16[12,12,4,512]{3,2,1,0:T(4,128)(2,1)} custom-call(bf16[12,12,4,512]{3,2,1,0:T(4,128)(2,1)} %get-tuple-element.35.out_in, bf16[152,512]{1,0:T(8,128)(2,1)S(1)} %get-tuple-element.30.own_one.a, bf16[152,512]{1,0:T(8,128)(2,1)S(1)} %get-tuple-element.36.own_two.b, ...), custom_call_target="tpu_custom_call", output_to_operand_aliasing={{}: (0, {})} | custom-call | flops 2500000000 | bytes 8000000 | tf_op jit(solution)/shard_map/second_edge/pallas_call | solution.py:439
Async XLA Ops:
  9.1 6.6 %collective-permute-start = (bf16[152,512]{1,0:T(8,128)(2,1)S(1)}, bf16[152,512]{1,0:T(8,128)(2,1)S(1)}, u32[]{:S(2)}, u32[]{:S(2)}) collective-permute-start(bf16[152,512]{1,0:T(8,128)(2,1)S(1)} %get-tuple-element.30.own_one.a), channel_id=1, source_target_pairs={{0,32},{32,0},{64,96},{96,64},{1,33},{33,1},{65,97},{97,65},{2,34}... | collective-permute-start | bytes 466952 | tf_op jit(solution)/shard_map/ppermute | solution.py:386
  9.2 13.9 %collective-permute-start.3 = (bf16[152,512]{1,0:T(8,128)(2,1)S(1)}, bf16[152,512]{1,0:T(8,128)(2,1)S(1)}, u32[]{:S(2)}, u32[]{:S(2)}) collective-permute-start(bf16[152,512]{1,0:T(8,128)(2,1)S(1)} %get-tuple-element.36.own_two.b), channel_id=1, source_target_pairs={{0,96},{32,64},{64,32},{96,0},{1,97},{33,65},{65,33},{97,1},{2,98}... | collective-permute-start | bytes 466952 | tf_op jit(solution)/shard_map/ppermute | solution.py:386
  15.8 9.4 %collective-permute-start.1 = (bf16[152,512]{1,0:T(8,128)(2,1)S(1)}, bf16[152,512]{1,0:T(8,128)(2,1)S(1)}, u32[]{:S(2)}, u32[]{:S(2)}) collective-permute-start(bf16[152,512]{1,0:T(8,128)(2,1)S(1)} %get-tuple-element.31.a), channel_id=1, source_target_pairs={{0,1},{1,0},{2,3},{3,2},{4,5},{5,4},{6,7},{7,6},{8,9},{9,8},{10,11... | collective-permute-start | bytes 466952 | tf_op jit(solution)/shard_map/ppermute | solution.py:386
  17.4 10.0 %collective-permute-start.2 = (bf16[152,512]{1,0:T(8,128)(2,1)S(1)}, bf16[152,512]{1,0:T(8,128)(2,1)S(1)}, u32[]{:S(2)}, u32[]{:S(2)}) collective-permute-start(bf16[152,512]{1,0:T(8,128)(2,1)S(1)} %get-tuple-element.32.b), channel_id=1, source_target_pairs={{0,31},{1,2},{2,1},{3,4},{4,3},{5,6},{6,5},{7,8},{8,7},{9,10},{10,... | collective-permute-start | bytes 466952 | tf_op jit(solution)/shard_map/ppermute | solution.py:386
  23.3 10.9 %collective-permute-start.4 = (bf16[312,512]{1,0:T(8,128)(2,1)S(1)}, bf16[312,512]{1,0:T(8,128)(2,1)S(1)}, u32[]{:S(2)}, u32[]{:S(2)}) collective-permute-start(bf16[312,512]{1,0:T(8,128)(2,1)S(1)} %get-tuple-element.38), channel_id=1, source_target_pairs={{0,1},{1,0},{2,3},{3,2},{4,5},{5,4},{6,7},{7,6},{8,9},{9,8},{10,11... | collective-permute-start | bytes 958472 | tf_op jit(solution)/shard_map/ppermute | solution.py:386
  23.4 13.4 %collective-permute-start.5 = (bf16[312,512]{1,0:T(8,128)(2,1)S(1)}, bf16[312,512]{1,0:T(8,128)(2,1)S(1)}, u32[]{:S(2)}, u32[]{:S(2)}) collective-permute-start(bf16[312,512]{1,0:T(8,128)(2,1)S(1)} %get-tuple-element.39), channel_id=1, source_target_pairs={{0,31},{1,2},{2,1},{3,4},{4,3},{5,6},{6,5},{7,8},{8,7},{9,10},{10,... | collective-permute-start | bytes 958472 | tf_op jit(solution)/shard_map/ppermute | solution.py:386

commit v6 on v5

--- a/solution.py
+++ b/solution.py
@@ -21,8 +21,8 @@
 BIG = 1e30
 EXP_SCALE = math.log2(math.e) / math.sqrt(HD)
 VMEM_LIMIT = 24 * 1024 * 1024
-FCHUNK = 512
-STAGE = 8
+FCHUNK = 1024
+PER_LEVEL = HALF // LEV
 
 
 def token_tables():
@@ -37,7 +37,6 @@
     level = np.arange(HALF) % LEV
     row = np.arange(HALF) // (COLS * LEV)
     adds = np.zeros((HALF, 128), np.float32)
-    adds[:, 0] = level // 2
     adds[:, 1] = 4 * (level == 0) + np.where((level == 1) | (level == 2), 0, 1)
     adds[:, 2] = 2 * (row < 3)
     return pick, lane, adds
@@ -67,33 +66,39 @@
     return lax.broadcasted_iota(jnp.int32, (rows, 128), 1) < 64
 
 
-def attend(q, k, v, qf, kf):
-    m, n = q.shape[0], k.shape[0]
-    low_q, low_k = low_lanes(m), low_lanes(n)
-    ones = jnp.ones((n, 128), BF)
-    tiles = []
-    for first in range(0, HEADS, STAGE):
-        heads = range(first, first + STAGE)
-        scores, weights, got = [], [], []
-        for h in heads:
-            lanes = slice(h // 2 * 128, (h // 2 + 1) * 128)
-            if h % 2:
-                qh, kh = jnp.where(low_q, qf, q[:, lanes]), jnp.where(low_k, kf, k[:, lanes])
-            else:
-                qh, kh = jnp.where(low_q, q[:, lanes], qf), jnp.where(low_k, k[:, lanes], kf)
-            scores.append(lax.dot_general(qh, kh, (((1,), (1,)), ((), ())), preferred_element_type=F32))
-        for s in scores:
-            peak = jnp.max(s, axis=-1, keepdims=True)
-            weights.append(jnp.exp2((s - peak) * EXP_SCALE).astype(BF))
-        for h, e in zip(heads, weights):
-            lanes = slice(h // 2 * 128, (h // 2 + 1) * 128)
-            vh = jnp.where(low_k, ones, v[:, lanes]) if h % 2 else jnp.where(low_k, v[:, lanes], ones)
-            got.append(jnp.dot(e, vh, preferred_element_type=F32))
-        for even, odd in zip(got[::2], got[1::2]):
+def attend_all(parts):
+    jobs = [(part, h) for part in parts for h in range(HEADS)]
+    scores, weights, got = [], [], []
+    for (q, k, v, qf, kf), h in jobs:
+        lanes = slice(h // 2 * 128, (h // 2 + 1) * 128)
+        low_q, low_k = low_lanes(q.shape[0]), low_lanes(k.shape[0])
+        if h % 2:
+            qh, kh = jnp.where(low_q, qf, q[:, lanes]), jnp.where(low_k, kf, k[:, lanes])
+        else:
+            qh, kh = jnp.where(low_q, q[:, lanes], qf), jnp.where(low_k, k[:, lanes], kf)
+        scores.append(lax.dot_general(qh, kh, (((1,), (1,)), ((), ())), preferred_element_type=F32))
+    for s in scores:
+        peak = jnp.max(s, axis=-1, keepdims=True)
+        weights.append(jnp.exp2((s - peak) * EXP_SCALE).astype(BF))
+    for ((q, k, v, qf, kf), h), e in zip(jobs, weights):
+        lanes = slice(h // 2 * 128, (h // 2 + 1) * 128)
+        low_k, ones = low_lanes(k.shape[0]), jnp.ones((k.shape[0], 128), BF)
+        vh = jnp.where(low_k, ones, v[:, lanes]) if h % 2 else jnp.where(low_k, v[:, lanes], ones)
+        got.append(jnp.dot(e, vh, preferred_element_type=F32))
+    outs = []
+    for i, part in enumerate(parts):
+        low_q = low_lanes(part[0].shape[0])
+        tiles = []
+        for even, odd in zip(got[i * HEADS : (i + 1) * HEADS : 2], got[i * HEADS + 1 : (i + 1) * HEADS : 2]):
             num = jnp.where(low_q, even, odd)
             den = pltpu.roll(jnp.where(low_q, odd, even), 64, 1)
             tiles.append(num / den)
-    return jnp.concatenate(tiles, axis=1)
+        outs.append(jnp.concatenate(tiles, axis=1))
+    return outs
+
+
+def attend(*part):
+    return attend_all([part])[0]
 
 
 def is_odd(axis):
@@ -101,16 +106,26 @@
 
 
 def token_labels(region_ref, half, pick_ref, lane_ref, adds_ref, lab_s, first_row):
-    lab_s[...] = jnp.zeros_like(lab_s)
+    lab_s[0:128, :] = jnp.zeros((128, 128), F32)
     for row in range(6):
         lab_s[row * LEV : (row + 1) * LEV, 0:COLS] = region_ref[half * 6 + row].astype(F32)
-    rows = jnp.dot(pick_ref[...], lab_s[...].astype(BF), preferred_element_type=F32)
+    rows = jnp.dot(pick_ref[...], lab_s[0:128, :].astype(BF), preferred_element_type=F32)
     region = jnp.sum(rows * lane_ref[...].astype(F32), axis=-1, keepdims=True)
-    lab1 = region * 2 + adds_ref[:, 0:1]
     lab2 = region * 8 + adds_ref[:, 1:2]
     if half == 0:
         lab2 = lab2 + adds_ref[:, 2:3] * first_row
+    lab_s[...] = jnp.broadcast_to(region, (HALF, 128))
+    lab1 = jnp.concatenate([lab_s[pl.ds(level, PER_LEVEL, stride=LEV), :] for level in range(LEV)], axis=0)[:, 0:1]
     return lab1, lab2
+
+
+def load_rows(ref, rows):
+    return jnp.concatenate([ref[j, rows, :] for j in range(D // 128)], axis=1)
+
+
+def store_rows(ref, rows, value):
+    for j in range(D // 128):
+        ref[j, rows, :] = value[:, j * 128 : (j + 1) * 128]
 
 
 def piece(row, side):
@@ -173,35 +188,40 @@
     first_row = (lax.axis_index("lat") == 0).astype(F32)
     small.wait(*range(6))
     g1, g2 = g1_ref[0:1, :], g2_ref[0:1, :]
-    tiles = []
+    tiles, features, strides = [], [], []
     for half in range(2):
         lab1, lab2 = token_labels(region_ref, half, pick_ref, lane_ref, adds_ref, lab_s, first_row)
-        inputs.wait(2 * half)
-        for n in range(half * 72, half * 72 + 72):
-            xs[n * LEV : (n + 1) * LEV, :] = xv[n // COLS, n % COLS].astype(F32)
-        rows = slice(half * HALF, (half + 1) * HALF)
-        a = layer_norm(xs[rows], g1).astype(BF)
-        if half == 0:
-            inputs.wait(1)
-            mlp_inputs = Inputs(mlp_chunks(wu_hbm, wd_hbm, 0, wu, wd), mlp_sem)
-        qkv = jnp.dot(a, wq[...], preferred_element_type=F32).astype(BF)
-        o = attend(
-            qkv[:, :D], qkv[:, D : 2 * D], qkv[:, 2 * D :], query_features(lab1, HALF), key_features(lab1, HALF)
-        ).astype(BF)
-        if half == 0:
-            inputs.wait(3)
-        xs[rows] = xs[rows] + jnp.dot(o, wp[...], preferred_element_type=F32)
+        features += [(query_features(lab1[p], 144), key_features(lab1[p], 144)) for p in (slice(0, 144), slice(144, 288))]
         for i in range(2):
             for side in range(2):
                 start = (i * 2 + side) * GROUP
                 labs[start : start + GROUP, :] = jnp.broadcast_to(grouped(lab2, i, side), (GROUP, 128))
         tiles.append(jnp.transpose(labs[...], (1, 0))[0:8])
-    mid_ref[...] = xs[PER_RT : 3 * PER_RT]
+    for half in range(2):
+        inputs.wait(2 * half)
+        for n in range(half * 72, half * 72 + 72):
+            store_rows(xs, slice(n * LEV, (n + 1) * LEV), xv[n // COLS, n % COLS].astype(F32))
+        strides += [pl.ds(half * HALF + level, PER_LEVEL, stride=LEV) for level in range(LEV)]
+    x = jnp.concatenate([load_rows(xs, rows) for rows in strides], axis=0)
+    a = layer_norm(x, g1).astype(BF)
+    inputs.wait(1)
+    mlp_inputs = Inputs(mlp_chunks(wu_hbm, wd_hbm, 0, wu, wd), mlp_sem)
+    qkv = jnp.dot(a, wq[...], preferred_element_type=F32).astype(BF)
+    parts = []
+    for i, (qf, kf) in enumerate(features):
+        p = slice(i * 144, (i + 1) * 144)
+        parts.append((qkv[p, :D], qkv[p, D : 2 * D], qkv[p, 2 * D :], qf, kf))
+    o = jnp.concatenate(attend_all(parts), axis=0).astype(BF)
+    inputs.wait(3)
+    h = x + jnp.dot(o, wp[...], preferred_element_type=F32)
+    for i, rows in enumerate(strides):
+        store_rows(xs, rows, h[i * PER_LEVEL : (i + 1) * PER_LEVEL])
+    mid_ref[...] = load_rows(xs, slice(PER_RT, 3 * PER_RT))
     row = lax.broadcasted_iota(jnp.int32, (8, 384), 0)
     tile = jnp.where(row == 0, tiles[0], tiles[1])
     tile = jnp.concatenate([tile, jnp.zeros((8, 128), F32)], axis=1).astype(BF)
     tile_ref[...] = tile
-    h = jnp.concatenate([xs[0:PER_RT], xs[3 * PER_RT :]], axis=0)
+    h = jnp.concatenate([load_rows(xs, slice(0, PER_RT)), load_rows(xs, slice(3 * PER_RT, TOKENS))], axis=0)
     y = mlp(h, g2, wu, wd, mlp_inputs.wait)
     odd = is_odd("lat")
     for side in range(2):
@@ -267,14 +287,17 @@
     wq, wp, wu, wd = weights
     arrived = (lambda *which: None) if hbm is None else Inputs(second_copies(hbm, weights), sem[0]).wait
     g1, g2 = g1_ref[1:2, :], g2_ref[1:2, :]
-    for own, halo in windows_of(*arrays):
+    windows, parts, inner = windows_of(*arrays), [], []
+    for own, halo in windows:
         n_own = len(own) * GROUP
         x = jnp.concatenate([s[0].astype(F32) for s in own + halo], axis=0)
         lab = jnp.concatenate([s[1] for s in own + halo], axis=0)
         a = layer_norm(x, g1).astype(BF)
         kv = jnp.dot(a, wq[:, D:], preferred_element_type=F32).astype(BF)
         q = jnp.dot(a[:n_own], wq[:, :D], preferred_element_type=F32).astype(BF)
-        o = attend(q, kv[:, :D], kv[:, D:], query_features(lab[:n_own], n_own), key_features(lab, 4 * GROUP))
+        inner.append(x[:n_own])
+        parts.append((q, kv[:, :D], kv[:, D:], query_features(lab[:n_own], n_own), key_features(lab, 4 * GROUP)))
+    for (own, _), x, o in zip(windows, inner, attend_all(parts)):
         for i, s in enumerate(own):
             at, side = s[2]
             for r in range(3):
@@ -400,7 +423,7 @@
         in_specs=[HBM] * 11,
         out_specs=[VM] * 7,
         scratch_shapes=[
-            pltpu.VMEM((ROWS, COLS, LEV, D), BF), pltpu.VMEM((TOKENS, D), F32), pltpu.VMEM((128, 128), F32),
+            pltpu.VMEM((ROWS, COLS, LEV, D), BF), pltpu.VMEM((D // 128, TOKENS, 128), F32), pltpu.VMEM((HALF, 128), F32),
             pltpu.VMEM((384, 128), F32), pltpu.VMEM((ROWS, LEV, COLS), jnp.int32), pltpu.VMEM((HALF, 128), BF),
             pltpu.VMEM((HALF, 128), BF), pltpu.VMEM((HALF, 128), F32),
         ] + WEIGHT_SCRATCH + [pltpu.VMEM((FF, D), BF), dma(4), dma(N_CHUNK), dma(6)],

time: 44.9 us -> 42.5 us (0.947)
  Pallas kernels: 27.3 us -> 23.7 us
  waiting for transfers between devices: 4.87 us -> 5.77 us
    pallas_call x1, Pallas kernels: 7.77 us -> 6.57 us  [second_calls(): pl.pallas_call(edge_kernel, out_shape=out_shape, in_specs=[HBM] + [VM] *...]
    pallas_call x1, Pallas kernels: 6.84 us -> 5.73 us  [second_calls(): pl.pallas_call(middle_kernel, out_shape=(out_shape, pltpu.VMEM((D, D), BF...]
    pallas_call x1, Pallas kernels: 9.13 us -> 8.1 us  [first_calls(): pl.pallas_call(first_kernel, out_shape=(edge_out, edge_out, pltpu.VMEM((8...]
    ppermute x3, waiting for transfers between devices: 4.87 us -> 5.76 us  [exchange(): lax.ppermute(two, axis, odd_pairs)]
  transfers between devices with their start and end apart: 6 -> 6, of which waited for: 2 -> 2; matrix products, arithmetic and copies ran while one was open for 0% -> 0% of each run, Pallas kernels for 23% -> 21%
where the time goes in v6:
time: 42.5 us; the launch traced here: 42.4 us
  Pallas kernels  23.7 us (56%)
  starting transfers between devices  12.6 us (30%)
  waiting for transfers between devices  5.77 us (14%)
    ppermute x3, starting transfers between devices, exchange(): lax.ppermute(two, axis, odd_pairs)  10.8 us
    pallas_call x1, Pallas kernels, first_calls(): pl.pallas_call(first_kernel, out_shape=(edge_out, edge_out, pltpu.VMEM((8...  8.1 us
    pallas_call x1, Pallas kernels, second_calls(): pl.pallas_call(edge_kernel, out_shape=out_shape, in_specs=[HBM] + [VM] *...  6.57 us
    ppermute x3, waiting for transfers between devices, exchange(): lax.ppermute(two, axis, odd_pairs)  5.76 us
    pallas_call x1, Pallas kernels, second_calls(): pl.pallas_call(middle_kernel, out_shape=(out_shape, pltpu.VMEM((D, D), BF...  5.73 us
    pallas_call x1, Pallas kernels, first_calls(): pl.pallas_call(middle_mlp_kernel, out_shape=(edge_out, edge_out, pltpu.VM...  3.1 us
    ppermute x3, starting transfers between devices, exchange(): lax.ppermute(one, axis, even_pairs)  1.83 us
  transfers between devices with their start and end apart: 6, of which 2 were waited for; matrix products, arithmetic and copies ran while one was open for 0% of the time, Pallas kernels for 21%

profile of v6, /device:TPU:0, one launch (start us, length us, event | category | flops | bytes accessed | tf_op | source)
XLA Modules:
  0.0 42.4 jit_solution(13963505581840095905)
XLA Ops:
  0.0 8.1 %first_block.1 = (bf16[152,512]{1,0:T(8,128)(2,1)S(1)}, bf16[152,512]{1,0:T(8,128)(2,1)S(1)}, bf16[8,512]{1,0:T(8,128)(2,1)S(1)}, f32[288,512]{1,0:T(8,128)S(1)}...) custom-call(bf16[12,12,4,512]{3,2,1,0:T(4,128)(2,1)} %bitcast.3, ...), custom_call_target="tpu_custom_call" | custom-call | flops 4000000000 | bytes 8000000 | tf_op jit(solution)/shard_map/first_block/pallas_call | solution.py:417
  8.1 0.1 collective-permute-start
  8.2 3.2 %collective-permute-start.3 = (bf16[152,512]{1,0:T(8,128)(2,1)S(1)}, bf16[152,512]{1,0:T(8,128)(2,1)S(1)}, u32[]{:S(2)}, u32[]{:S(2)}) collective-permute-start(bf16[152,512]{1,0:T(8,128)(2,1)S(1)} %get-tuple-element.36.own_two.b), channel_id=1, source_target_pairs={{0,96},{32,64},{64,32},{96,0},{1,97},{33,65},{65,33},{97,1},{2,98}... | collective-permute-start | bytes 466952 | tf_op jit(solution)/shard_map/ppermute | solution.py:409
  11.4 3.1 %first_middle.1 = (bf16[152,512]{1,0:T(8,128)(2,1)S(1)}, bf16[152,512]{1,0:T(8,128)(2,1)S(1)}, bf16[512,1536]{1,0:T(8,128)(2,1)S(1)}) custom-call(f32[288,512]{1,0:T(8,128)S(1)} %get-tuple-element.24.mid, bf16[8,512]{1,0:T(8,128)(2,1)S(1)} %get-tuple-element.25.tile_ref, f32[2,512]{1,0:T(2,128)S(1)} %get-tuple-element.26.g2_ref, ...), custom_call_target="tpu_custom_call" | custom-call | flops 1300000000 | bytes 5000000 | tf_op jit(solution)/shard_map/first_middle/pallas_call | solution.py:434
  14.5 0.0 collective-permute-done.one.c
  14.5 1.7 %collective-permute-start.1 = (bf16[152,512]{1,0:T(8,128)(2,1)S(1)}, bf16[152,512]{1,0:T(8,128)(2,1)S(1)}, u32[]{:S(2)}, u32[]{:S(2)}) collective-permute-start(bf16[152,512]{1,0:T(8,128)(2,1)S(1)} %get-tuple-element.31.a), channel_id=1, source_target_pairs={{0,1},{1,0},{2,3},{3,2},{4,5},{5,4},{6,7},{7,6},{8,9},{9,8},{10,11... | collective-permute-start | bytes 466952 | tf_op jit(solution)/shard_map/ppermute | solution.py:409
  16.2 5.7 %collective-permute-start.2 = (bf16[152,512]{1,0:T(8,128)(2,1)S(1)}, bf16[152,512]{1,0:T(8,128)(2,1)S(1)}, u32[]{:S(2)}, u32[]{:S(2)}) collective-permute-start(bf16[152,512]{1,0:T(8,128)(2,1)S(1)} %get-tuple-element.32.b), channel_id=1, source_target_pairs={{0,31},{1,2},{2,1},{3,4},{4,3},{5,6},{6,5},{7,8},{8,7},{9,10},{10,... | collective-permute-start | bytes 466952 | tf_op jit(solution)/shard_map/ppermute | solution.py:409
  21.8 0.0 collective-permute-done.3.two.d
  21.8 0.2 pack_edges.1
  22.1 0.1 collective-permute-start.4
  22.2 2.0 %collective-permute-start.5 = (bf16[312,512]{1,0:T(8,128)(2,1)S(1)}, bf16[312,512]{1,0:T(8,128)(2,1)S(1)}, u32[]{:S(2)}, u32[]{:S(2)}) collective-permute-start(bf16[312,512]{1,0:T(8,128)(2,1)S(1)} %get-tuple-element.39), channel_id=1, source_target_pairs={{0,31},{1,2},{2,1},{3,4},{4,3},{5,6},{6,5},{7,8},{8,7},{9,10},{10,... | collective-permute-start | bytes 958472 | tf_op jit(solution)/shard_map/ppermute | solution.py:409
  24.1 0.0 collective-permute-done.1.c
  24.1 2.0 %collective-permute-done.2.d = bf16[152,512]{1,0:T(8,128)(2,1)S(1)} collective-permute-done((bf16[152,512]{1,0:T(8,128)(2,1)S(1)}, bf16[152,512]{1,0:T(8,128)(2,1)S(1)}, u32[]{:S(2)}, u32[]{:S(2)}) %collective-permute-start.2) | collective-permute-done | bytes 155680 | tf_op jit(solution)/shard_map/ppermute | solution.py:409
  26.1 5.7 %second_middle.1 = (bf16[12,12,4,512]{3,2,1,0:T(4,128)(2,1)}, bf16[512,512]{1,0:T(8,128)(2,1)S(1)}, bf16[512,2048]{1,0:T(8,128)(2,1)S(1)}, bf16[2048,512]{1,0:T(8,128)(2,1)S(1)}) custom-call(bf16[152,512]{1,0:T(8,128)(2,1)S(1)} %get-tuple-element.31.a, bf16[152,512]{1,0:T(8,128)(2,1)S(1)} %get-tuple-element.32.b, ...), custom_call_target="tpu_custom_call" | custom-call | flops 2500000000 | bytes 8000000 | tf_op jit(solution)/shard_map/second_middle/pallas_call | solution.py:450
  31.9 0.0 collective-permute-done.4.e
  31.9 3.7 %collective-permute-done.5.f = bf16[312,512]{1,0:T(8,128)(2,1)S(1)} collective-permute-done((bf16[312,512]{1,0:T(8,128)(2,1)S(1)}, bf16[312,512]{1,0:T(8,128)(2,1)S(1)}, u32[]{:S(2)}, u32[]{:S(2)}) %collective-permute-start.5) | collective-permute-done | bytes 319520 | tf_op jit(solution)/shard_map/ppermute | solution.py:409
  35.6 6.6 %second_edge.1 = bf16[12,12,4,512]{3,2,1,0:T(4,128)(2,1)} custom-call(bf16[12,12,4,512]{3,2,1,0:T(4,128)(2,1)} %get-tuple-element.35.out_in, bf16[152,512]{1,0:T(8,128)(2,1)S(1)} %get-tuple-element.30.own_one.a, bf16[152,512]{1,0:T(8,128)(2,1)S(1)} %get-tuple-element.36.own_two.b, ...), custom_call_target="tpu_custom_call", output_to_operand_aliasing={{}: (0, {})} | custom-call | flops 2500000000 | bytes 8000000 | tf_op jit(solution)/shard_map/second_edge/pallas_call | solution.py:462
Async XLA Ops:
  8.1 6.4 %collective-permute-start = (bf16[152,512]{1,0:T(8,128)(2,1)S(1)}, bf16[152,512]{1,0:T(8,128)(2,1)S(1)}, u32[]{:S(2)}, u32[]{:S(2)}) collective-permute-start(bf16[152,512]{1,0:T(8,128)(2,1)S(1)} %get-tuple-element.30.own_one.a), channel_id=1, source_target_pairs={{0,32},{32,0},{64,96},{96,64},{1,33},{33,1},{65,97},{97,65},{2,34}... | collective-permute-start | bytes 466952 | tf_op jit(solution)/shard_map/ppermute | solution.py:409
  8.2 13.6 %collective-permute-start.3 = (bf16[152,512]{1,0:T(8,128)(2,1)S(1)}, bf16[152,512]{1,0:T(8,128)(2,1)S(1)}, u32[]{:S(2)}, u32[]{:S(2)}) collective-permute-start(bf16[152,512]{1,0:T(8,128)(2,1)S(1)} %get-tuple-element.36.own_two.b), channel_id=1, source_target_pairs={{0,96},{32,64},{64,32},{96,0},{1,97},{33,65},{65,33},{97,1},{2,98}... | collective-permute-start | bytes 466952 | tf_op jit(solution)/shard_map/ppermute | solution.py:409
  14.5 9.6 %collective-permute-start.1 = (bf16[152,512]{1,0:T(8,128)(2,1)S(1)}, bf16[152,512]{1,0:T(8,128)(2,1)S(1)}, u32[]{:S(2)}, u32[]{:S(2)}) collective-permute-start(bf16[152,512]{1,0:T(8,128)(2,1)S(1)} %get-tuple-element.31.a), channel_id=1, source_target_pairs={{0,1},{1,0},{2,3},{3,2},{4,5},{5,4},{6,7},{7,6},{8,9},{9,8},{10,11... | collective-permute-start | bytes 466952 | tf_op jit(solution)/shard_map/ppermute | solution.py:409
  16.2 10.0 %collective-permute-start.2 = (bf16[152,512]{1,0:T(8,128)(2,1)S(1)}, bf16[152,512]{1,0:T(8,128)(2,1)S(1)}, u32[]{:S(2)}, u32[]{:S(2)}) collective-permute-start(bf16[152,512]{1,0:T(8,128)(2,1)S(1)} %get-tuple-element.32.b), channel_id=1, source_target_pairs={{0,31},{1,2},{2,1},{3,4},{4,3},{5,6},{6,5},{7,8},{8,7},{9,10},{10,... | collective-permute-start | bytes 466952 | tf_op jit(solution)/shard_map/ppermute | solution.py:409
  22.1 9.8 %collective-permute-start.4 = (bf16[312,512]{1,0:T(8,128)(2,1)S(1)}, bf16[312,512]{1,0:T(8,128)(2,1)S(1)}, u32[]{:S(2)}, u32[]{:S(2)}) collective-permute-start(bf16[312,512]{1,0:T(8,128)(2,1)S(1)} %get-tuple-element.38), channel_id=1, source_target_pairs={{0,1},{1,0},{2,3},{3,2},{4,5},{5,4},{6,7},{7,6},{8,9},{9,8},{10,11... | collective-permute-start | bytes 958472 | tf_op jit(solution)/shard_map/ppermute | solution.py:409
  22.2 13.5 %collective-permute-start.5 = (bf16[312,512]{1,0:T(8,128)(2,1)S(1)}, bf16[312,512]{1,0:T(8,128)(2,1)S(1)}, u32[]{:S(2)}, u32[]{:S(2)}) collective-permute-start(bf16[312,512]{1,0:T(8,128)(2,1)S(1)} %get-tuple-element.39), channel_id=1, source_target_pairs={{0,31},{1,2},{2,1},{3,4},{4,3},{5,6},{6,5},{7,8},{8,7},{9,10},{10,... | collective-permute-start | bytes 958472 | tf_op jit(solution)/shard_map/ppermute | solution.py:409

commit v7 on v6

--- a/solution.py
+++ b/solution.py
@@ -159,14 +159,14 @@
 N_CHUNK = 2 * (FF // FCHUNK)
 
 
-def mlp(h, gain, wup, wdown, arrived):
+def mlp(h, gain, wup, wdown, arrived, chunk=FCHUNK):
     a = layer_norm(h, gain).astype(BF)
     acc = h
-    for i, c in enumerate(range(0, FF, FCHUNK)):
-        arrived(2 * i, 2 * i + 1)
-        u = jnp.dot(a, wup[:, c : c + FCHUNK], preferred_element_type=F32)
+    for c in range(0, FF, chunk):
+        arrived(*range(2 * (c // FCHUNK), 2 * ((c + chunk) // FCHUNK)))
+        u = jnp.dot(a, wup[:, c : c + chunk], preferred_element_type=F32)
         g = jax.nn.gelu(u).astype(BF)
-        acc = acc + jnp.dot(g, wdown[c : c + FCHUNK, :], preferred_element_type=F32)
+        acc = acc + jnp.dot(g, wdown[c : c + chunk, :], preferred_element_type=F32)
     return acc
 
 
@@ -222,7 +222,7 @@
     tile = jnp.concatenate([tile, jnp.zeros((8, 128), F32)], axis=1).astype(BF)
     tile_ref[...] = tile
     h = jnp.concatenate([load_rows(xs, slice(0, PER_RT)), load_rows(xs, slice(3 * PER_RT, TOKENS))], axis=0)
-    y = mlp(h, g2, wu, wd, mlp_inputs.wait)
+    y = mlp(h, g2, wu, wd, mlp_inputs.wait, FF)
     odd = is_odd("lat")
     for side in range(2):
         rows = slice(side * GROUP, (side + 1) * GROUP)
@@ -306,7 +306,7 @@
                 x_s[rows, :] = x[i * GROUP + r * PIECE : i * GROUP + (r + 1) * PIECE]
     arrived(0)
     h = x_s[...] + jnp.dot(o_s[...].astype(BF), wp[...], preferred_element_type=F32)
-    o_s[...] = mlp(h, g2, wu, wd, lambda *which: arrived(*[1 + w for w in which]))
+    o_s[...] = mlp(h, g2, wu, wd, lambda *which: arrived(*[1 + w for w in which]), FF if hbm is None else FCHUNK)
     copies = []
     for i, rt in enumerate(rts):
         for n in range(36):

time: 42.5 us -> 42.2 us (level)
  transfers between devices with their start and end apart: 6 -> 6, of which waited for: 2 -> 2; matrix products, arithmetic and copies ran while one was open for 0% -> 0% of each run, Pallas kernels for 21% -> 22%
where the time goes in v7:
time: 42.2 us; the launch traced here: 42 us
  Pallas kernels  23.3 us (55%)
  starting transfers between devices  12.7 us (30%)
  waiting for transfers between devices  5.77 us (14%)
    ppermute x3, starting transfers between devices, exchange(): lax.ppermute(two, axis, odd_pairs)  10.8 us
    pallas_call x1, Pallas kernels, first_calls(): pl.pallas_call(first_kernel, out_shape=(edge_out, edge_out, pltpu.VMEM((8...  7.83 us
    pallas_call x1, Pallas kernels, second_calls(): pl.pallas_call(edge_kernel, out_shape=out_shape, in_specs=[HBM] + [VM] *...  6.47 us
    ppermute x3, waiting for transfers between devices, exchange(): lax.ppermute(two, axis, odd_pairs)  5.77 us
    pallas_call x1, Pallas kernels, second_calls(): pl.pallas_call(middle_kernel, out_shape=(out_shape, pltpu.VMEM((D, D), BF...  5.73 us
    pallas_call x1, Pallas kernels, first_calls(): pl.pallas_call(middle_mlp_kernel, out_shape=(edge_out, edge_out, pltpu.VM...  3.09 us
    ppermute x3, starting transfers between devices, exchange(): lax.ppermute(one, axis, even_pairs)  1.83 us
  transfers between devices with their start and end apart: 6, of which 2 were waited for; matrix products, arithmetic and copies ran while one was open for 0% of the time, Pallas kernels for 22%

profile of v7, /device:TPU:0, one launch (start us, length us, event | category | flops | bytes accessed | tf_op | source)
XLA Modules:
  0.0 42.0 jit_solution(14117261482124542740)
XLA Ops:
  0.0 7.8 %first_block.1 = (bf16[152,512]{1,0:T(8,128)(2,1)S(1)}, bf16[152,512]{1,0:T(8,128)(2,1)S(1)}, bf16[8,512]{1,0:T(8,128)(2,1)S(1)}, f32[288,512]{1,0:T(8,128)S(1)}...) custom-call(bf16[12,12,4,512]{3,2,1,0:T(4,128)(2,1)} %bitcast.3, ...), custom_call_target="tpu_custom_call" | custom-call | flops 4000000000 | bytes 8000000 | tf_op jit(solution)/shard_map/first_block/pallas_call | solution.py:417
  7.8 0.1 collective-permute-start
  7.9 3.2 %collective-permute-start.3 = (bf16[152,512]{1,0:T(8,128)(2,1)S(1)}, bf16[152,512]{1,0:T(8,128)(2,1)S(1)}, u32[]{:S(2)}, u32[]{:S(2)}) collective-permute-start(bf16[152,512]{1,0:T(8,128)(2,1)S(1)} %get-tuple-element.36.own_two.b), channel_id=1, source_target_pairs={{0,96},{32,64},{64,32},{96,0},{1,97},{33,65},{65,33},{97,1},{2,98}... | collective-permute-start | bytes 466952 | tf_op jit(solution)/shard_map/ppermute | solution.py:409
  11.2 3.1 %first_middle.1 = (bf16[152,512]{1,0:T(8,128)(2,1)S(1)}, bf16[152,512]{1,0:T(8,128)(2,1)S(1)}, bf16[512,1536]{1,0:T(8,128)(2,1)S(1)}) custom-call(f32[288,512]{1,0:T(8,128)S(1)} %get-tuple-element.24.mid, bf16[8,512]{1,0:T(8,128)(2,1)S(1)} %get-tuple-element.25.tile_ref, f32[2,512]{1,0:T(2,128)S(1)} %get-tuple-element.26.g2_ref, ...), custom_call_target="tpu_custom_call" | custom-call | flops 1300000000 | bytes 5000000 | tf_op jit(solution)/shard_map/first_middle/pallas_call | solution.py:434
  14.3 0.0 collective-permute-done.one.c
  14.3 1.7 %collective-permute-start.1 = (bf16[152,512]{1,0:T(8,128)(2,1)S(1)}, bf16[152,512]{1,0:T(8,128)(2,1)S(1)}, u32[]{:S(2)}, u32[]{:S(2)}) collective-permute-start(bf16[152,512]{1,0:T(8,128)(2,1)S(1)} %get-tuple-element.31.a), channel_id=1, source_target_pairs={{0,1},{1,0},{2,3},{3,2},{4,5},{5,4},{6,7},{7,6},{8,9},{9,8},{10,11... | collective-permute-start | bytes 466952 | tf_op jit(solution)/shard_map/ppermute | solution.py:409
  15.9 5.7 %collective-permute-start.2 = (bf16[152,512]{1,0:T(8,128)(2,1)S(1)}, bf16[152,512]{1,0:T(8,128)(2,1)S(1)}, u32[]{:S(2)}, u32[]{:S(2)}) collective-permute-start(bf16[152,512]{1,0:T(8,128)(2,1)S(1)} %get-tuple-element.32.b), channel_id=1, source_target_pairs={{0,31},{1,2},{2,1},{3,4},{4,3},{5,6},{6,5},{7,8},{8,7},{9,10},{10,... | collective-permute-start | bytes 466952 | tf_op jit(solution)/shard_map/ppermute | solution.py:409
  21.6 0.0 collective-permute-done.3.two.d
  21.6 0.2 pack_edges.1
  21.9 0.1 collective-permute-start.4
  22.0 1.9 %collective-permute-start.5 = (bf16[312,512]{1,0:T(8,128)(2,1)S(1)}, bf16[312,512]{1,0:T(8,128)(2,1)S(1)}, u32[]{:S(2)}, u32[]{:S(2)}) collective-permute-start(bf16[312,512]{1,0:T(8,128)(2,1)S(1)} %get-tuple-element.39), channel_id=1, source_target_pairs={{0,31},{1,2},{2,1},{3,4},{4,3},{5,6},{6,5},{7,8},{8,7},{9,10},{10,... | collective-permute-start | bytes 958472 | tf_op jit(solution)/shard_map/ppermute | solution.py:409
  23.9 0.0 collective-permute-done.1.c
  23.9 2.0 %collective-permute-done.2.d = bf16[152,512]{1,0:T(8,128)(2,1)S(1)} collective-permute-done((bf16[152,512]{1,0:T(8,128)(2,1)S(1)}, bf16[152,512]{1,0:T(8,128)(2,1)S(1)}, u32[]{:S(2)}, u32[]{:S(2)}) %collective-permute-start.2) | collective-permute-done | bytes 155680 | tf_op jit(solution)/shard_map/ppermute | solution.py:409
  25.9 5.7 %second_middle.1 = (bf16[12,12,4,512]{3,2,1,0:T(4,128)(2,1)}, bf16[512,512]{1,0:T(8,128)(2,1)S(1)}, bf16[512,2048]{1,0:T(8,128)(2,1)S(1)}, bf16[2048,512]{1,0:T(8,128)(2,1)S(1)}) custom-call(bf16[152,512]{1,0:T(8,128)(2,1)S(1)} %get-tuple-element.31.a, bf16[152,512]{1,0:T(8,128)(2,1)S(1)} %get-tuple-element.32.b, ...), custom_call_target="tpu_custom_call" | custom-call | flops 2500000000 | bytes 8000000 | tf_op jit(solution)/shard_map/second_middle/pallas_call | solution.py:450
  31.6 0.0 collective-permute-done.4.e
  31.6 3.7 %collective-permute-done.5.f = bf16[312,512]{1,0:T(8,128)(2,1)S(1)} collective-permute-done((bf16[312,512]{1,0:T(8,128)(2,1)S(1)}, bf16[312,512]{1,0:T(8,128)(2,1)S(1)}, u32[]{:S(2)}, u32[]{:S(2)}) %collective-permute-start.5) | collective-permute-done | bytes 319520 | tf_op jit(solution)/shard_map/ppermute | solution.py:409
  35.4 6.5 %second_edge.1 = bf16[12,12,4,512]{3,2,1,0:T(4,128)(2,1)} custom-call(bf16[12,12,4,512]{3,2,1,0:T(4,128)(2,1)} %get-tuple-element.35.out_in, bf16[152,512]{1,0:T(8,128)(2,1)S(1)} %get-tuple-element.30.own_one.a, bf16[152,512]{1,0:T(8,128)(2,1)S(1)} %get-tuple-element.36.own_two.b, ...), custom_call_target="tpu_custom_call", output_to_operand_aliasing={{}: (0, {})} | custom-call | flops 2500000000 | bytes 8000000 | tf_op jit(solution)/shard_map/second_edge/pallas_call | solution.py:462
Async XLA Ops:
  7.8 6.4 %collective-permute-start = (bf16[152,512]{1,0:T(8,128)(2,1)S(1)}, bf16[152,512]{1,0:T(8,128)(2,1)S(1)}, u32[]{:S(2)}, u32[]{:S(2)}) collective-permute-start(bf16[152,512]{1,0:T(8,128)(2,1)S(1)} %get-tuple-element.30.own_one.a), channel_id=1, source_target_pairs={{0,32},{32,0},{64,96},{96,64},{1,33},{33,1},{65,97},{97,65},{2,34}... | collective-permute-start | bytes 466952 | tf_op jit(solution)/shard_map/ppermute | solution.py:409
  7.9 13.7 %collective-permute-start.3 = (bf16[152,512]{1,0:T(8,128)(2,1)S(1)}, bf16[152,512]{1,0:T(8,128)(2,1)S(1)}, u32[]{:S(2)}, u32[]{:S(2)}) collective-permute-start(bf16[152,512]{1,0:T(8,128)(2,1)S(1)} %get-tuple-element.36.own_two.b), channel_id=1, source_target_pairs={{0,96},{32,64},{64,32},{96,0},{1,97},{33,65},{65,33},{97,1},{2,98}... | collective-permute-start | bytes 466952 | tf_op jit(solution)/shard_map/ppermute | solution.py:409
  14.3 9.6 %collective-permute-start.1 = (bf16[152,512]{1,0:T(8,128)(2,1)S(1)}, bf16[152,512]{1,0:T(8,128)(2,1)S(1)}, u32[]{:S(2)}, u32[]{:S(2)}) collective-permute-start(bf16[152,512]{1,0:T(8,128)(2,1)S(1)} %get-tuple-element.31.a), channel_id=1, source_target_pairs={{0,1},{1,0},{2,3},{3,2},{4,5},{5,4},{6,7},{7,6},{8,9},{9,8},{10,11... | collective-permute-start | bytes 466952 | tf_op jit(solution)/shard_map/ppermute | solution.py:409
  15.9 10.0 %collective-permute-start.2 = (bf16[152,512]{1,0:T(8,128)(2,1)S(1)}, bf16[152,512]{1,0:T(8,128)(2,1)S(1)}, u32[]{:S(2)}, u32[]{:S(2)}) collective-permute-start(bf16[152,512]{1,0:T(8,128)(2,1)S(1)} %get-tuple-element.32.b), channel_id=1, source_target_pairs={{0,31},{1,2},{2,1},{3,4},{4,3},{5,6},{6,5},{7,8},{8,7},{9,10},{10,... | collective-permute-start | bytes 466952 | tf_op jit(solution)/shard_map/ppermute | solution.py:409
  21.9 9.8 %collective-permute-start.4 = (bf16[312,512]{1,0:T(8,128)(2,1)S(1)}, bf16[312,512]{1,0:T(8,128)(2,1)S(1)}, u32[]{:S(2)}, u32[]{:S(2)}) collective-permute-start(bf16[312,512]{1,0:T(8,128)(2,1)S(1)} %get-tuple-element.38), channel_id=1, source_target_pairs={{0,1},{1,0},{2,3},{3,2},{4,5},{5,4},{6,7},{7,6},{8,9},{9,8},{10,11... | collective-permute-start | bytes 958472 | tf_op jit(solution)/shard_map/ppermute | solution.py:409
  22.0 13.4 %collective-permute-start.5 = (bf16[312,512]{1,0:T(8,128)(2,1)S(1)}, bf16[312,512]{1,0:T(8,128)(2,1)S(1)}, u32[]{:S(2)}, u32[]{:S(2)}) collective-permute-start(bf16[312,512]{1,0:T(8,128)(2,1)S(1)} %get-tuple-element.39), channel_id=1, source_target_pairs={{0,31},{1,2},{2,1},{3,4},{4,3},{5,6},{6,5},{7,8},{8,7},{9,10},{10,... | collective-permute-start | bytes 958472 | tf_op jit(solution)/shard_map/ppermute | solution.py:409

commit v8 on v7

--- a/solution.py
+++ b/solution.py
@@ -175,15 +175,15 @@
     one_ref, two_ref, tile_ref, mid_ref, wu, g1_ref, g2_ref,
     xv, xs, lab_s, labs, region_ref, pick_ref, lane_ref, adds_ref, wq, wp, wd, sem, mlp_sem, small_sem,
 ):
+    inputs = Inputs(
+        [(x_hbm.at[0:6], xv.at[0:6]), (wq_hbm.at[0], wq), (x_hbm.at[6:12], xv.at[6:12]), (wp_hbm.at[0], wp)], sem
+    )
     small = Inputs(
         [
             (region_hbm, region_ref), (pick_hbm, pick_ref), (lane_hbm, lane_ref), (adds_hbm, adds_ref),
             (g1_hbm, g1_ref), (g2_hbm, g2_ref),
         ],
         small_sem,
-    )
-    inputs = Inputs(
-        [(x_hbm.at[0:6], xv.at[0:6]), (wq_hbm.at[0], wq), (x_hbm.at[6:12], xv.at[6:12]), (wp_hbm.at[0], wp)], sem
     )
     first_row = (lax.axis_index("lat") == 0).astype(F32)
     small.wait(*range(6))

time: 42.2 us -> 42.3 us (level)
  transfers between devices with their start and end apart: 6 -> 6, of which waited for: 2 -> 2; matrix products, arithmetic and copies ran while one was open for 0% -> 0% of each run, Pallas kernels for 22% -> 21%
where the time goes in v8:
time: 42.3 us; the launch traced here: 42.1 us
  Pallas kernels  23.5 us (56%)
  starting transfers between devices  12.7 us (30%)
  waiting for transfers between devices  5.78 us (14%)
    ppermute x3, starting transfers between devices, exchange(): lax.ppermute(two, axis, odd_pairs)  10.8 us
    pallas_call x1, Pallas kernels, first_calls(): pl.pallas_call(first_kernel, out_shape=(edge_out, edge_out, pltpu.VMEM((8...  7.97 us
    pallas_call x1, Pallas kernels, second_calls(): pl.pallas_call(edge_kernel, out_shape=out_shape, in_specs=[HBM] + [VM] *...  6.47 us
    ppermute x3, waiting for transfers between devices, exchange(): lax.ppermute(two, axis, odd_pairs)  5.77 us
    pallas_call x1, Pallas kernels, second_calls(): pl.pallas_call(middle_kernel, out_shape=(out_shape, pltpu.VMEM((D, D), BF...  5.73 us
    pallas_call x1, Pallas kernels, first_calls(): pl.pallas_call(middle_mlp_kernel, out_shape=(edge_out, edge_out, pltpu.VM...  3.09 us
    ppermute x3, starting transfers between devices, exchange(): lax.ppermute(one, axis, even_pairs)  1.83 us
  transfers between devices with their start and end apart: 6, of which 2 were waited for; matrix products, arithmetic and copies ran while one was open for 0% of the time, Pallas kernels for 21%

profile of v8, /device:TPU:0, one launch (start us, length us, event | category | flops | bytes accessed | tf_op | source)
XLA Modules:
  0.0 42.1 jit_solution(15747829676813645009)
XLA Ops:
  0.0 8.0 %first_block.1 = (bf16[152,512]{1,0:T(8,128)(2,1)S(1)}, bf16[152,512]{1,0:T(8,128)(2,1)S(1)}, bf16[8,512]{1,0:T(8,128)(2,1)S(1)}, f32[288,512]{1,0:T(8,128)S(1)}...) custom-call(bf16[12,12,4,512]{3,2,1,0:T(4,128)(2,1)} %bitcast.3, ...), custom_call_target="tpu_custom_call" | custom-call | flops 4000000000 | bytes 8000000 | tf_op jit(solution)/shard_map/first_block/pallas_call | solution.py:417
  8.0 0.1 collective-permute-start
  8.1 3.2 %collective-permute-start.3 = (bf16[152,512]{1,0:T(8,128)(2,1)S(1)}, bf16[152,512]{1,0:T(8,128)(2,1)S(1)}, u32[]{:S(2)}, u32[]{:S(2)}) collective-permute-start(bf16[152,512]{1,0:T(8,128)(2,1)S(1)} %get-tuple-element.36.own_two.b), channel_id=1, source_target_pairs={{0,96},{32,64},{64,32},{96,0},{1,97},{33,65},{65,33},{97,1},{2,98}... | collective-permute-start | bytes 466952 | tf_op jit(solution)/shard_map/ppermute | solution.py:409
  11.3 3.1 %first_middle.1 = (bf16[152,512]{1,0:T(8,128)(2,1)S(1)}, bf16[152,512]{1,0:T(8,128)(2,1)S(1)}, bf16[512,1536]{1,0:T(8,128)(2,1)S(1)}) custom-call(f32[288,512]{1,0:T(8,128)S(1)} %get-tuple-element.24.mid, bf16[8,512]{1,0:T(8,128)(2,1)S(1)} %get-tuple-element.25.tile_ref, f32[2,512]{1,0:T(2,128)S(1)} %get-tuple-element.26.g2_ref, ...), custom_call_target="tpu_custom_call" | custom-call | flops 1300000000 | bytes 5000000 | tf_op jit(solution)/shard_map/first_middle/pallas_call | solution.py:434
  14.4 0.0 collective-permute-done.one.c
  14.4 1.7 %collective-permute-start.1 = (bf16[152,512]{1,0:T(8,128)(2,1)S(1)}, bf16[152,512]{1,0:T(8,128)(2,1)S(1)}, u32[]{:S(2)}, u32[]{:S(2)}) collective-permute-start(bf16[152,512]{1,0:T(8,128)(2,1)S(1)} %get-tuple-element.31.a), channel_id=1, source_target_pairs={{0,1},{1,0},{2,3},{3,2},{4,5},{5,4},{6,7},{7,6},{8,9},{9,8},{10,11... | collective-permute-start | bytes 466952 | tf_op jit(solution)/shard_map/ppermute | solution.py:409
  16.1 5.7 %collective-permute-start.2 = (bf16[152,512]{1,0:T(8,128)(2,1)S(1)}, bf16[152,512]{1,0:T(8,128)(2,1)S(1)}, u32[]{:S(2)}, u32[]{:S(2)}) collective-permute-start(bf16[152,512]{1,0:T(8,128)(2,1)S(1)} %get-tuple-element.32.b), channel_id=1, source_target_pairs={{0,31},{1,2},{2,1},{3,4},{4,3},{5,6},{6,5},{7,8},{8,7},{9,10},{10,... | collective-permute-start | bytes 466952 | tf_op jit(solution)/shard_map/ppermute | solution.py:409
  21.8 0.0 collective-permute-done.3.two.d
  21.8 0.2 pack_edges.1
  22.0 0.1 collective-permute-start.4
  22.1 1.9 %collective-permute-start.5 = (bf16[312,512]{1,0:T(8,128)(2,1)S(1)}, bf16[312,512]{1,0:T(8,128)(2,1)S(1)}, u32[]{:S(2)}, u32[]{:S(2)}) collective-permute-start(bf16[312,512]{1,0:T(8,128)(2,1)S(1)} %get-tuple-element.39), channel_id=1, source_target_pairs={{0,31},{1,2},{2,1},{3,4},{4,3},{5,6},{6,5},{7,8},{8,7},{9,10},{10,... | collective-permute-start | bytes 958472 | tf_op jit(solution)/shard_map/ppermute | solution.py:409
  24.0 0.0 collective-permute-done.1.c
  24.0 2.0 %collective-permute-done.2.d = bf16[152,512]{1,0:T(8,128)(2,1)S(1)} collective-permute-done((bf16[152,512]{1,0:T(8,128)(2,1)S(1)}, bf16[152,512]{1,0:T(8,128)(2,1)S(1)}, u32[]{:S(2)}, u32[]{:S(2)}) %collective-permute-start.2) | collective-permute-done | bytes 155680 | tf_op jit(solution)/shard_map/ppermute | solution.py:409
  26.0 5.7 %second_middle.1 = (bf16[12,12,4,512]{3,2,1,0:T(4,128)(2,1)}, bf16[512,512]{1,0:T(8,128)(2,1)S(1)}, bf16[512,2048]{1,0:T(8,128)(2,1)S(1)}, bf16[2048,512]{1,0:T(8,128)(2,1)S(1)}) custom-call(bf16[152,512]{1,0:T(8,128)(2,1)S(1)} %get-tuple-element.31.a, bf16[152,512]{1,0:T(8,128)(2,1)S(1)} %get-tuple-element.32.b, ...), custom_call_target="tpu_custom_call" | custom-call | flops 2500000000 | bytes 8000000 | tf_op jit(solution)/shard_map/second_middle/pallas_call | solution.py:450
  31.8 0.0 collective-permute-done.4.e
  31.8 3.7 %collective-permute-done.5.f = bf16[312,512]{1,0:T(8,128)(2,1)S(1)} collective-permute-done((bf16[312,512]{1,0:T(8,128)(2,1)S(1)}, bf16[312,512]{1,0:T(8,128)(2,1)S(1)}, u32[]{:S(2)}, u32[]{:S(2)}) %collective-permute-start.5) | collective-permute-done | bytes 319520 | tf_op jit(solution)/shard_map/ppermute | solution.py:409
  35.5 6.5 %second_edge.1 = bf16[12,12,4,512]{3,2,1,0:T(4,128)(2,1)} custom-call(bf16[12,12,4,512]{3,2,1,0:T(4,128)(2,1)} %get-tuple-element.35.out_in, bf16[152,512]{1,0:T(8,128)(2,1)S(1)} %get-tuple-element.30.own_one.a, bf16[152,512]{1,0:T(8,128)(2,1)S(1)} %get-tuple-element.36.own_two.b, ...), custom_call_target="tpu_custom_call", output_to_operand_aliasing={{}: (0, {})} | custom-call | flops 2500000000 | bytes 8000000 | tf_op jit(solution)/shard_map/second_edge/pallas_call | solution.py:462
Async XLA Ops:
  8.0 6.4 %collective-permute-start = (bf16[152,512]{1,0:T(8,128)(2,1)S(1)}, bf16[152,512]{1,0:T(8,128)(2,1)S(1)}, u32[]{:S(2)}, u32[]{:S(2)}) collective-permute-start(bf16[152,512]{1,0:T(8,128)(2,1)S(1)} %get-tuple-element.30.own_one.a), channel_id=1, source_target_pairs={{0,32},{32,0},{64,96},{96,64},{1,33},{33,1},{65,97},{97,65},{2,34}... | collective-permute-start | bytes 466952 | tf_op jit(solution)/shard_map/ppermute | solution.py:409
  8.1 13.7 %collective-permute-start.3 = (bf16[152,512]{1,0:T(8,128)(2,1)S(1)}, bf16[152,512]{1,0:T(8,128)(2,1)S(1)}, u32[]{:S(2)}, u32[]{:S(2)}) collective-permute-start(bf16[152,512]{1,0:T(8,128)(2,1)S(1)} %get-tuple-element.36.own_two.b), channel_id=1, source_target_pairs={{0,96},{32,64},{64,32},{96,0},{1,97},{33,65},{65,33},{97,1},{2,98}... | collective-permute-start | bytes 466952 | tf_op jit(solution)/shard_map/ppermute | solution.py:409
  14.4 9.6 %collective-permute-start.1 = (bf16[152,512]{1,0:T(8,128)(2,1)S(1)}, bf16[152,512]{1,0:T(8,128)(2,1)S(1)}, u32[]{:S(2)}, u32[]{:S(2)}) collective-permute-start(bf16[152,512]{1,0:T(8,128)(2,1)S(1)} %get-tuple-element.31.a), channel_id=1, source_target_pairs={{0,1},{1,0},{2,3},{3,2},{4,5},{5,4},{6,7},{7,6},{8,9},{9,8},{10,11... | collective-permute-start | bytes 466952 | tf_op jit(solution)/shard_map/ppermute | solution.py:409
  16.1 10.0 %collective-permute-start.2 = (bf16[152,512]{1,0:T(8,128)(2,1)S(1)}, bf16[152,512]{1,0:T(8,128)(2,1)S(1)}, u32[]{:S(2)}, u32[]{:S(2)}) collective-permute-start(bf16[152,512]{1,0:T(8,128)(2,1)S(1)} %get-tuple-element.32.b), channel_id=1, source_target_pairs={{0,31},{1,2},{2,1},{3,4},{4,3},{5,6},{6,5},{7,8},{8,7},{9,10},{10,... | collective-permute-start | bytes 466952 | tf_op jit(solution)/shard_map/ppermute | solution.py:409
  22.0 9.8 %collective-permute-start.4 = (bf16[312,512]{1,0:T(8,128)(2,1)S(1)}, bf16[312,512]{1,0:T(8,128)(2,1)S(1)}, u32[]{:S(2)}, u32[]{:S(2)}) collective-permute-start(bf16[312,512]{1,0:T(8,128)(2,1)S(1)} %get-tuple-element.38), channel_id=1, source_target_pairs={{0,1},{1,0},{2,3},{3,2},{4,5},{5,4},{6,7},{7,6},{8,9},{9,8},{10,11... | collective-permute-start | bytes 958472 | tf_op jit(solution)/shard_map/ppermute | solution.py:409
  22.1 13.4 %collective-permute-start.5 = (bf16[312,512]{1,0:T(8,128)(2,1)S(1)}, bf16[312,512]{1,0:T(8,128)(2,1)S(1)}, u32[]{:S(2)}, u32[]{:S(2)}) collective-permute-start(bf16[312,512]{1,0:T(8,128)(2,1)S(1)} %get-tuple-element.39), channel_id=1, source_target_pairs={{0,31},{1,2},{2,1},{3,4},{4,3},{5,6},{6,5},{7,8},{8,7},{9,10},{10,... | collective-permute-start | bytes 958472 | tf_op jit(solution)/shard_map/ppermute | solution.py:409
